TPU v7x, 32 devices: a whole 2x2x4 slice. The times are simulated.
32 devices in a mesh: row: 4 (over y, x), col: 8 (over z, core).
Axes of the slice: x: 2, y: 2, z: 4, core: 2. Of those that a mesh axis runs over, the one named last changes fastest.
Arguments:
- layer_input: bfloat16 [8192, 2048], P(('row', 'col')), may hold values from -6 to 6
- per_layer_input: bfloat16 [8192, 256], P(('row', 'col')), may hold values from -6 to 6
- out_cotangent: bfloat16 [8192, 2048], P(('row', 'col')), may hold values from -6 to 6
- seq_lengths: int32 [4, 3], P('row'), may hold values from 1 to 1024, 2048 in all within a row
- query_weight: bfloat16 [2048, 2048], P('row', 'col'), may hold values from -0.125 to 0.125
- key_weight: bfloat16 [2048, 512], P('row', 'col'), may hold values from -0.125 to 0.125
- value_weight: bfloat16 [2048, 512], P('row', 'col'), may hold values from -0.125 to 0.125
- out_weight: bfloat16 [2048, 2048], P('row', 'col'), may hold values from -0.125 to 0.125
- gate_weight: bfloat16 [2048, 8192], P('row', 'col'), may hold values from -0.125 to 0.125
- up_weight: bfloat16 [2048, 8192], P('row', 'col'), may hold values from -0.125 to 0.125
- down_weight: bfloat16 [2048, 8192], P('row', 'col'), may hold values from -0.0625 to 0.0625
- laurel_down: bfloat16 [2048, 64], P(('row', 'col')), may hold values from -0.125 to 0.125
- laurel_up: bfloat16 [2048, 64], P(('row', 'col')), may hold values from -0.75 to 0.75
- per_layer_gate: bfloat16 [2048, 256], P(('row', 'col')), may hold values from -0.125 to 0.125
- per_layer_projection: bfloat16 [2048, 256], P(('row', 'col')), may hold values from -0.375 to 0.375
- input_gain: bfloat16 [2048], P(('row', 'col')), may hold values from 0.099609375 to 1.8984375
- query_gain: bfloat16 [256], P(('row', 'col')), may hold values from 0.099609375 to 1.8984375
- key_gain: bfloat16 [256], P(('row', 'col')), may hold values from 0.099609375 to 1.8984375
- attention_gain: bfloat16 [2048], P(('row', 'col')), may hold values from 0.099609375 to 1.8984375
- laurel_gain: bfloat16 [2048], P(('row', 'col')), may hold values from 0.099609375 to 1.8984375
- pre_feed_gain: bfloat16 [2048], P(('row', 'col')), may hold values from 0.099609375 to 1.8984375
- post_feed_gain: bfloat16 [2048], P(('row', 'col')), may hold values from 0.099609375 to 1.8984375
- per_layer_gain: bfloat16 [2048], P(('row', 'col')), may hold values from 0.099609375 to 1.8984375
Outputs:
- layer_output: bfloat16 [8192, 2048], P(('row', 'col'))
- input_grad: bfloat16 [8192, 2048], P(('row', 'col'))
- per_layer_grad: bfloat16 [8192, 256], P(('row', 'col'))
- query_weight_grad: float32 [2048, 2048], P('row', 'col')
- key_weight_grad: float32 [2048, 512], P('row', 'col')
- value_weight_grad: float32 [2048, 512], P('row', 'col')
- out_weight_grad: float32 [2048, 2048], P('row', 'col')
- gate_weight_grad: float32 [2048, 8192], P('row', 'col')
- up_weight_grad: float32 [2048, 8192], P('row', 'col')
- down_weight_grad: float32 [2048, 8192], P('row', 'col')
- laurel_down_grad: float32 [2048, 64], P(('row', 'col'))
- laurel_up_grad: float32 [2048, 64], P(('row', 'col'))
- per_layer_gate_grad: float32 [2048, 256], P(('row', 'col'))
- per_layer_projection_grad: float32 [2048, 256], P(('row', 'col'))
- input_gain_grad: float32 [2048], P(('row', 'col'))
- query_gain_grad: float32 [256], P(('row', 'col'))
- key_gain_grad: float32 [256], P(('row', 'col'))
- attention_gain_grad: float32 [2048], P(('row', 'col'))
- laurel_gain_grad: float32 [2048], P(('row', 'col'))
- pre_feed_gain_grad: float32 [2048], P(('row', 'col'))
- post_feed_gain_grad: float32 [2048], P(('row', 'col'))
- per_layer_gain_grad: float32 [2048], P(('row', 'col'))
Inputs may be any that keep to these rules, and one draw needn't show every extreme that they name: `seq_lengths`: row r holds the lengths of the 3 sequences of row group r in token order; they sum to 2048, and the longest is exactly 1024.
All inputs are finite; a program needn't handle non-finite values.
Results may differ from a plain program's by a relative error of at most 0.025.
Values may be sent and summed in bfloat16 or wider, within the bound.
No kernel may reach another device: no remote copies, remote signals or barrier semaphores. Data moves between devices by JAX's collectives and lax.ppermute only.
A program may use at most 320 MiB of HBM per device.

v0:
```python
from functools import partial
import math

import jax
import jax.numpy as jnp
from jax import lax
from jax.experimental import pallas as pl
from jax.experimental.pallas import tpu as pltpu
from jax.sharding import PartitionSpec as P


HEADS = 8
KV_HEADS = 2
HEAD = 256
BLOCK = 256
ROW = "row"
COL = "col"


NORM_EPS = 1e-06
ROOT_HALF = 0.7071067811865476
ROPE_THETA = 1000000.0


def rms_scale(values, scale_gain):
    return (
        values
        * lax.rsqrt(jnp.mean(values * values, axis=-1, keepdims=True) + NORM_EPS)
        * scale_gain
    )


def angles(position):
    half_width = HEAD // 2
    steps_up = jnp.arange(half_width, dtype=jnp.float32)
    frequency = jnp.exp(steps_up * (-2.0 * math.log(ROPE_THETA) / HEAD))
    angle_grid = position.astype(jnp.float32)[:, None] * frequency[None, :]
    return (jnp.cos(angle_grid), jnp.sin(angle_grid))


def turn(values, cosine, sine_part):
    half_width = HEAD // 2
    first_half = values[:, :half_width]
    second_half = values[:, half_width:]
    return jnp.concatenate(
        [
            first_half * cosine - second_half * sine_part,
            second_half * cosine + first_half * sine_part,
        ],
        axis=1,
    )


def inverse_rms(values):
    return lax.rsqrt(jnp.mean(values * values, axis=1, keepdims=True) + NORM_EPS)


def norm_back(values, inverse, grad):
    return inverse * (
        grad - values * (inverse * inverse * jnp.mean(grad * values, axis=1, keepdims=True))
    )


def query_body(scale, query_ref, gain_ref, cosine_ref, sine_ref, out_ref):
    for head in range(query_ref.shape[1] // HEAD):
        span = slice(head * HEAD, (head + 1) * HEAD)
        values = query_ref[:, span].astype(jnp.float32)
        normed = values * inverse_rms(values) * gain_ref[...]
        turned = turn(normed, cosine_ref[...], sine_ref[...]).astype(jnp.bfloat16)
        out_ref[:, span] = turned * jnp.bfloat16(scale)


def query_back_body(query_ref, grad_ref, gain_ref, cosine_ref, sine_ref, out_ref, gain_grad_ref):
    total = jnp.zeros((1, HEAD), jnp.float32)
    for head in range(query_ref.shape[1] // HEAD):
        span = slice(head * HEAD, (head + 1) * HEAD)
        values = query_ref[:, span].astype(jnp.float32)
        inverse = inverse_rms(values)
        grad = turn(grad_ref[:, span], cosine_ref[...], -sine_ref[...])
        total = total + jnp.sum(grad * values * inverse, axis=0, keepdims=True)
        out_ref[:, span] = norm_back(values, inverse, grad * gain_ref[...]).astype(jnp.bfloat16)
    gain_grad_ref[...] = total


def head_of(columns, head, kind, count):
    width = columns.shape[1] // count // 2
    per_head = HEAD // width
    parts = [
        columns[:, (2 * c + kind) * width : (2 * c + kind + 1) * width]
        for c in range(head * per_head, (head + 1) * per_head)
    ]
    return jnp.concatenate(parts, axis=1)


def pair_body(count, columns_ref, gain_ref, cosine_ref, sine_ref, out_ref):
    columns = columns_ref[...].astype(jnp.float32)
    for head in range(KV_HEADS):
        span = slice(head * HEAD, (head + 1) * HEAD)
        keys = head_of(columns, head, 0, count)
        normed = keys * inverse_rms(keys) * gain_ref[...]
        out_ref[0, :, span] = turn(normed, cosine_ref[...], sine_ref[...]).astype(jnp.bfloat16)
        values = head_of(columns, head, 1, count)
        out_ref[1, :, span] = (values * inverse_rms(values)).astype(jnp.bfloat16)


def pair_back_body(
    count, columns_ref, grad_ref, gain_ref, cosine_ref, sine_ref, out_ref, gain_grad_ref
):
    columns = columns_ref[...].astype(jnp.float32)
    width = columns.shape[1] // count // 2
    total = jnp.zeros((1, HEAD), jnp.float32)
    pieces = []
    for head in range(KV_HEADS):
        span = slice(head * HEAD, (head + 1) * HEAD)
        keys = head_of(columns, head, 0, count)
        inverse = inverse_rms(keys)
        grad = grad_ref[0, :, span].astype(jnp.float32)
        grad = turn(grad, cosine_ref[...], -sine_ref[...])
        total = total + jnp.sum(grad * keys * inverse, axis=0, keepdims=True)
        key_grad = norm_back(keys, inverse, grad * gain_ref[...])
        values = head_of(columns, head, 1, count)
        value_grad = norm_back(
            values, inverse_rms(values), grad_ref[1, :, span].astype(jnp.float32)
        )
        for c in range(HEAD // width):
            pieces.append(key_grad[:, c * width : (c + 1) * width])
            pieces.append(value_grad[:, c * width : (c + 1) * width])
    out_ref[...] = jnp.concatenate(pieces, axis=1).astype(jnp.bfloat16)
    gain_grad_ref[...] = total


def small_call(body, shapes, *operands):
    size = 4 * sum(one.size for one in operands)
    return pl.pallas_call(
        body,
        out_shape=shapes,
        cost_estimate=pl.CostEstimate(flops=4 * size, transcendentals=0, bytes_accessed=size),
    )(*operands)


def placement_info(lengths, tokens_at):
    finish = jnp.cumsum(lengths)
    begins = finish - lengths
    segment = jnp.sum((tokens_at[:, None] >= finish[None, :]).astype(jnp.int32), axis=1)
    chosen = segment[:, None] == jnp.arange(lengths.shape[0], dtype=jnp.int32)[None, :]
    begin = jnp.sum(jnp.where(chosen, begins[None, :], 0), axis=1)
    end = jnp.sum(jnp.where(chosen, finish[None, :], 0), axis=1)
    position = tokens_at - begin
    reach = jnp.minimum(end, begin + (position // BLOCK + 1) * BLOCK)
    return (position, begin, reach)


def geglu(gate_in, up_in):
    return jax.nn.gelu(gate_in, approximate=True) * up_in


def residual_mix(inputs, attention_out, normed, laurel_out, attention_gain, laurel_gain, pre_gain):
    mixed = (
        inputs
        + rms_scale(attention_out, attention_gain)
        + normed
        + rms_scale(laurel_out, laurel_gain)
    ) * ROOT_HALF
    return (mixed, rms_scale(mixed, pre_gain))


def feed_mix(mixed, down_out, post_gain):
    return mixed + rms_scale(down_out, post_gain)


def final_mix(after_feed, per_out, final_gain):
    return after_feed + rms_scale(per_out, final_gain)


def product(left, right):
    return jnp.dot(left, right, preferred_element_type=jnp.float32)


def product_t(left, right):
    return lax.dot_general(
        left, right, (((1,), (1,)), ((), ())), preferred_element_type=jnp.float32
    )


def product_tn(left, right):
    return lax.dot_general(
        left, right, (((0,), (0,)), ((), ())), preferred_element_type=jnp.float32
    )


def hop(values, axis, mask):
    size = lax.axis_size(axis)
    return lax.ppermute(values, axis, [(i, i ^ mask) for i in range(size)])


def split_hop(values, even_mask, odd_mask):
    size = lax.axis_size(ROW) * lax.axis_size(COL)
    pairs = [(i, i ^ (odd_mask if i % 2 else even_mask)) for i in range(size)]
    return lax.ppermute(values, (ROW, COL), pairs)


def after(values, *others):
    return lax.optimization_barrier((values,) + others)[0]


def xor_blocks(values, me, count):
    width = values.shape[-1] // count
    blocks = [values[..., i * width : (i + 1) * width] for i in range(count)]
    bit = 1
    while bit < count:
        flip = (me & bit) != 0
        blocks = [jnp.where(flip, blocks[i ^ bit], blocks[i]) for i in range(count)]
        bit *= 2
    return jnp.concatenate(blocks, axis=-1)


def unit_of(axis):
    return lax.axis_size(COL) if axis == ROW else 2


def direct_gather(piece, axis, count):
    unit = 1 if axis == ROW else 2
    return [piece] + [hop(piece, axis, j * unit) for j in range(1, count)]


def xor_gather(piece, axis, count, middle=None):
    unit = 1 if axis == ROW else 2
    if count == 4:
        near = hop(piece, axis, unit)
        far = hop(piece, axis, 2 * unit)
        odd = lax.axis_index(COL) % 2 == 1
        flat = unit_of(axis)
        chosen_far, chosen_near = far, near
        if middle is not None:
            chosen_far, chosen_near = after(far, middle), after(near, middle)
        across = split_hop(jnp.where(odd, chosen_far, chosen_near), 2 * flat, flat)
        return [piece, near, far, across]
    pieces = [piece]
    bit = 1
    while bit < count:
        pieces = pieces + [hop(one, axis, bit * unit) for one in pieces]
        bit *= 2
    return pieces


def add_low(left, right):
    return (left.astype(jnp.float32) + right.astype(jnp.float32)).astype(jnp.bfloat16)


def xor_scatter(parts, axis, late=None, last=None, marks=None):
    count = parts.shape[0]
    unit = 1 if axis == ROW else 2
    if marks is not None and count != 4:
        marks.append(parts[0])
    if count == 4:
        odd = lax.axis_index(COL) % 2 == 1
        flat = unit_of(axis)
        across = split_hop(parts[3], 2 * flat, flat)
        early = split_hop(jnp.where(odd, parts[1], parts[2]), 2 * flat, flat)
        if late is not None:
            across = after(across, late)
        rest = add_low(jnp.where(odd, parts[2], parts[1]), across)
        if marks is not None:
            marks.append(rest)
        rest = split_hop(rest, flat, 2 * flat)
        if last is not None:
            rest = after(rest, last)
            early = after(early, last)
        return parts[0].astype(jnp.float32) + early.astype(jnp.float32) + rest.astype(jnp.float32)
    parts = [parts[j] for j in range(count)]
    bit = count // 2
    while bit > 0:
        parts = [add_low(parts[j], hop(parts[j + bit], axis, bit * unit)) for j in range(bit)]
        bit //= 2
    return parts[0].astype(jnp.float32)


def scatter_rows(total, row_total, late=None, last=None, marks=None):
    parts = total.reshape(row_total, -1, total.shape[1])
    return xor_scatter(parts, ROW, late, last, marks)


def scatter_cols(total, row_total, pairs, late=None, last=None, marks=None):
    mine = scatter_rows(total, row_total, late, last, marks).astype(jnp.bfloat16)
    width = mine.shape[1] // pairs
    parts = jnp.stack([mine[:, z * width : (z + 1) * width] for z in range(pairs)])
    return xor_scatter(parts, COL, None, None, marks)


def deal_rows_body(pairs, me_ref, block_ref, keep_ref, give_ref):
    for z in range(pairs):
        keep_ref[z] = block_ref[lax.bitwise_xor(me_ref[0], 2 * z)]
        give_ref[z] = block_ref[lax.bitwise_xor(me_ref[0], 2 * z + 1)]


def scatter_small(me, total, row_total, col_total):
    pairs = col_total // 2
    width = total.shape[1]
    blocks = total.reshape(row_total, col_total, -1, width)
    height = blocks.shape[2]
    half = jax.ShapeDtypeStruct((row_total, pairs, height, width), total.dtype)
    out_block = pl.BlockSpec((None, pairs, height, width), lambda r, s: (r, 0, 0, 0))
    keep, give = pl.pallas_call(
        partial(deal_rows_body, pairs),
        out_shape=(half, half),
        grid_spec=pltpu.PrefetchScalarGridSpec(
            num_scalar_prefetch=1,
            grid=(row_total,),
            in_specs=[
                pl.BlockSpec((None, col_total, height, width), lambda r, s: (r, 0, 0, 0))
            ],
            out_specs=(out_block, out_block),
        ),
        cost_estimate=pl.CostEstimate(
            flops=0, transcendentals=0, bytes_accessed=4 * total.size
        ),
    )(me, blocks)
    both = add_low(keep, hop(give, COL, 1)).reshape(row_total, pairs * height, width)
    mine = xor_scatter(both, ROW).astype(jnp.bfloat16)
    return xor_scatter(mine.reshape(pairs, height, width), COL)


def stack_body(*refs):
    for i, ref in enumerate(refs[:-1]):
        refs[-1][i] = ref[...]


def stack_pieces(pieces):
    shape = (len(pieces),) + pieces[0].shape
    return pl.pallas_call(
        stack_body,
        out_shape=jax.ShapeDtypeStruct(shape, pieces[0].dtype),
        cost_estimate=pl.CostEstimate(
            flops=0, transcendentals=0, bytes_accessed=4 * math.prod(shape)
        ),
    )(*pieces)


def gather_weight(shard, pairs, row_total, direct, first=None, second=None, middle=None):
    along = direct_gather(shard if first is None else after(shard, first), COL, pairs)
    stacked = stack_pieces(along)
    if second is not None:
        stacked = after(stacked, second)
    if direct:
        mine = direct_gather(stacked, ROW, row_total)
    else:
        mine = xor_gather(stacked, ROW, row_total, middle)
    return (mine, [hop(one, COL, 1) for one in mine]), along[-1], mine[-1]


def place_body(pairs, me_ref, own_ref, other_ref, out_ref):
    for z in range(pairs):
        out_ref[lax.bitwise_xor(me_ref[0], 2 * z)] = own_ref[z]
        out_ref[lax.bitwise_xor(me_ref[0], 2 * z + 1)] = other_ref[z]


def over_col(me, own, pairs):
    stacked = stack_pieces(direct_gather(own, COL, pairs))
    other = hop(stacked, COL, 1)
    vmem = pl.BlockSpec(memory_space=pltpu.VMEM)
    return pl.pallas_call(
        partial(place_body, pairs),
        out_shape=jax.ShapeDtypeStruct((2 * pairs,) + own.shape, own.dtype),
        in_specs=[pl.BlockSpec(memory_space=pltpu.SMEM), vmem, vmem],
    )(me, stacked, other)


def block_of(ref, index, width):
    if len(ref.shape) == 3:
        return ref.at[index]
    return ref.at[:, pl.ds(pl.multiple_of(index * width, 128), width)]


def blocked(values, count):
    rows = values.shape[0]
    width = values.shape[1] // count
    if width % 128 == 0:
        return values
    return jnp.transpose(values.reshape(rows, count, width), (1, 0, 2))


def project_body(me_ref, left_ref, *refs):
    pieces, out_ref = refs[:-1], refs[-1]
    row_total = len(pieces) // 2
    pairs, height, width = pieces[0].shape
    for z in range(pairs):
        for core in range(2):
            total = None
            for r in range(row_total):
                part = jnp.dot(
                    left_ref[:, r * height : (r + 1) * height],
                    pieces[core * row_total + r][z],
                    preferred_element_type=jnp.float32,
                )
                total = part if total is None else total + part
            out = block_of(out_ref, lax.bitwise_xor(me_ref[0], 2 * z + core), width)
            out[...] = total.astype(out_ref.dtype)


def contract_body(me_ref, left_ref, *refs):
    pieces, out_ref = refs[:-1], refs[-1]
    row_total = len(pieces) // 2
    pairs, height, width = pieces[0].shape
    for r in range(row_total):
        total = None
        for z in range(pairs):
            for core in range(2):
                block = block_of(left_ref, lax.bitwise_xor(me_ref[0], 2 * z + core), width)
                part = lax.dot_general(
                    block[...],
                    pieces[core * row_total + r][z],
                    (((1,), (1,)), ((), ())),
                    preferred_element_type=jnp.float32,
                )
                total = part if total is None else total + part
        out_ref[:, r * height : (r + 1) * height] = total


def whole_call(body, shape, dtype, flops, me, left, pieces):
    mine, other = pieces
    operands = [left, *mine, *other]
    size = sum(one.size for one in operands) * 2
    vmem = pl.BlockSpec(memory_space=pltpu.VMEM)
    return pl.pallas_call(
        body,
        out_shape=jax.ShapeDtypeStruct(shape, dtype),
        in_specs=[pl.BlockSpec(memory_space=pltpu.SMEM)] + [vmem] * len(operands),
        out_specs=vmem,
        cost_estimate=pl.CostEstimate(flops=flops, transcendentals=0, bytes_accessed=size),
    )(me, *operands)


def project(me, left, pieces):
    pairs, _, width = pieces[0][0].shape
    rows = left.shape[0]
    shape = (rows, 2 * pairs * width) if width % 128 == 0 else (2 * pairs, rows, width)
    flops = 4 * rows * left.shape[1] * pairs * width
    out = whole_call(project_body, shape, jnp.bfloat16, flops, me, left, pieces)
    if len(shape) == 3:
        out = jnp.transpose(out, (1, 0, 2)).reshape(rows, 2 * pairs * width)
    return out


def contract(me, left, pieces):
    pairs, height, _ = pieces[0][0].shape
    shape = (left.shape[0], len(pieces[0]) * height)
    flops = 2 * left.size * shape[1]
    left = blocked(left, 2 * pairs)
    return whole_call(contract_body, shape, jnp.float32, flops, me, left, pieces)


def deal_body(pairs, me_ref, columns_ref, keep_ref, give_ref):
    width = keep_ref.shape[1] // pairs
    for z in range(pairs):
        span = slice(z * width, (z + 1) * width)
        for core, out_ref in enumerate((keep_ref, give_ref)):
            index = lax.bitwise_xor(me_ref[0], 2 * z + core)
            out_ref[:, span] = block_of(columns_ref, index, width)[...]


def pair_columns(me, columns, count):
    rows, width = columns.shape
    half = jax.ShapeDtypeStruct((rows, width // 2), columns.dtype)
    values = blocked(columns, count)
    keep, give = pl.pallas_call(
        partial(deal_body, count // 2),
        out_shape=(half, half),
        in_specs=[
            pl.BlockSpec(memory_space=pltpu.SMEM),
            pl.BlockSpec(memory_space=pltpu.VMEM),
        ],
        cost_estimate=pl.CostEstimate(
            flops=0, transcendentals=0, bytes_accessed=4 * rows * width
        ),
    )(me, values)
    return jnp.concatenate([keep, hop(give, COL, 1)], axis=0)


def pair_rows(own):
    return jnp.concatenate([own, hop(own, COL, 1)], axis=0)


def attend_body(span_ref, window_ref, query_ref, key_ref, value_ref, out_ref, inverse_ref, sums, weights):
    rows = query_ref.shape[0]
    low_edge = window_ref[:, 0:1]
    high_edge = window_ref[:, 1:2]
    query = query_ref[...]
    sums[...] = jnp.zeros_like(sums)
    weights[...] = jnp.zeros_like(weights)

    def one_tile(tile, carry):
        scores = lax.dot_general(
            query, key_ref[tile], (((1,), (1,)), ((), ())), preferred_element_type=jnp.float32
        )
        place = tile * rows + lax.broadcasted_iota(jnp.int32, scores.shape, 1)
        exps = jnp.where((place >= low_edge) & (place < high_edge), jnp.exp(scores), 0.0)
        part = exps[:, :128]
        for start in range(128, rows, 128):
            part = part + exps[:, start : start + 128]
        weights[...] += part
        sums[...] += jnp.dot(
            exps.astype(jnp.bfloat16), value_ref[tile], preferred_element_type=jnp.float32
        )
        return carry

    lax.fori_loop(span_ref[0], span_ref[1], one_tile, 0)
    inverse = 1.0 / jnp.sum(weights[...], axis=1, keepdims=True)
    out_ref[...] = (sums[...] * inverse).astype(jnp.bfloat16)
    inverse_ref[...] = jnp.broadcast_to(inverse, inverse_ref.shape)


def attend(span, window, query, gathered):
    rows, width = query.shape
    tiles = gathered.shape[0]
    groups = HEADS // KV_HEADS
    half = pl.BlockSpec((rows, HEAD), lambda h, s: (0, h))
    flops = 4 * rows * rows * tiles * width
    return pl.pallas_call(
        attend_body,
        out_shape=(
            jax.ShapeDtypeStruct((rows, width), jnp.bfloat16),
            jax.ShapeDtypeStruct((rows, HEADS * 128), jnp.float32),
        ),
        grid_spec=pltpu.PrefetchScalarGridSpec(
            num_scalar_prefetch=1,
            grid=(HEADS,),
            in_specs=[
                pl.BlockSpec((rows, 2), lambda h, s: (0, 0)),
                half,
                pl.BlockSpec((tiles, None, rows, HEAD), lambda h, s: (0, 0, 0, h // groups)),
                pl.BlockSpec((tiles, None, rows, HEAD), lambda h, s: (0, 1, 0, h // groups)),
            ],
            out_specs=(half, pl.BlockSpec((rows, 128), lambda h, s: (0, h))),
            scratch_shapes=[
                pltpu.VMEM((rows, HEAD), jnp.float32),
                pltpu.VMEM((rows, 128), jnp.float32),
            ],
        ),
        cost_estimate=pl.CostEstimate(
            flops=flops, transcendentals=rows * rows * tiles * HEADS, bytes_accessed=8 * rows * width
        ),
    )(span, window, query, gathered, gathered)


def attend_back_body(
    span_ref, window_ref, query_ref, key_ref, value_ref, grad_ref, out_ref, inverse_ref,
    query_grad_ref, pair_grad_ref, query_sum, key_sum, value_sum,
):
    rows = query_ref.shape[0]
    groups = HEADS // KV_HEADS
    head = pl.program_id(0)
    low_edge = window_ref[0:1, :]
    high_edge = window_ref[1:2, :]
    query = query_ref[...]
    grad_wide = grad_ref[...].astype(jnp.float32)
    inverse = inverse_ref[:, 0:1]
    delta = jnp.sum(grad_wide * out_ref[...].astype(jnp.float32), axis=1, keepdims=True) * inverse
    delta_row = jnp.transpose(jnp.broadcast_to(delta, (rows, 128)))[0:1, :]
    grad_scaled = (grad_wide * inverse).astype(jnp.bfloat16)
    query_sum[...] = jnp.zeros_like(query_sum)

    @pl.when(lax.rem(head, groups) == 0)
    def _():
        key_sum[...] = jnp.zeros_like(key_sum)
        value_sum[...] = jnp.zeros_like(value_sum)

    def one_tile(tile, carry):
        keys = key_ref[tile]
        contract_last = (((1,), (1,)), ((), ()))
        scores = lax.dot_general(keys, query, contract_last, preferred_element_type=jnp.float32)
        place = tile * rows + lax.broadcasted_iota(jnp.int32, scores.shape, 0)
        exps = jnp.where((place >= low_edge) & (place < high_edge), jnp.exp(scores), 0.0)
        prob_grad = lax.dot_general(
            value_ref[tile], grad_scaled, contract_last, preferred_element_type=jnp.float32
        )
        score_grad = (exps * (prob_grad - delta_row)).astype(jnp.bfloat16)
        key_sum[tile] += jnp.dot(score_grad, query, preferred_element_type=jnp.float32)
        value_sum[tile] += jnp.dot(
            exps.astype(jnp.bfloat16), grad_scaled, preferred_element_type=jnp.float32
        )
        query_sum[...] += lax.dot_general(
            score_grad, keys, (((0,), (0,)), ((), ())), preferred_element_type=jnp.float32
        )
        return carry

    lax.fori_loop(span_ref[0], span_ref[1], one_tile, 0)
    query_grad_ref[...] = query_sum[...] * (1.0 / math.sqrt(HEAD))

    @pl.when(lax.rem(head, groups) == groups - 1)
    def _():
        pair_grad_ref[:, 0] = key_sum[...].astype(jnp.bfloat16)
        pair_grad_ref[:, 1] = value_sum[...].astype(jnp.bfloat16)


def attend_back(span, window, query, gathered, grad, out, inverse):
    rows, width = query.shape
    tiles = gathered.shape[0]
    groups = HEADS // KV_HEADS
    half = pl.BlockSpec((rows, HEAD), lambda h, s: (0, h))
    return pl.pallas_call(
        attend_back_body,
        out_shape=(
            jax.ShapeDtypeStruct((rows, width), jnp.float32),
            jax.ShapeDtypeStruct(gathered.shape, jnp.bfloat16),
        ),
        grid_spec=pltpu.PrefetchScalarGridSpec(
            num_scalar_prefetch=1,
            grid=(HEADS,),
            in_specs=[
                pl.BlockSpec((2, rows), lambda h, s: (0, 0)),
                half,
                pl.BlockSpec((tiles, None, rows, HEAD), lambda h, s: (0, 0, 0, h // groups)),
                pl.BlockSpec((tiles, None, rows, HEAD), lambda h, s: (0, 1, 0, h // groups)),
                half,
                half,
                pl.BlockSpec((rows, 128), lambda h, s: (0, h)),
            ],
            out_specs=(
                half,
                pl.BlockSpec((tiles, 2, rows, HEAD), lambda h, s: (0, 0, 0, h // groups)),
            ),
            scratch_shapes=[
                pltpu.VMEM((rows, HEAD), jnp.float32),
                pltpu.VMEM((tiles, rows, HEAD), jnp.float32),
                pltpu.VMEM((tiles, rows, HEAD), jnp.float32),
            ],
        ),
        cost_estimate=pl.CostEstimate(
            flops=10 * rows * rows * tiles * width,
            transcendentals=rows * rows * tiles * HEADS,
            bytes_accessed=16 * rows * width,
        ),
    )(span, window, query, gathered, gathered, grad, out, inverse)


def local(
    layer_input,
    per_layer_input,
    out_cotangent,
    seq_lengths,
    query_weight,
    key_weight,
    value_weight,
    out_weight,
    gate_weight,
    up_weight,
    down_weight,
    laurel_down,
    laurel_up,
    per_layer_gate,
    per_layer_projection,
    input_gain,
    query_gain,
    key_gain,
    attention_gain,
    laurel_gain,
    pre_feed_gain,
    post_feed_gain,
    per_layer_gain,
):
    rows, width = layer_input.shape
    row_total = lax.axis_size(ROW)
    col_total = lax.axis_size(COL)
    pairs = col_total // 2
    me_row = lax.axis_index(ROW)
    me_col = lax.axis_index(COL)
    rank = laurel_down.shape[1]
    embed = per_layer_gate.shape[1]
    kv_width = key_weight.shape[1]
    feed_width = gate_weight.shape[1]
    low = jnp.bfloat16
    wide = jnp.float32

    me = me_col.astype(jnp.int32).reshape(1)
    small_rows = laurel_down.shape[0]
    head_part = query_gain.shape[0]

    gains_own = jnp.concatenate(
        [
            input_gain,
            attention_gain,
            laurel_gain,
            pre_feed_gain,
            post_feed_gain,
            per_layer_gain,
            query_gain,
            key_gain,
        ]
    )
    gain_total = gains_own.shape[0]
    laurel_own = jnp.concatenate([laurel_down, laurel_up], axis=1)
    line = laurel_own.shape[1]
    gain_lines = -(-gain_total // line)
    gains_block = jnp.pad(gains_own, (0, gain_lines * line - gain_total)).reshape(gain_lines, line)
    first_own = jnp.concatenate(
        [laurel_own, jnp.pad(gains_block, ((0, 16 - gain_lines), (0, 0)))], axis=0
    )

    spread = jnp.broadcast_to(first_own[None], (col_total,) + first_own.shape)
    first_group = lax.all_to_all(spread, COL, 0, 0, tiled=True)
    first_all = jnp.stack(direct_gather(first_group, ROW, row_total))
    laurel_all = first_all[:, :, :small_rows].reshape(-1, line)
    laurel_down_all = laurel_all[:, :rank]
    laurel_up_all = laurel_all[:, rank:]
    gain_rows = first_all[:, :, small_rows : small_rows + gain_lines].astype(wide)
    gain_rows = gain_rows.reshape(row_total, col_total, gain_lines * line)
    gains = gain_rows[:, :, : 6 * small_rows].reshape(row_total, col_total, 6, small_rows)
    gains = jnp.transpose(gains, (2, 0, 1, 3)).reshape(6, width)
    gain_list = [gains[i] for i in range(6)]
    head_gains = []
    for i in range(2):
        start = 6 * small_rows + i * head_part
        rel = gain_rows[:, :, start : start + head_part].reshape(-1)
        head_gains.append(xor_blocks(rel, me_row, row_total))

    kv_pieces, kv_first, kv_last = gather_weight(
        jnp.concatenate([key_weight, value_weight], axis=1), pairs, row_total, True
    )
    query_pieces, _, query_last = gather_weight(
        query_weight, pairs, row_total, False, kv_first, kv_last
    )
    tokens_at = me_col * rows + jnp.arange(rows, dtype=jnp.int32)
    position, begin, reach = placement_info(seq_lengths[0], tokens_at)
    window = jnp.stack([begin, reach])
    span = jnp.stack([jnp.min(begin) // rows, (jnp.max(reach) + rows - 1) // rows])
    inputs = xor_blocks(layer_input, me_row, row_total).astype(wide)
    cotangent = xor_blocks(out_cotangent, me_row, row_total).astype(wide)
    normed, input_pull = jax.vjp(rms_scale, inputs, gain_list[0])
    normed_low = normed.astype(low)
    cosine, sine_part = angles(position)
    query_gain_row = head_gains[0].reshape(1, HEAD)
    key_gain_row = head_gains[1].reshape(1, HEAD)
    kv_own = project(me, normed_low, kv_pieces)
    pair_own = small_call(
        partial(pair_body, col_total),
        jax.ShapeDtypeStruct((2, rows, KV_HEADS * HEAD), low),
        kv_own,
        key_gain_row,
        cosine,
        sine_part,
    )
    pair_all = lax.all_gather(pair_own, COL, axis=0, tiled=True)
    pair_all = pair_all.reshape(col_total, 2, rows, KV_HEADS * HEAD)
    query_own = project(me, normed_low, query_pieces)
    query_scaled = small_call(
        partial(query_body, 1.0 / math.sqrt(HEAD)),
        jax.ShapeDtypeStruct((rows, HEADS * HEAD), low),
        query_own,
        query_gain_row,
        cosine,
        sine_part,
    )
    out_pieces, _, out_last = gather_weight(
        out_weight, pairs, row_total, False, kv_first, query_last, query_own
    )
    attended, inverse = attend(span, jnp.transpose(window), query_scaled, pair_all)
    attention_out = contract(me, attended, out_pieces)
    laurel_mid = product(normed_low, laurel_down_all).astype(low)
    laurel_out = product_t(laurel_mid, laurel_up_all)
    (mixed, feed_in), mix_pull = jax.vjp(
        residual_mix,
        inputs,
        attention_out,
        normed_low.astype(wide),
        laurel_out,
        gain_list[1],
        gain_list[2],
        gain_list[3],
    )
    feed_low = feed_in.astype(low)
    feed_pieces = xor_gather(
        after(jnp.concatenate([gate_weight, up_weight], axis=1), out_last), ROW, row_total, feed_low
    )
    down_pieces = xor_gather(down_weight, ROW, row_total, feed_pieces[-1])
    layer_own = jnp.concatenate([per_layer_gate, per_layer_projection], axis=1)
    layer_group = over_col(me, after(layer_own, feed_low), pairs)
    layer_pieces = direct_gather(after(layer_group, down_pieces[-1]), ROW, row_total)
    layer_all = jnp.concatenate([one.reshape(-1, 2 * embed) for one in layer_pieces], axis=0)
    layer_gate_all = layer_all[:, :embed]
    layer_proj_all = layer_all[:, embed:]
    feed_all = jnp.concatenate(feed_pieces, axis=0)
    down_all = jnp.concatenate(down_pieces, axis=0)
    halves = 2
    part_rows = rows // halves
    feed_tokens, hidden_pulls, hidden_lows, down_outs = [], [], [], []
    done = None
    for h in range(halves):
        tokens = lax.all_gather(
            feed_low[h * part_rows : (h + 1) * part_rows], COL, axis=0, tiled=True
        )
        tokens = tokens if done is None else after(tokens, done)
        gate_up = product(tokens, feed_all).astype(low)
        hidden, hidden_pull = jax.vjp(
            geglu, gate_up[:, :feed_width].astype(wide), gate_up[:, feed_width:].astype(wide)
        )
        hidden_low = hidden.astype(low)
        done = product_t(hidden_low, down_all).astype(low)
        down_outs.append(lax.psum_scatter(done, COL, scatter_dimension=0, tiled=True))
        feed_tokens.append(tokens)
        hidden_pulls.append(hidden_pull)
        hidden_lows.append(hidden_low)
    down_out = jnp.concatenate(down_outs, axis=0).astype(wide)
    after_feed, feed_pull = jax.vjp(feed_mix, mixed, down_out, gain_list[4])
    after_low = after_feed.astype(low)
    per_pre = product(after_low, layer_gate_all)
    per_hidden, per_pull = jax.vjp(geglu, per_pre, per_layer_input.astype(wide))
    per_low = per_hidden.astype(low)
    per_out = product_t(per_low, layer_proj_all)
    output, final_pull = jax.vjp(final_mix, after_feed, per_out, gain_list[5])
    after_grad, per_out_grad, final_gain_grad = final_pull(cotangent)
    per_out_low = per_out_grad.astype(low)
    per_hidden_grad = product(per_out_low, layer_proj_all)
    layer_proj_grad = product_tn(per_out_low, per_low)
    per_pre_grad, embed_grad = per_pull(per_hidden_grad)
    per_pre_low = per_pre_grad.astype(low)
    after_grad = after_grad + product_t(per_pre_low, layer_gate_all)
    layer_gate_grad = product_tn(after_low, per_pre_low)
    mixed_grad, down_grad, post_gain_grad = feed_pull(after_grad)
    down_low = down_grad.astype(low)
    layer_grad = scatter_small(
        me,
        after(jnp.concatenate([layer_gate_grad, layer_proj_grad], axis=1).astype(low), down_low),
        row_total,
        col_total,
    )
    attended_pair = pair_columns(me, after(attended, down_low), col_total)
    normed_pair = pair_rows(after(normed_low, down_low))
    down_tokens, feed_grads, feed_in_grads = [], [], []
    done = None
    for h in range(halves):
        tokens = lax.all_gather(
            down_low[h * part_rows : (h + 1) * part_rows], COL, axis=0, tiled=True
        )
        if done is None:
            tokens, layer_grad, attended_pair, normed_pair = lax.optimization_barrier(
                (tokens, layer_grad, attended_pair, normed_pair)
            )
        else:
            tokens = after(tokens, done)
        hidden_grad = product(tokens, down_all)
        gate_grad, up_grad = hidden_pulls[h](hidden_grad)
        feed_grad_low = jnp.concatenate([gate_grad.astype(low), up_grad.astype(low)], axis=1)
        done = product_t(feed_grad_low, feed_all).astype(low)
        feed_in_grads.append(lax.psum_scatter(done, COL, scatter_dimension=0, tiled=True))
        down_tokens.append(tokens)
        feed_grads.append(feed_grad_low)
    feed_in_grad = jnp.concatenate(feed_in_grads, axis=0).astype(wide)
    down_total = sum(
        product_tn(after(down_tokens[h], done), hidden_lows[h]) for h in range(halves)
    ).astype(low)
    feed_total = sum(
        product_tn(after(feed_tokens[h], down_total), feed_grads[h]) for h in range(halves)
    ).astype(low)
    (
        inputs_grad,
        attention_grad,
        normed_grad,
        laurel_out_grad,
        attention_gain_grad,
        laurel_gain_grad,
        pre_gain_grad,
    ) = mix_pull((mixed_grad, feed_in_grad))
    attention_low = attention_grad.astype(low)
    attended_grad = project(me, attention_low, out_pieces)
    query_rot_grad, pair_parts = attend_back(
        span, window, query_scaled, pair_all, attended_grad, attended, inverse
    )
    pair_sum = lax.psum_scatter(
        pair_parts.reshape(2 * col_total, rows, KV_HEADS * HEAD),
        COL,
        scatter_dimension=0,
        tiled=True,
    )
    attention_pair = pair_rows(attention_low)
    out_total = product_tn(after(attention_pair, pair_parts), attended_pair).astype(low)
    query_rot_grad = after(query_rot_grad, out_total)
    gain_row = jax.ShapeDtypeStruct((1, HEAD), wide)
    query_low, query_gain_grad = small_call(
        query_back_body,
        (jax.ShapeDtypeStruct((rows, HEADS * HEAD), low), gain_row),
        query_own,
        query_rot_grad,
        query_gain_row,
        cosine,
        sine_part,
    )
    query_total = product_tn(
        after(normed_pair, out_total), pair_columns(me, query_low, col_total)
    ).astype(low)
    query_part = contract(me, after(query_low, query_total), query_pieces)

    laurel_out_low = after(laurel_out_grad.astype(low), query_total)
    laurel_mid_grad = product(laurel_out_low, laurel_up_all)
    laurel_up_grad = product_tn(laurel_out_low, laurel_mid)
    laurel_mid_low = laurel_mid_grad.astype(low)
    laurel_down_grad = product_tn(normed_low, laurel_mid_low)
    small_total = jnp.concatenate([laurel_down_grad, laurel_up_grad], axis=1)
    normed_grad = normed_grad + product_t(laurel_mid_low, laurel_down_all) + query_part
    pair_sum = after(pair_sum, normed_grad, small_total)
    kv_grad, key_gain_grad = small_call(
        partial(pair_back_body, col_total),
        (jax.ShapeDtypeStruct(kv_own.shape, low), gain_row),
        kv_own,
        pair_sum,
        key_gain_row,
        cosine,
        sine_part,
    )
    kv_total = product_tn(normed_pair, pair_columns(me, kv_grad, col_total)).astype(low)
    marks = []
    normed_grad = normed_grad + contract(me, after(kv_grad, kv_total), kv_pieces)
    kv_weight_grad = scatter_cols(kv_total, row_total, pairs, normed_grad, None, marks)
    mark = marks[0]
    query_marks = []
    query_weight_grad = scatter_cols(query_total, row_total, pairs, mark, mark, query_marks)
    out_weight_grad = scatter_cols(out_total, row_total, pairs, query_part, mark)
    down_weight_grad = scatter_rows(down_total, row_total, feed_total, query_marks[0])
    feed_weight_grad = scatter_rows(feed_total, row_total, attended_grad, marks[-1])
    input_part, input_gain_grad = input_pull(after(normed_grad, mark))
    input_total = xor_blocks((inputs_grad + input_part).astype(low), me_row, row_total)

    wide_gains = jnp.stack(
        [
            input_gain_grad,
            attention_gain_grad,
            laurel_gain_grad,
            pre_gain_grad,
            post_gain_grad,
            final_gain_grad,
        ]
    ).reshape(6, row_total, col_total, small_rows)
    wide_gains = jnp.transpose(wide_gains, (2, 1, 0, 3)).reshape(col_total, row_total, -1)
    both_gains = jnp.concatenate([query_gain_grad, key_gain_grad], axis=0)
    both_gains = xor_blocks(both_gains, me_row, row_total)
    both_gains = both_gains.reshape(2, row_total, col_total, head_part)
    both_gains = jnp.transpose(both_gains, (2, 1, 0, 3)).reshape(col_total, row_total, -1)
    gain_sums = jnp.concatenate([wide_gains, both_gains], axis=2)
    gain_sums = jnp.pad(gain_sums, ((0, 0), (0, 0), (0, gain_lines * line - gain_total)))
    gain_sums = gain_sums.reshape(col_total, row_total, gain_lines, line)
    laurel_parts = jnp.transpose(
        small_total.reshape(row_total, col_total, small_rows, line), (1, 0, 2, 3)
    )
    sums = jnp.concatenate([laurel_parts, gain_sums], axis=2)
    sums = lax.all_to_all(after(sums, query_marks[0]), COL, 0, 0, tiled=True)
    sums = jnp.sum(after(sums, query_marks[-1]), axis=0)
    sums = sums[0] + sum(hop(sums[j], ROW, j) for j in range(1, row_total))
    laurel_grad = sums[:small_rows]
    gain_sums = sums[small_rows:].reshape(-1)
    gain_out = [gain_sums[i * small_rows : (i + 1) * small_rows] for i in range(6)]
    head_out = gain_sums[6 * small_rows : gain_total]
    return (
        xor_blocks(output.astype(low), me_row, row_total),
        input_total,
        embed_grad.astype(low),
        query_weight_grad,
        kv_weight_grad[:, :kv_width],
        kv_weight_grad[:, kv_width:],
        out_weight_grad,
        feed_weight_grad[:, :feed_width],
        feed_weight_grad[:, feed_width:],
        down_weight_grad,
        laurel_grad[:, :rank],
        laurel_grad[:, rank:],
        layer_grad[:, :embed],
        layer_grad[:, embed:],
        gain_out[0],
        head_out[:head_part],
        head_out[head_part:],
        gain_out[1],
        gain_out[2],
        gain_out[3],
        gain_out[4],
        gain_out[5],
    )


def solution(mesh):
    in_specs = (
        P((ROW, COL), None),
        P((ROW, COL), None),
        P((ROW, COL), None),
        P(ROW, None),
        P(ROW, COL),
        P(ROW, COL),
        P(ROW, COL),
        P(ROW, COL),
        P(ROW, COL),
        P(ROW, COL),
        P(ROW, COL),
        P((ROW, COL), None),
        P((ROW, COL), None),
        P((ROW, COL), None),
        P((ROW, COL), None),
        P((ROW, COL)),
        P((ROW, COL)),
        P((ROW, COL)),
        P((ROW, COL)),
        P((ROW, COL)),
        P((ROW, COL)),
        P((ROW, COL)),
        P((ROW, COL)),
    )
    out_specs = (
        P((ROW, COL), None),
        P((ROW, COL), None),
        P((ROW, COL), None),
        P(ROW, COL),
        P(ROW, COL),
        P(ROW, COL),
        P(ROW, COL),
        P(ROW, COL),
        P(ROW, COL),
        P(ROW, COL),
        P((ROW, COL), None),
        P((ROW, COL), None),
        P((ROW, COL), None),
        P((ROW, COL), None),
        P((ROW, COL)),
        P((ROW, COL)),
        P((ROW, COL)),
        P((ROW, COL)),
        P((ROW, COL)),
        P((ROW, COL)),
        P((ROW, COL)),
        P((ROW, COL)),
    )

    return jax.shard_map(local, mesh=mesh, in_specs=in_specs, out_specs=out_specs, check_vma=False)
```

profile of v0, /device:TPU:0, one launch (start us, length us, event | category | flops | bytes accessed | tf_op | source)
XLA Modules:
  0.0 1123.1 jit_solution(9205688647706219161)
XLA Ops:
  44.5 9.7 collective-permute-done.1
  58.9 7.9 collective-permute-done.17.refs_1_
  83.4 14.0 %collective-permute-done.4.refs_1_ = bf16[512,256]{1,0:T(8,128)(2,1)S(1)} collective-permute-done((bf16[512,256]{1,0:T(8,128)(2,1)S(1)}, bf16[512,256]{1,0:T(8,128)(2,1)S(1)}, u32[]{:S(2)}, u32[]{:S(2)}) %collective-permute-start.4) | collective-permute-done | bytes 262176 | tf_op jit(solution)/shard_map/ppermute | solution.py:193
  97.4 12.0 %collective-permute-done.5.refs_2_ = bf16[512,256]{1,0:T(8,128)(2,1)S(1)} collective-permute-done((bf16[512,256]{1,0:T(8,128)(2,1)S(1)}, bf16[512,256]{1,0:T(8,128)(2,1)S(1)}, u32[]{:S(2)}, u32[]{:S(2)}) %collective-permute-start.5) | collective-permute-done | bytes 262176 | tf_op jit(solution)/shard_map/ppermute | solution.py:193
  115.1 21.1 %collective-permute-done.10.refs_1_ = bf16[4,512,256]{2,1,0:T(8,128)(2,1)S(1)} collective-permute-done((bf16[4,512,256]{2,1,0:T(8,128)(2,1)}, bf16[4,512,256]{2,1,0:T(8,128)(2,1)S(1)}, u32[]{:S(2)}, u32[]{:S(2)}) %collective-permute-start.10) | collective-permute-done | bytes 1048608 | tf_op jit(solution)/shard_map/ppermute | solution.py:193
  138.0 14.1 %collective-permute-start.23 = (bf16[512,256]{1,0:T(8,128)(2,1)S(1)}, bf16[512,256]{1,0:T(8,128)(2,1)S(1)}, u32[]{:S(2)}, u32[]{:S(2)}) collective-permute-start(bf16[512,256]{1,0:T(8,128)(2,1)S(1)} %copy-done.70), channel_id=1, source_target_pairs={{0,2},{1,3},{2,0},{3,1},{4,6},{5,7},{6,4},{7,5},{8,10},{9,11},{10,... | collective-permute-start | bytes 786440 | tf_op jit(solution)/shard_map/ppermute | solution.py:193
  154.6 8.7 collective-permute-done.23.refs_1_
  163.3 10.2 collective-permute-done.24.refs_2_
  180.5 7.1 shard_map.392.query_ref
  187.7 14.2 %collective-permute-done.27.refs_2_ = bf16[4,512,256]{2,1,0:T(8,128)(2,1)} collective-permute-done((bf16[4,512,256]{2,1,0:T(8,128)(2,1)}, bf16[4,512,256]{2,1,0:T(8,128)(2,1)}, u32[]{:S(2)}, u32[]{:S(2)}) %collective-permute-start.27) | collective-permute-done | bytes 1048608 | tf_op jit(solution)/shard_map/ppermute | solution.py:193
  213.5 7.7 collective-permute-done.28.refs_3_
  228.1 9.8 shard_map.396
  237.9 7.4 shard_map.398
  258.1 45.3 %collective-permute-done.34 = bf16[512,2048]{1,0:T(8,128)(2,1)} collective-permute-done((bf16[512,2048]{1,0:T(8,128)(2,1)}, bf16[512,2048]{1,0:T(8,128)(2,1)}, u32[]{:S(2)}, u32[]{:S(2)}) %collective-permute-start.34) | collective-permute-done | bytes 2097184 | tf_op jit(solution)/shard_map/ppermute | solution.py:193
  308.3 22.8 %collective-permute-done.36 = bf16[512,1024]{1,0:T(8,128)(2,1)S(1)} collective-permute-done((bf16[512,1024]{1,0:T(8,128)(2,1)S(1)}, bf16[512,1024]{1,0:T(8,128)(2,1)S(1)}, u32[]{:S(2)}, u32[]{:S(2)}) %collective-permute-start.36) | collective-permute-done | bytes 1048608 | tf_op jit(solution)/shard_map/ppermute | solution.py:193
  332.2 21.6 %collective-permute-done.37 = bf16[512,1024]{1,0:T(8,128)(2,1)S(1)} collective-permute-done((bf16[512,1024]{1,0:T(8,128)(2,1)S(1)}, bf16[512,1024]{1,0:T(8,128)(2,1)S(1)}, u32[]{:S(2)}, u32[]{:S(2)}) %collective-permute-start.37) | collective-permute-done | bytes 1048608 | tf_op jit(solution)/shard_map/ppermute | solution.py:193
  360.9 9.0 collective-permute-done.38
  370.9 13.0 %convolution_convert_fusion.5 = bf16[1024,2048]{1,0:T(8,128)(2,1)S(1)} fusion(bf16[1024,2048]{1,0:T(8,128)(2,1)} %all-gather.8.cloned.1.call-done, bf16[2048,2048]{1,0:T(8,128)(2,1)} %copy-done.63), kind=kOutput, calls=%fused_computation.52 | convolution fusion | flops 8592031744 | bytes 16777216 | tf_op jit(solution)/shard_map/dot_general | solution.py:176
  385.9 8.9 convolution_convert_fusion.7
  394.9 12.5 %convolution_convert_fusion.4 = bf16[1024,2048]{1,0:T(8,128)(2,1)S(1)} fusion(bf16[1024,2048]{1,0:T(8,128)(2,1)} %all-gather.10.cloned.1.call-done, bf16[2048,2048]{1,0:T(8,128)(2,1)} %copy-done.63), kind=kOutput, calls=%fused_computation.51 | convolution fusion | flops 8592031744 | bytes 16777216 | tf_op jit(solution)/shard_map/dot_general | solution.py:176
  409.4 8.9 convolution_convert_fusion.6
  419.2 12.3 %collective-permute-start.39 = (bf16[64,512]{1,0:T(8,128)(2,1)S(1)}, bf16[64,512]{1,0:T(8,128)(2,1)S(1)}, u32[]{:S(2)}, u32[]{:S(2)}) collective-permute-start(bf16[64,512]{1,0:T(8,128)(2,1)S(1)} %pad_maximum_fusion.24.refs_0_), channel_id=1, source_target_pairs={{0,2},{1,3},{2,0},{3,1},{4,6},{5,7},{6,4},{7,5},{8,10},{9,11},{10,... | collective-permute-start | bytes 196616 | tf_op jit(solution)/shard_map/ppermute | solution.py:193
  434.5 7.5 collective-permute-done.40.refs_2_
  455.2 10.1 collective-permute-done.45
  465.3 9.6 collective-permute-done.44
  478.5 53.5 %reduce-scatter.6.cloned.1.call-done = bf16[128,2048]{1,0:T(8,128)(2,1)} async-done(((bf16[1024,2048]{1,0:T(8,128)(2,1)}), bf16[128,2048]{1,0:T(8,128)(2,1)}) %reduce-scatter.6.cloned.1.call-update) | async-done | bytes 524304 | tf_op jit(solution)/shard_map/reduce_scatter | solution.py:798
  596.0 11.4 %fusion.9 = (bf16[1024,1024]{1,0:T(8,128)(2,1)S(1)}, bf16[1024,1024]{1,0:T(8,128)(2,1)S(1)}) fusion(bf16[1024,2048]{1,0:T(8,128)(2,1)} %copy-done.133, bf16[1024,2048]{1,0:T(8,128)(2,1)} %all-gather.12.cloned.1.call-done, bf16[2048,1024]{1,0:T(8,128)(2,1)} %constant_dynamic-update-slice_fusion.4), kind=kOutput, calls=%fused_computation.25 | convolution fusion | flops 4322230272 | bytes 16777216 | tf_op jit(solution)/shard_map/dot_general | solution.py:176
  609.4 12.7 %convolution_convert_fusion.3 = bf16[1024,2048]{1,0:T(8,128)(2,1)} fusion(bf16[2048,2048]{1,0:T(8,128)(2,1)} %copy-done.63, bf16[1024,1024]{1,0:T(8,128)(2,1)S(1)} %get-tuple-element.189, bf16[1024,1024]{1,0:T(8,128)(2,1)S(1)} %get-tuple-element.188), kind=kOutput, calls=%fused_computation.50 | convolution fusion | flops 8600420352 | bytes 16777216 | tf_op jit(solution)/shard_map/dot_general | solution.py:180
  622.1 21.6 %all-gather.14.cloned.1.call-done = bf16[1024,2048]{1,0:T(8,128)(2,1)} async-done(((bf16[128,2048]{1,0:T(8,128)(2,1)}), bf16[1024,2048]{1,0:T(8,128)(2,1)}) %all-gather.14.cloned.1.call-update) | async-done | bytes 4194320 | tf_op jit(solution)/shard_map/all_gather | solution.py:831
  643.7 11.7 %fusion.6 = (bf16[1024,1024]{1,0:T(8,128)(2,1)S(1)}, bf16[1024,1024]{1,0:T(8,128)(2,1)S(1)}) fusion(bf16[1024,2048]{1,0:T(8,128)(2,1)} %copy-done.134, bf16[1024,2048]{1,0:T(8,128)(2,1)} %all-gather.14.cloned.1.call-done, bf16[2048,1024]{1,0:T(8,128)(2,1)} %constant_dynamic-update-slice_fusion.4), kind=kOutput, calls=%fused_computation.22 | convolution fusion | flops 4322230272 | bytes 16777216 | tf_op jit(solution)/shard_map/dot_general | solution.py:176
  657.4 12.6 %convolution_convert_fusion.2 = bf16[1024,2048]{1,0:T(8,128)(2,1)} fusion(bf16[2048,2048]{1,0:T(8,128)(2,1)} %copy-done.63, bf16[1024,1024]{1,0:T(8,128)(2,1)S(1)} %get-tuple-element.187, bf16[1024,1024]{1,0:T(8,128)(2,1)S(1)} %get-tuple-element.186), kind=kOutput, calls=%fused_computation.49 | convolution fusion | flops 8600420352 | bytes 16777216 | tf_op jit(solution)/shard_map/dot_general | solution.py:180
  670.9 10.8 fusion.108
  681.8 9.5 add_convert_fusion.1
  691.3 12.8 %fusion.21 = f32[2048,2048]{1,0:T(8,128)} fusion(bf16[1024,2048]{1,0:T(8,128)(2,1)S(1)} %copy-done.129, bf16[1024,1024]{1,0:T(8,128)(2,1)} %copy-done.137, bf16[1024,1024]{1,0:T(8,128)(2,1)S(1)} %copy-done.136), kind=kOutput, calls=%fused_computation.71 | convolution fusion | flops 8598323200 | bytes 25165824 | tf_op jit(solution)/shard_map/dot_general | solution.py:186
  704.1 14.8 %reduce-scatter.12.cloned.1.call-done = bf16[128,2048]{1,0:T(8,128)(2,1)} async-done(((bf16[1024,2048]{1,0:T(8,128)(2,1)}), bf16[128,2048]{1,0:T(8,128)(2,1)}) %reduce-scatter.12.cloned.1.call-update) | async-done | bytes 524304 | tf_op jit(solution)/shard_map/reduce_scatter | solution.py:844
  718.9 50.7 %reduce-scatter.10.cloned.1.call-done = bf16[128,2048]{1,0:T(8,128)(2,1)} async-done(((bf16[1024,2048]{1,0:T(8,128)(2,1)}), bf16[128,2048]{1,0:T(8,128)(2,1)}) %reduce-scatter.10.cloned.1.call-update) | async-done | bytes 524304 | tf_op jit(solution)/shard_map/reduce_scatter | solution.py:844
  778.4 7.1 shard_map.403.grad_ref
  785.4 13.1 %shard_map.404 = (f32[256,2048]{1,0:T(8,128)}, bf16[8,2,256,512]{3,2,1,0:T(8,128)(2,1)}) custom-call(s32[2]{0:T(128)} %pad_add_fusion.1.span_ref, s32[2,256]{1,0:T(2,128)} %get-tuple-element.267.window_ref, bf16[256,2048]{1,0:T(8,128)(2,1)} %shard_map.393.query_ref, bf16[8,2,256,512]{3,2,1,0:T(8,128)(2,1)} %bitcast.129, bf16[8,2,256,512]{3,2,1,0:T(8,128)(2,1)} %bitcast.130, ...), custom_call_target="tpu_custom_call" | custom-call | flops 10737418240 | bytes 8388608 | tf_op jit(solution)/shard_map/pallas_call | solution.py:600
  800.2 16.2 %add_convert_fusion = bf16[2048,2048]{1,0:T(8,128)(2,1)} fusion(f32[2048,2048]{1,0:T(8,128)} %fusion.21, bf16[1024,2048]{1,0:T(8,128)(2,1)} %all-gather.10.cloned.1.call-done, bf16[1024,1024]{1,0:T(8,128)(2,1)} %copy-done.140, bf16[1024,1024]{1,0:T(8,128)(2,1)S(1)} %copy-done.139), kind=kOutput, calls=%fused_computation | convolution fusion | flops 8606711808 | bytes 33554432 | tf_op jit(solution)/shard_map/dot_general | solution.py:186
  833.0 26.4 %collective-permute-done.80 = bf16[512,1024]{1,0:T(8,128)(2,1)} collective-permute-done((bf16[512,1024]{1,0:T(8,128)(2,1)}, bf16[512,1024]{1,0:T(8,128)(2,1)}, u32[]{:S(2)}, u32[]{:S(2)}) %collective-permute-start.80) | collective-permute-done | bytes 1048608 | tf_op jit(solution)/shard_map/ppermute | solution.py:199
  901.7 8.0 shard_map.407
  928.8 6.0 shard_map.410
  957.8 44.7 %collective-permute-done.79 = bf16[512,1024]{1,0:T(8,128)(2,1)} collective-permute-done((bf16[512,1024]{1,0:T(8,128)(2,1)S(1)}, bf16[512,1024]{1,0:T(8,128)(2,1)}, u32[]{:S(2)}, u32[]{:S(2)}) %collective-permute-start.79) | collective-permute-done | bytes 1048608 | tf_op jit(solution)/shard_map/ppermute | solution.py:199
  1010.1 16.7 %all-to-all-start.1 = ((f32[8,4,68,128]{3,1,2,0:T(4,128)}), f32[8,4,68,128]{3,1,2,0:T(4,128)}, u32[]{:S(2)}, u32[]{:S(2)}) async-start(f32[8,4,68,128]{3,1,2,0:T(4,128)} %copy.98), calls=%async_computation.6 | async-start | bytes 2228224 | tf_op jit(solution)/shard_map/all_to_all | solution.py:944
  1037.2 24.6 %collective-permute-done.74 = bf16[512,256]{1,0:T(8,128)(2,1)S(1)} collective-permute-done((bf16[512,256]{1,0:T(8,128)(2,1)S(1)}, bf16[512,256]{1,0:T(8,128)(2,1)S(1)}, u32[]{:S(2)}, u32[]{:S(2)}) %collective-permute-start.74) | collective-permute-done | bytes 262176 | tf_op jit(solution)/shard_map/ppermute | solution.py:199
  1061.8 5.9 collective-permute-start.61
  1069.5 8.4 collective-permute-done.73
  1096.0 7.3 collective-permute-done.63
  (650 shorter events, 372.1 us)
Async XLA Ops:
  9.3 27.9 %collective-permute-start.3 = (bf16[512,128]{1,0:T(8,128)(2,1)S(1)}, bf16[512,128]{1,0:T(8,128)(2,1)S(1)}, u32[]{:S(2)}, u32[]{:S(2)}) collective-permute-start(bf16[512,128]{1,0:T(8,128)(2,1)S(1)} %pad_maximum_fusion.23.refs_0_), channel_id=1, source_target_pairs={{0,6},{1,7},{2,4},{3,5},{4,2},{5,3},{6,0},{7,1},{8,14},{9,15},{10,... | collective-permute-start | bytes 393224 | tf_op jit(solution)/shard_map/ppermute | solution.py:193
  14.5 23.3 %collective-permute-start.7 = (bf16[512,128]{1,0:T(8,128)(2,1)S(1)}, bf16[512,128]{1,0:T(8,128)(2,1)S(1)}, u32[]{:S(2)}, u32[]{:S(2)}) collective-permute-start(bf16[512,128]{1,0:T(8,128)(2,1)S(1)} %pad_maximum_fusion.23.refs_0_), channel_id=1, source_target_pairs={{0,2},{1,3},{2,0},{3,1},{4,6},{5,7},{6,4},{7,5},{8,10},{9,11},{10,... | collective-permute-start | bytes 393224 | tf_op jit(solution)/shard_map/ppermute | solution.py:193
  14.5 23.3 %collective-permute-start.8 = (bf16[512,128]{1,0:T(8,128)(2,1)S(1)}, bf16[512,128]{1,0:T(8,128)(2,1)S(1)}, u32[]{:S(2)}, u32[]{:S(2)}) collective-permute-start(bf16[512,128]{1,0:T(8,128)(2,1)S(1)} %pad_maximum_fusion.23.refs_0_), channel_id=1, source_target_pairs={{0,4},{1,5},{2,6},{3,7},{4,0},{5,1},{6,2},{7,3},{8,12},{9,13},{10,... | collective-permute-start | bytes 393224 | tf_op jit(solution)/shard_map/ppermute | solution.py:193
  27.1 201.0 %all-gather.6.cloned.1.call-start = ((), (), s32[]{:S(2)}) async-start(), calls=%async_computation.7 | async-start | bytes 4718592 | tf_op jit(solution)/shard_map/all_gather | solution.py:742
  41.0 26.3 %collective-permute-start.9 = (bf16[4,512,128]{2,1,0:T(8,128)(2,1)}, bf16[4,512,128]{2,1,0:T(8,128)(2,1)S(1)}, u32[]{:S(2)}, u32[]{:S(2)}) collective-permute-start(bf16[4,512,128]{2,1,0:T(8,128)(2,1)} %shard_map.391.refs_0_), channel_id=1, source_target_pairs={{0,24},{8,16},{16,8},{24,0},{1,25},{9,17},{17,9},{25,1},{2,26},{10... | collective-permute-start | bytes 1572872 | tf_op jit(solution)/shard_map/ppermute | solution.py:193
  43.5 23.3 %collective-permute-start.17 = (bf16[4,512,128]{2,1,0:T(8,128)(2,1)}, bf16[4,512,128]{2,1,0:T(8,128)(2,1)S(1)}, u32[]{:S(2)}, u32[]{:S(2)}) collective-permute-start(bf16[4,512,128]{2,1,0:T(8,128)(2,1)} %shard_map.391.refs_0_), channel_id=1, source_target_pairs={{0,8},{8,0},{16,24},{24,16},{1,9},{9,1},{17,25},{25,17},{2,10},{10... | collective-permute-start | bytes 1572872 | tf_op jit(solution)/shard_map/ppermute | solution.py:193
  78.6 292.4 %all-gather.8.cloned.1.call-start = ((), (), s32[]{:S(2)}) async-start(), calls=%async_computation.8 | async-start | bytes 4718592 | tf_op jit(solution)/shard_map/all_gather | solution.py:788
  80.2 29.1 %collective-permute-start.5 = (bf16[512,256]{1,0:T(8,128)(2,1)S(1)}, bf16[512,256]{1,0:T(8,128)(2,1)S(1)}, u32[]{:S(2)}, u32[]{:S(2)}) collective-permute-start(bf16[512,256]{1,0:T(8,128)(2,1)S(1)} %copy-done.69), channel_id=1, source_target_pairs={{0,4},{1,5},{2,6},{3,7},{4,0},{5,1},{6,2},{7,3},{8,12},{9,13},{10,... | collective-permute-start | bytes 786440 | tf_op jit(solution)/shard_map/ppermute | solution.py:193
  81.9 27.7 %collective-permute-start.6 = (bf16[512,256]{1,0:T(8,128)(2,1)S(1)}, bf16[512,256]{1,0:T(8,128)(2,1)S(1)}, u32[]{:S(2)}, u32[]{:S(2)}) collective-permute-start(bf16[512,256]{1,0:T(8,128)(2,1)S(1)} %copy-done.69), channel_id=1, source_target_pairs={{0,6},{1,7},{2,4},{3,5},{4,2},{5,3},{6,0},{7,1},{8,14},{9,15},{10,... | collective-permute-start | bytes 786440 | tf_op jit(solution)/shard_map/ppermute | solution.py:193
  137.6 35.9 %collective-permute-start.12 = (bf16[4,512,256]{2,1,0:T(8,128)(2,1)S(1)}, bf16[4,512,256]{2,1,0:T(8,128)(2,1)}, u32[]{:S(2)}, u32[]{:S(2)}) collective-permute-start(bf16[4,512,256]{2,1,0:T(8,128)(2,1)S(1)} %broadcast_select_fusion.7), channel_id=1, source_target_pairs={{0,16},{1,9},{2,18},{3,11},{4,20},{5,13},{6,22},{7,15},{8,24},{9,1... | collective-permute-start | bytes 3145736 | tf_op jit(solution)/shard_map/ppermute | solution.py:199
  138.0 40.4 %collective-permute-start.13 = (bf16[4,512,256]{2,1,0:T(8,128)(2,1)S(1)}, bf16[4,512,256]{2,1,0:T(8,128)(2,1)}, u32[]{:S(2)}, u32[]{:S(2)}) collective-permute-start(bf16[4,512,256]{2,1,0:T(8,128)(2,1)S(1)} %copy-done.11), channel_id=1, source_target_pairs={{0,1},{1,0},{2,3},{3,2},{4,5},{5,4},{6,7},{7,6},{8,9},{9,8},{10,11... | collective-permute-start | bytes 3145736 | tf_op jit(solution)/shard_map/ppermute | solution.py:193
  138.0 25.3 %collective-permute-start.23 = (bf16[512,256]{1,0:T(8,128)(2,1)S(1)}, bf16[512,256]{1,0:T(8,128)(2,1)S(1)}, u32[]{:S(2)}, u32[]{:S(2)}) collective-permute-start(bf16[512,256]{1,0:T(8,128)(2,1)S(1)} %copy-done.70), channel_id=1, source_target_pairs={{0,2},{1,3},{2,0},{3,1},{4,6},{5,7},{6,4},{7,5},{8,10},{9,11},{10,... | collective-permute-start | bytes 786440 | tf_op jit(solution)/shard_map/ppermute | solution.py:193
  176.5 25.4 %collective-permute-start.27 = (bf16[4,512,256]{2,1,0:T(8,128)(2,1)}, bf16[4,512,256]{2,1,0:T(8,128)(2,1)}, u32[]{:S(2)}, u32[]{:S(2)}) collective-permute-start(bf16[4,512,256]{2,1,0:T(8,128)(2,1)} %shard_map.397.refs_0_), channel_id=1, source_target_pairs={{0,16},{8,24},{16,0},{24,8},{1,17},{9,25},{17,1},{25,9},{2,18},{10... | collective-permute-start | bytes 3145736 | tf_op jit(solution)/shard_map/ppermute | solution.py:193
  178.4 25.5 %collective-permute-start.26 = (bf16[4,512,256]{2,1,0:T(8,128)(2,1)}, bf16[4,512,256]{2,1,0:T(8,128)(2,1)}, u32[]{:S(2)}, u32[]{:S(2)}) collective-permute-start(bf16[4,512,256]{2,1,0:T(8,128)(2,1)} %shard_map.397.refs_0_), channel_id=1, source_target_pairs={{0,8},{8,0},{16,24},{24,16},{1,9},{9,1},{17,25},{25,17},{2,10},{10... | collective-permute-start | bytes 3145736 | tf_op jit(solution)/shard_map/ppermute | solution.py:193
  212.8 25.0 %collective-permute-start.29 = (bf16[4,512,256]{2,1,0:T(8,128)(2,1)S(1)}, bf16[4,512,256]{2,1,0:T(8,128)(2,1)}, u32[]{:S(2)}, u32[]{:S(2)}) collective-permute-start(bf16[4,512,256]{2,1,0:T(8,128)(2,1)S(1)} %copy-done.14), channel_id=1, source_target_pairs={{0,1},{1,0},{2,3},{3,2},{4,5},{5,4},{6,7},{7,6},{8,9},{9,8},{10,11... | collective-permute-start | bytes 3145736 | tf_op jit(solution)/shard_map/ppermute | solution.py:193
  212.9 24.9 %collective-permute-start.30 = (bf16[4,512,256]{2,1,0:T(8,128)(2,1)}, bf16[4,512,256]{2,1,0:T(8,128)(2,1)}, u32[]{:S(2)}, u32[]{:S(2)}) collective-permute-start(bf16[4,512,256]{2,1,0:T(8,128)(2,1)} %collective-permute-done.26.refs_1_), channel_id=1, source_target_pairs={{0,1},{1,0},{2,3},{3,2},{4,5},{5,4},{6,7},{7,6},{8,9},{9,8},{10,11... | collective-permute-start | bytes 3145736 | tf_op jit(solution)/shard_map/ppermute | solution.py:193
  213.4 24.4 %collective-permute-start.31 = (bf16[4,512,256]{2,1,0:T(8,128)(2,1)}, bf16[4,512,256]{2,1,0:T(8,128)(2,1)}, u32[]{:S(2)}, u32[]{:S(2)}) collective-permute-start(bf16[4,512,256]{2,1,0:T(8,128)(2,1)} %collective-permute-done.27.refs_2_), channel_id=1, source_target_pairs={{0,1},{1,0},{2,3},{3,2},{4,5},{5,4},{6,7},{7,6},{8,9},{9,8},{10,11... | collective-permute-start | bytes 3145736 | tf_op jit(solution)/shard_map/ppermute | solution.py:193
  252.7 142.2 %all-gather.10.cloned.1.call-start = ((), (), s32[]{:S(2)}) async-start(), calls=%async_computation.10 | async-start | bytes 4718592 | tf_op jit(solution)/shard_map/all_gather | solution.py:788
  255.9 47.5 %collective-permute-start.34 = (bf16[512,2048]{1,0:T(8,128)(2,1)}, bf16[512,2048]{1,0:T(8,128)(2,1)}, u32[]{:S(2)}, u32[]{:S(2)}) collective-permute-start(bf16[512,2048]{1,0:T(8,128)(2,1)} %pad_maximum_fusion.6), channel_id=1, source_target_pairs={{0,16},{8,24},{16,0},{24,8},{1,17},{9,25},{17,1},{25,9},{2,18},{10... | collective-permute-start | bytes 6291464 | tf_op jit(solution)/shard_map/ppermute | solution.py:193
  256.3 47.1 %collective-permute-start.33 = (bf16[512,2048]{1,0:T(8,128)(2,1)}, bf16[512,2048]{1,0:T(8,128)(2,1)}, u32[]{:S(2)}, u32[]{:S(2)}) collective-permute-start(bf16[512,2048]{1,0:T(8,128)(2,1)} %pad_maximum_fusion.6), channel_id=1, source_target_pairs={{0,8},{8,0},{16,24},{24,16},{1,9},{9,1},{17,25},{25,17},{2,10},{10... | collective-permute-start | bytes 6291464 | tf_op jit(solution)/shard_map/ppermute | solution.py:193
  258.0 220.5 %reduce-scatter.8.cloned.1.call-start = ((), (), s32[]{:S(2)}) async-start(), calls=%async_computation.11 | async-start | bytes 4718592 | tf_op jit(solution)/shard_map/reduce_scatter | solution.py:798
  305.2 49.7 %collective-permute-start.35 = (bf16[512,2048]{1,0:T(8,128)(2,1)S(1)}, bf16[512,2048]{1,0:T(8,128)(2,1)S(1)}, u32[]{:S(2)}, u32[]{:S(2)}) collective-permute-start(bf16[512,2048]{1,0:T(8,128)(2,1)S(1)} %broadcast_select_fusion.1), channel_id=1, source_target_pairs={{0,16},{1,9},{2,18},{3,11},{4,20},{5,13},{6,22},{7,15},{8,24},{9,1... | collective-permute-start | bytes 6291464 | tf_op jit(solution)/shard_map/ppermute | solution.py:199
  305.6 25.5 %collective-permute-start.36 = (bf16[512,1024]{1,0:T(8,128)(2,1)S(1)}, bf16[512,1024]{1,0:T(8,128)(2,1)S(1)}, u32[]{:S(2)}, u32[]{:S(2)}) collective-permute-start(bf16[512,1024]{1,0:T(8,128)(2,1)S(1)} %copy-done.56), channel_id=1, source_target_pairs={{0,8},{8,0},{16,24},{24,16},{1,9},{9,1},{17,25},{25,17},{2,10},{10... | collective-permute-start | bytes 3145736 | tf_op jit(solution)/shard_map/ppermute | solution.py:193
  306.6 47.2 %collective-permute-start.37 = (bf16[512,1024]{1,0:T(8,128)(2,1)S(1)}, bf16[512,1024]{1,0:T(8,128)(2,1)S(1)}, u32[]{:S(2)}, u32[]{:S(2)}) collective-permute-start(bf16[512,1024]{1,0:T(8,128)(2,1)S(1)} %copy-done.56), channel_id=1, source_target_pairs={{0,16},{8,24},{16,0},{24,8},{1,17},{9,25},{17,1},{25,9},{2,18},{10... | collective-permute-start | bytes 3145736 | tf_op jit(solution)/shard_map/ppermute | solution.py:193
  418.4 113.6 %reduce-scatter.6.cloned.1.call-start = ((), (), s32[]{:S(2)}) async-start(), calls=%async_computation.9 | async-start | bytes 4718592 | tf_op jit(solution)/shard_map/reduce_scatter | solution.py:798
  419.0 177.0 %all-gather.12.cloned.1.call-start = ((), (), s32[]{:S(2)}) async-start(), calls=%async_computation.12 | async-start | bytes 4718592 | tf_op jit(solution)/shard_map/all_gather | solution.py:831
  449.3 25.5 %collective-permute-start.44 = (bf16[8,64,512]{2,1,0:T(8,128)(2,1)}, bf16[8,64,512]{2,1,0:T(8,128)(2,1)}, u32[]{:S(2)}, u32[]{:S(2)}) collective-permute-start(bf16[8,64,512]{2,1,0:T(8,128)(2,1)} %shard_map.400), channel_id=1, source_target_pairs={{0,16},{8,24},{16,0},{24,8},{1,17},{9,25},{17,1},{25,9},{2,18},{10... | collective-permute-start | bytes 1572872 | tf_op jit(solution)/shard_map/ppermute | solution.py:193
  449.3 25.5 %collective-permute-start.43 = (bf16[8,64,512]{2,1,0:T(8,128)(2,1)}, bf16[8,64,512]{2,1,0:T(8,128)(2,1)}, u32[]{:S(2)}, u32[]{:S(2)}) collective-permute-start(bf16[8,64,512]{2,1,0:T(8,128)(2,1)} %shard_map.400), channel_id=1, source_target_pairs={{0,8},{8,0},{16,24},{24,16},{1,9},{9,1},{17,25},{25,17},{2,10},{10... | collective-permute-start | bytes 1572872 | tf_op jit(solution)/shard_map/ppermute | solution.py:193
  546.8 96.9 %all-gather.14.cloned.1.call-start = ((), (), s32[]{:S(2)}) async-start(), calls=%async_computation.14 | async-start | bytes 4718592 | tf_op jit(solution)/shard_map/all_gather | solution.py:831
  550.9 168.1 %reduce-scatter.12.cloned.1.call-start = ((), (), s32[]{:S(2)}) async-start(), calls=%async_computation.15 | async-start | bytes 4718592 | tf_op jit(solution)/shard_map/reduce_scatter | solution.py:844
  670.1 99.6 %reduce-scatter.10.cloned.1.call-start = ((), (), s32[]{:S(2)}) async-start(), calls=%async_computation.13 | async-start | bytes 4718592 | tf_op jit(solution)/shard_map/reduce_scatter | solution.py:844
  670.8 242.4 %reduce-scatter.14.cloned.1.call-start = ((), (), s32[]{:S(2)}) async-start(), calls=%async_computation.16 | async-start | bytes 4718592 | tf_op jit(solution)/shard_map/reduce_scatter | solution.py:868
  821.7 42.0 %collective-permute-start.77 = (bf16[512,2048]{1,0:T(8,128)(2,1)}, bf16[512,2048]{1,0:T(8,128)(2,1)}, u32[]{:S(2)}, u32[]{:S(2)}) collective-permute-start(bf16[512,2048]{1,0:T(8,128)(2,1)} %get-tuple-element.185), channel_id=1, source_target_pairs={{0,16},{1,9},{2,18},{3,11},{4,20},{5,13},{6,22},{7,15},{8,24},{9,1... | collective-permute-start | bytes 6291464 | tf_op jit(solution)/shard_map/ppermute | solution.py:199
  824.7 34.6 %collective-permute-start.80 = (bf16[512,1024]{1,0:T(8,128)(2,1)}, bf16[512,1024]{1,0:T(8,128)(2,1)}, u32[]{:S(2)}, u32[]{:S(2)}) collective-permute-start(bf16[512,1024]{1,0:T(8,128)(2,1)} %get-tuple-element.191), channel_id=1, source_target_pairs={{0,16},{1,9},{2,18},{3,11},{4,20},{5,13},{6,22},{7,15},{8,24},{9,1... | collective-permute-start | bytes 3145736 | tf_op jit(solution)/shard_map/ppermute | solution.py:199
  825.3 38.4 %collective-permute-start.55 = (bf16[256,2048]{1,0:T(8,128)(2,1)S(1)}, bf16[256,2048]{1,0:T(8,128)(2,1)}, u32[]{:S(2)}, u32[]{:S(2)}) collective-permute-start(bf16[256,2048]{1,0:T(8,128)(2,1)S(1)} %copy-done.26), channel_id=1, source_target_pairs={{0,1},{1,0},{2,3},{3,2},{4,5},{5,4},{6,7},{7,6},{8,9},{9,8},{10,11... | collective-permute-start | bytes 3145736 | tf_op jit(solution)/shard_map/ppermute | solution.py:193
  862.3 90.4 %collective-permute-start.81 = (bf16[512,1024]{1,0:T(8,128)(2,1)}, bf16[512,1024]{1,0:T(8,128)(2,1)}, u32[]{:S(2)}, u32[]{:S(2)}) collective-permute-start(bf16[512,1024]{1,0:T(8,128)(2,1)} %add_convert_fusion.3), channel_id=1, source_target_pairs={{0,8},{1,17},{2,10},{3,19},{4,12},{5,21},{6,14},{7,23},{8,0},{9,25... | collective-permute-start | bytes 3145736 | tf_op jit(solution)/shard_map/ppermute | solution.py:199
  891.6 56.3 %collective-permute-start.70 = (bf16[512,1024]{1,0:T(8,128)(2,1)}, bf16[512,1024]{1,0:T(8,128)(2,1)}, u32[]{:S(2)}, u32[]{:S(2)}) collective-permute-start(bf16[512,1024]{1,0:T(8,128)(2,1)} %get-tuple-element.194), channel_id=1, source_target_pairs={{0,16},{1,9},{2,18},{3,11},{4,20},{5,13},{6,22},{7,15},{8,24},{9,1... | collective-permute-start | bytes 3145736 | tf_op jit(solution)/shard_map/ppermute | solution.py:199
  897.1 48.9 %collective-permute-start.60 = (bf16[512,1024]{1,0:T(8,128)(2,1)}, bf16[512,1024]{1,0:T(8,128)(2,1)}, u32[]{:S(2)}, u32[]{:S(2)}) collective-permute-start(bf16[512,1024]{1,0:T(8,128)(2,1)} %get-tuple-element.197), channel_id=1, source_target_pairs={{0,16},{1,9},{2,18},{3,11},{4,20},{5,13},{6,22},{7,15},{8,24},{9,1... | collective-permute-start | bytes 3145736 | tf_op jit(solution)/shard_map/ppermute | solution.py:199
  921.9 24.7 %collective-permute-start.72 = (bf16[512,1024]{1,0:T(8,128)(2,1)}, bf16[512,1024]{1,0:T(8,128)(2,1)}, u32[]{:S(2)}, u32[]{:S(2)}) collective-permute-start(bf16[512,1024]{1,0:T(8,128)(2,1)} %add_convert_fusion.5), channel_id=1, source_target_pairs={{0,8},{1,17},{2,10},{3,19},{4,12},{5,21},{6,14},{7,23},{8,0},{9,25... | collective-permute-start | bytes 3145736 | tf_op jit(solution)/shard_map/ppermute | solution.py:199
  942.5 141.6 %collective-permute-start.76 = (bf16[512,2048]{1,0:T(8,128)(2,1)}, bf16[512,2048]{1,0:T(8,128)(2,1)}, u32[]{:S(2)}, u32[]{:S(2)}) collective-permute-start(bf16[512,2048]{1,0:T(8,128)(2,1)} %get-tuple-element.184), channel_id=1, source_target_pairs={{0,16},{1,9},{2,18},{3,11},{4,20},{5,13},{6,22},{7,15},{8,24},{9,1... | collective-permute-start | bytes 6291464 | tf_op jit(solution)/shard_map/ppermute | solution.py:199
  945.9 56.6 %collective-permute-start.79 = (bf16[512,1024]{1,0:T(8,128)(2,1)S(1)}, bf16[512,1024]{1,0:T(8,128)(2,1)}, u32[]{:S(2)}, u32[]{:S(2)}) collective-permute-start(bf16[512,1024]{1,0:T(8,128)(2,1)S(1)} %copy-done.60), channel_id=1, source_target_pairs={{0,16},{1,9},{2,18},{3,11},{4,20},{5,13},{6,22},{7,15},{8,24},{9,1... | collective-permute-start | bytes 3145736 | tf_op jit(solution)/shard_map/ppermute | solution.py:199
  946.6 137.5 %collective-permute-start.78 = (bf16[512,2048]{1,0:T(8,128)(2,1)}, bf16[512,2048]{1,0:T(8,128)(2,1)}, u32[]{:S(2)}, u32[]{:S(2)}) collective-permute-start(bf16[512,2048]{1,0:T(8,128)(2,1)} %add_convert_fusion.2), channel_id=1, source_target_pairs={{0,8},{1,17},{2,10},{3,19},{4,12},{5,21},{6,14},{7,23},{8,0},{9,25... | collective-permute-start | bytes 6291464 | tf_op jit(solution)/shard_map/ppermute | solution.py:199
  947.9 85.1 %collective-permute-start.59 = (bf16[512,1024]{1,0:T(8,128)(2,1)}, bf16[512,1024]{1,0:T(8,128)(2,1)}, u32[]{:S(2)}, u32[]{:S(2)}) collective-permute-start(bf16[512,1024]{1,0:T(8,128)(2,1)} %get-tuple-element.196), channel_id=1, source_target_pairs={{0,16},{1,9},{2,18},{3,11},{4,20},{5,13},{6,22},{7,15},{8,24},{9,1... | collective-permute-start | bytes 3145736 | tf_op jit(solution)/shard_map/ppermute | solution.py:199
  952.7 115.1 %collective-permute-start.65 = (bf16[512,512]{0,1:T(8,128)(2,1)}, bf16[512,512]{0,1:T(8,128)(2,1)}, u32[]{:S(2)}, u32[]{:S(2)}) collective-permute-start(bf16[512,512]{0,1:T(8,128)(2,1)} %get-tuple-element.200), channel_id=1, source_target_pairs={{0,16},{1,9},{2,18},{3,11},{4,20},{5,13},{6,22},{7,15},{8,24},{9,1... | collective-permute-start | bytes 1572872 | tf_op jit(solution)/shard_map/ppermute | solution.py:199
  1002.6 65.3 %collective-permute-start.66 = (bf16[512,512]{0,1:T(8,128)(2,1)}, bf16[512,512]{0,1:T(8,128)(2,1)}, u32[]{:S(2)}, u32[]{:S(2)}) collective-permute-start(bf16[512,512]{0,1:T(8,128)(2,1)} %add_convert_fusion.11), channel_id=1, source_target_pairs={{0,8},{1,17},{2,10},{3,19},{4,12},{5,21},{6,14},{7,23},{8,0},{9,25... | collective-permute-start | bytes 1572872 | tf_op jit(solution)/shard_map/ppermute | solution.py:199
  1010.1 94.1 %all-to-all-start.1 = ((f32[8,4,68,128]{3,1,2,0:T(4,128)}), f32[8,4,68,128]{3,1,2,0:T(4,128)}, u32[]{:S(2)}, u32[]{:S(2)}) async-start(f32[8,4,68,128]{3,1,2,0:T(4,128)} %copy.98), calls=%async_computation.6 | async-start | bytes 2228224 | tf_op jit(solution)/shard_map/all_to_all | solution.py:944
  1033.0 28.8 %collective-permute-start.74 = (bf16[512,256]{1,0:T(8,128)(2,1)S(1)}, bf16[512,256]{1,0:T(8,128)(2,1)S(1)}, u32[]{:S(2)}, u32[]{:S(2)}) collective-permute-start(bf16[512,256]{1,0:T(8,128)(2,1)S(1)} %copy-done.66), channel_id=1, source_target_pairs={{0,4},{1,3},{2,6},{3,1},{4,0},{5,7},{6,2},{7,5},{8,12},{9,11},{10,... | collective-permute-start | bytes 786440 | tf_op jit(solution)/shard_map/ppermute | solution.py:199
  1061.8 26.4 %collective-permute-start.61 = (bf16[512,1024]{1,0:T(8,128)(2,1)S(1)}, bf16[512,1024]{1,0:T(8,128)(2,1)S(1)}, u32[]{:S(2)}, u32[]{:S(2)}) collective-permute-start(bf16[512,1024]{1,0:T(8,128)(2,1)S(1)} %copy-done.55), channel_id=1, source_target_pairs={{0,8},{1,17},{2,10},{3,19},{4,12},{5,21},{6,14},{7,23},{8,0},{9,25... | collective-permute-start | bytes 3145736 | tf_op jit(solution)/shard_map/ppermute | solution.py:199
  (190 other events, 2825.6 us)
Sparse Core Ops, SparseCore 0:
  78.7 62.7 all-gather.5
  252.8 60.3 all-gather.7
  314.8 45.6 all-gather.9
  418.5 59.9 reduce-scatter.7
  480.6 51.2 reduce-scatter.5
  546.9 48.3 all-gather.11
  596.9 46.7 all-gather.13
  670.2 48.6 reduce-scatter.11
  721.2 48.3 reduce-scatter.9
  798.7 66.5 reduce-scatter.13
where the time goes:
time: 1130 us; the launch traced here: 1120 us
  waiting for transfers between devices  523 us (46%)
  matrix products  164 us (15%)
  starting transfers between devices  136 us (12%)
  other arithmetic  118 us (10%)
  Pallas kernels  97.1 us (9%)
  local copies, waits for them, and re-layouts  65 us (6%)
  between operations  19.5 us (2%)
    ppermute x51, waiting for transfers between devices, hop(): return lax.ppermute(values, axis, [(i, i ^ mask) for i in range(size)])  227 us
    ppermute x34, waiting for transfers between devices, split_hop(): return lax.ppermute(values, (ROW, COL), pairs)  150 us
    reduce_scatter x4, waiting for transfers between devices, local(): lax.psum_scatter(done, COL, scatter_dimension=0, tiled=True)  120 us
    ppermute x51, starting transfers between devices, hop(): return lax.ppermute(values, axis, [(i, i ^ mask) for i in range(size)])  76.1 us
    dot_general x11, matrix products, product_tn(): lax.dot_general(left, right, (((0,), (0,)), ((), ())), preferred_element_...  62.2 us
    dot_general x8, matrix products, product(): return jnp.dot(left, right, preferred_element_type=jnp.float32)  51.4 us
    dot_general x8, matrix products, product_t(): lax.dot_general(left, right, (((1,), (1,)), ((), ())), preferred_element_...  50.7 us
    pallas_call x6, Pallas kernels, whole_call(): pl.pallas_call(body, out_shape=jax.ShapeDtypeStruct(shape, dtype), in_spe...  41.1 us
  transfers between devices with their start and end apart: 97, of which 46 were waited for; matrix products, arithmetic and copies ran while one was open for 22% of the time, Pallas kernels for 5%

commit v1 on v0

--- a/solution.py
+++ b/solution.py
@@ -345,7 +345,8 @@
         mine = direct_gather(stacked, ROW, row_total)
     else:
         mine = xor_gather(stacked, ROW, row_total, middle)
-    return (mine, [hop(one, COL, 1) for one in mine]), along[-1], mine[-1]
+    other = [hop(one, COL, 1) for one in mine]
+    return (mine, other), along[-1], mine[-1]
 
 
 def place_body(pairs, me_ref, own_ref, other_ref, out_ref):
@@ -750,10 +751,10 @@
         cosine,
         sine_part,
     )
-    out_pieces, _, out_last = gather_weight(
-        out_weight, pairs, row_total, False, kv_first, query_last, query_own
-    )
     attended, inverse = attend(span, jnp.transpose(window), query_scaled, pair_all)
+    out_pieces, _, _ = gather_weight(
+        out_weight, pairs, row_total, False, kv_first, query_last, attended
+    )
     attention_out = contract(me, attended, out_pieces)
     laurel_mid = product(normed_low, laurel_down_all).astype(low)
     laurel_out = product_t(laurel_mid, laurel_up_all)
@@ -769,17 +770,10 @@
     )
     feed_low = feed_in.astype(low)
     feed_pieces = xor_gather(
-        after(jnp.concatenate([gate_weight, up_weight], axis=1), out_last), ROW, row_total, feed_low
-    )
-    down_pieces = xor_gather(down_weight, ROW, row_total, feed_pieces[-1])
+        jnp.concatenate([gate_weight, up_weight], axis=1), ROW, row_total, feed_low
+    )
     layer_own = jnp.concatenate([per_layer_gate, per_layer_projection], axis=1)
-    layer_group = over_col(me, after(layer_own, feed_low), pairs)
-    layer_pieces = direct_gather(after(layer_group, down_pieces[-1]), ROW, row_total)
-    layer_all = jnp.concatenate([one.reshape(-1, 2 * embed) for one in layer_pieces], axis=0)
-    layer_gate_all = layer_all[:, :embed]
-    layer_proj_all = layer_all[:, embed:]
     feed_all = jnp.concatenate(feed_pieces, axis=0)
-    down_all = jnp.concatenate(down_pieces, axis=0)
     halves = 2
     part_rows = rows // halves
     feed_tokens, hidden_pulls, hidden_lows, down_outs = [], [], [], []
@@ -790,6 +784,9 @@
         )
         tokens = tokens if done is None else after(tokens, done)
         gate_up = product(tokens, feed_all).astype(low)
+        if h == 0:
+            down_pieces = xor_gather(down_weight, ROW, row_total, gate_up)
+            down_all = jnp.concatenate(down_pieces, axis=0)
         hidden, hidden_pull = jax.vjp(
             geglu, gate_up[:, :feed_width].astype(wide), gate_up[:, feed_width:].astype(wide)
         )
@@ -799,6 +796,11 @@
         feed_tokens.append(tokens)
         hidden_pulls.append(hidden_pull)
         hidden_lows.append(hidden_low)
+    layer_group = over_col(me, after(layer_own, done), pairs)
+    layer_pieces = direct_gather(layer_group, ROW, row_total)
+    layer_all = jnp.concatenate([one.reshape(-1, 2 * embed) for one in layer_pieces], axis=0)
+    layer_gate_all = layer_all[:, :embed]
+    layer_proj_all = layer_all[:, embed:]
     down_out = jnp.concatenate(down_outs, axis=0).astype(wide)
     after_feed, feed_pull = jax.vjp(feed_mix, mixed, down_out, gain_list[4])
     after_low = after_feed.astype(low)
@@ -825,7 +827,7 @@
     )
     attended_pair = pair_columns(me, after(attended, down_low), col_total)
     normed_pair = pair_rows(after(normed_low, down_low))
-    down_tokens, feed_grads, feed_in_grads = [], [], []
+    feed_in_grads = []
     done = None
     for h in range(halves):
         tokens = lax.all_gather(
@@ -836,21 +838,20 @@
                 (tokens, layer_grad, attended_pair, normed_pair)
             )
         else:
-            tokens = after(tokens, done)
+            tokens = after(tokens, done, down_first, feed_first)
         hidden_grad = product(tokens, down_all)
         gate_grad, up_grad = hidden_pulls[h](hidden_grad)
         feed_grad_low = jnp.concatenate([gate_grad.astype(low), up_grad.astype(low)], axis=1)
         done = product_t(feed_grad_low, feed_all).astype(low)
         feed_in_grads.append(lax.psum_scatter(done, COL, scatter_dimension=0, tiled=True))
-        down_tokens.append(tokens)
-        feed_grads.append(feed_grad_low)
+        if h == 0:
+            down_first = product_tn(after(tokens, done), hidden_lows[0]).astype(low)
+            feed_first = product_tn(after(feed_tokens[0], down_first), feed_grad_low).astype(low)
     feed_in_grad = jnp.concatenate(feed_in_grads, axis=0).astype(wide)
-    down_total = sum(
-        product_tn(after(down_tokens[h], done), hidden_lows[h]) for h in range(halves)
-    ).astype(low)
-    feed_total = sum(
-        product_tn(after(feed_tokens[h], down_total), feed_grads[h]) for h in range(halves)
-    ).astype(low)
+    down_total = product_tn(after(tokens, done), hidden_lows[1]) + down_first.astype(wide)
+    down_total = down_total.astype(low)
+    feed_total = product_tn(after(feed_tokens[1], down_total), feed_grad_low)
+    feed_total = (feed_total + feed_first.astype(wide)).astype(low)
     (
         inputs_grad,
         attention_grad,
@@ -913,9 +914,9 @@
     mark = marks[0]
     query_marks = []
     query_weight_grad = scatter_cols(query_total, row_total, pairs, mark, mark, query_marks)
-    out_weight_grad = scatter_cols(out_total, row_total, pairs, query_part, mark)
+    out_weight_grad = scatter_cols(out_total, row_total, pairs, query_part, normed_grad)
     down_weight_grad = scatter_rows(down_total, row_total, feed_total, query_marks[0])
-    feed_weight_grad = scatter_rows(feed_total, row_total, attended_grad, marks[-1])
+    feed_weight_grad = scatter_rows(feed_total, row_total, pair_parts, marks[-1])
     input_part, input_gain_grad = input_pull(after(normed_grad, mark))
     input_total = xor_blocks((inputs_grad + input_part).astype(low), me_row, row_total)
 
@@ -929,21 +930,19 @@
             final_gain_grad,
         ]
     ).reshape(6, row_total, col_total, small_rows)
-    wide_gains = jnp.transpose(wide_gains, (2, 1, 0, 3)).reshape(col_total, row_total, -1)
+    wide_gains = jnp.transpose(wide_gains, (1, 2, 0, 3)).reshape(row_total, col_total, -1)
     both_gains = jnp.concatenate([query_gain_grad, key_gain_grad], axis=0)
     both_gains = xor_blocks(both_gains, me_row, row_total)
     both_gains = both_gains.reshape(2, row_total, col_total, head_part)
-    both_gains = jnp.transpose(both_gains, (2, 1, 0, 3)).reshape(col_total, row_total, -1)
+    both_gains = jnp.transpose(both_gains, (1, 2, 0, 3)).reshape(row_total, col_total, -1)
     gain_sums = jnp.concatenate([wide_gains, both_gains], axis=2)
     gain_sums = jnp.pad(gain_sums, ((0, 0), (0, 0), (0, gain_lines * line - gain_total)))
-    gain_sums = gain_sums.reshape(col_total, row_total, gain_lines, line)
-    laurel_parts = jnp.transpose(
-        small_total.reshape(row_total, col_total, small_rows, line), (1, 0, 2, 3)
-    )
-    sums = jnp.concatenate([laurel_parts, gain_sums], axis=2)
-    sums = lax.all_to_all(after(sums, query_marks[0]), COL, 0, 0, tiled=True)
+    gain_sums = gain_sums.reshape(row_total, col_total, gain_lines, line)
+    laurel_parts = small_total.reshape(row_total, col_total, small_rows, line)
+    sums = after(jnp.concatenate([laurel_parts, gain_sums], axis=2), query_marks[0])
+    sums = sums[0] + sum(hop(sums[j], ROW, j) for j in range(1, row_total))
+    sums = lax.all_to_all(sums, COL, 0, 0, tiled=True)
     sums = jnp.sum(after(sums, query_marks[-1]), axis=0)
-    sums = sums[0] + sum(hop(sums[j], ROW, j) for j in range(1, row_total))
     laurel_grad = sums[:small_rows]
     gain_sums = sums[small_rows:].reshape(-1)
     gain_out = [gain_sums[i * small_rows : (i + 1) * small_rows] for i in range(6)]

time: 1130 us -> 1110 us (0.982)
  local copies, waits for them, and re-layouts: 65 us -> 52.4 us
    ppermute x51, waiting for transfers between devices: 227 us -> 174 us  [hop(): return lax.ppermute(values, axis, [(i, i ^ mask) for i in range(size)])]
    ppermute x34, waiting for transfers between devices: 150 us -> 200 us  [split_hop(): return lax.ppermute(values, (ROW, COL), pairs)]
    reduce_scatter x4, waiting for transfers between devices: 120 us -> 143 us  [local(): lax.psum_scatter(done, COL, scatter_dimension=0, tiled=True)]
    all_gather x2, waiting for transfers between devices: 21.6 us -> 2.22 us  [local(): lax.all_gather(down_low[h * part_rows:(h + 1) * part_rows], COL, axis=0,...]
    all_to_all x1, starting transfers between devices: 16.7 us -> 4.2 us  [local(): sums = lax.all_to_all(sums, COL, 0, 0, tiled=True)]
    unnamed x293 -> x282, local copies, waits for them, and re-layouts: 31.6 us -> 25.6 us
  transfers between devices with their start and end apart: 97 -> 97, of which waited for: 46 -> 44; matrix products, arithmetic and copies ran while one was open for 22% -> 21% of each run, Pallas kernels for 5% -> 6%
where the time goes in v1:
time: 1110 us; the launch traced here: 1100 us
  waiting for transfers between devices  524 us (47%)
  matrix products  167 us (15%)
  starting transfers between devices  131 us (12%)
  other arithmetic  114 us (10%)
  Pallas kernels  96.8 us (9%)
  local copies, waits for them, and re-layouts  52.4 us (5%)
  between operations  19.5 us (2%)
    ppermute x34, waiting for transfers between devices, split_hop(): return lax.ppermute(values, (ROW, COL), pairs)  200 us
    ppermute x51, waiting for transfers between devices, hop(): return lax.ppermute(values, axis, [(i, i ^ mask) for i in range(size)])  174 us
    reduce_scatter x4, waiting for transfers between devices, local(): lax.psum_scatter(done, COL, scatter_dimension=0, tiled=True)  143 us
    ppermute x51, starting transfers between devices, hop(): return lax.ppermute(values, axis, [(i, i ^ mask) for i in range(size)])  74.1 us
    dot_general x11, matrix products, product_tn(): lax.dot_general(left, right, (((0,), (0,)), ((), ())), preferred_element_...  64.3 us
    dot_general x8, matrix products, product(): return jnp.dot(left, right, preferred_element_type=jnp.float32)  53.6 us
    dot_general x8, matrix products, product_t(): lax.dot_general(left, right, (((1,), (1,)), ((), ())), preferred_element_...  48.9 us
    ppermute x34, starting transfers between devices, split_hop(): return lax.ppermute(values, (ROW, COL), pairs)  45.7 us
  transfers between devices with their start and end apart: 97, of which 44 were waited for; matrix products, arithmetic and copies ran while one was open for 21% of the time, Pallas kernels for 6%

profile of v1, /device:TPU:0, one launch (start us, length us, event | category | flops | bytes accessed | tf_op | source)
XLA Modules:
  0.0 1104.5 jit_solution(4928199245129737117)
XLA Ops:
  15.1 5.4 concatenate.94
  44.5 10.9 collective-permute-done.1
  70.0 5.6 shard_map.394.columns_ref
  83.3 14.3 %collective-permute-done.4.refs_1_ = bf16[512,256]{1,0:T(8,128)(2,1)S(1)} collective-permute-done((bf16[512,256]{1,0:T(8,128)(2,1)S(1)}, bf16[512,256]{1,0:T(8,128)(2,1)S(1)}, u32[]{:S(2)}, u32[]{:S(2)}) %collective-permute-start.4) | collective-permute-done | bytes 262176 | tf_op jit(solution)/shard_map/ppermute | solution.py:193
  97.6 8.8 collective-permute-done.5.refs_2_
  115.3 21.4 %collective-permute-done.10.refs_1_ = bf16[4,512,256]{2,1,0:T(8,128)(2,1)S(1)} collective-permute-done((bf16[4,512,256]{2,1,0:T(8,128)(2,1)}, bf16[4,512,256]{2,1,0:T(8,128)(2,1)S(1)}, u32[]{:S(2)}, u32[]{:S(2)}) %collective-permute-start.10) | collective-permute-done | bytes 1048608 | tf_op jit(solution)/shard_map/ppermute | solution.py:193
  138.4 15.5 %collective-permute-start.23 = (bf16[512,256]{1,0:T(8,128)(2,1)S(1)}, bf16[512,256]{1,0:T(8,128)(2,1)S(1)}, u32[]{:S(2)}, u32[]{:S(2)}) collective-permute-start(bf16[512,256]{1,0:T(8,128)(2,1)S(1)} %copy-done.70), channel_id=1, source_target_pairs={{0,2},{1,3},{2,0},{3,1},{4,6},{5,7},{6,4},{7,5},{8,10},{9,11},{10,... | collective-permute-start | bytes 786440 | tf_op jit(solution)/shard_map/ppermute | solution.py:193
  154.1 10.2 collective-permute-done.23.refs_1_
  169.6 8.8 collective-permute-done.25.refs_3_
  188.4 7.1 shard_map.392.query_ref
  198.5 9.8 shard_map.396
  213.6 11.2 %collective-permute-done.28.refs_3_ = bf16[4,512,256]{2,1,0:T(8,128)(2,1)} collective-permute-done((bf16[4,512,256]{2,1,0:T(8,128)(2,1)S(1)}, bf16[4,512,256]{2,1,0:T(8,128)(2,1)}, u32[]{:S(2)}, u32[]{:S(2)}) %collective-permute-start.28) | collective-permute-done | bytes 1048608 | tf_op jit(solution)/shard_map/ppermute | solution.py:199
  229.4 7.4 shard_map.398
  249.7 45.7 %collective-permute-done.34 = bf16[512,2048]{1,0:T(8,128)(2,1)} collective-permute-done((bf16[512,2048]{1,0:T(8,128)(2,1)}, bf16[512,2048]{1,0:T(8,128)(2,1)}, u32[]{:S(2)}, u32[]{:S(2)}) %collective-permute-start.34) | collective-permute-done | bytes 2097184 | tf_op jit(solution)/shard_map/ppermute | solution.py:193
  301.4 34.4 %collective-permute-done.35 = bf16[512,2048]{1,0:T(8,128)(2,1)} collective-permute-done((bf16[512,2048]{1,0:T(8,128)(2,1)S(1)}, bf16[512,2048]{1,0:T(8,128)(2,1)}, u32[]{:S(2)}, u32[]{:S(2)}) %collective-permute-start.35) | collective-permute-done | bytes 2097184 | tf_op jit(solution)/shard_map/ppermute | solution.py:199
  335.8 12.6 %convolution_convert_fusion.6 = bf16[1024,2048]{1,0:T(8,128)(2,1)S(1)} fusion(bf16[1024,2048]{1,0:T(8,128)(2,1)} %all-gather.8.cloned.1.call-done, bf16[512,2048]{1,0:T(8,128)(2,1)} %collective-permute-done.35, bf16[512,2048]{1,0:T(8,128)(2,1)} %collective-permute-done.34, bf16[512,2048]{1,0:T(8,128)(2,1)} %collective-permute-done.33, ...), kind=kOutput, calls=%fused_computation.54 | convolution fusion | flops 8625586176 | bytes 16777216 | tf_op jit(solution)/shard_map/dot_general | solution.py:176
  352.6 10.9 collective-permute-done.38
  365.6 6.9 convolution_convert_fusion.9
  372.4 12.6 %convolution_convert_fusion.5 = bf16[1024,2048]{1,0:T(8,128)(2,1)S(1)} fusion(bf16[1024,2048]{1,0:T(8,128)(2,1)} %all-gather.10.cloned.1.call-done, bf16[512,2048]{1,0:T(8,128)(2,1)} %collective-permute-done.35, bf16[512,2048]{1,0:T(8,128)(2,1)} %collective-permute-done.34, bf16[512,2048]{1,0:T(8,128)(2,1)} %collective-permute-done.33, ...), kind=kOutput, calls=%fused_computation.53 | convolution fusion | flops 8625586176 | bytes 16777216 | tf_op jit(solution)/shard_map/dot_general | solution.py:176
  387.1 6.8 convolution_convert_fusion.8
  394.8 10.5 collective-permute-start.39
  427.0 9.2 collective-permute-done.43
  436.1 11.1 %collective-permute-done.44 = bf16[8,64,512]{2,1,0:T(8,128)(2,1)} collective-permute-done((bf16[8,64,512]{2,1,0:T(8,128)(2,1)}, bf16[8,64,512]{2,1,0:T(8,128)(2,1)}, u32[]{:S(2)}, u32[]{:S(2)}) %collective-permute-start.44) | collective-permute-done | bytes 524320 | tf_op jit(solution)/shard_map/ppermute | solution.py:193
  454.4 52.3 %reduce-scatter.6.cloned.1.call-done = bf16[128,2048]{1,0:T(8,128)(2,1)} async-done(((bf16[1024,2048]{1,0:T(8,128)(2,1)}), bf16[128,2048]{1,0:T(8,128)(2,1)}) %reduce-scatter.6.cloned.1.call-update) | async-done | bytes 524304 | tf_op jit(solution)/shard_map/reduce_scatter | solution.py:795
  571.2 12.7 %fusion.9 = (bf16[1024,1024]{1,0:T(8,128)(2,1)}, bf16[1024,1024]{1,0:T(8,128)(2,1)}) fusion(bf16[1024,2048]{1,0:T(8,128)(2,1)} %copy-done.133, bf16[1024,2048]{1,0:T(8,128)(2,1)} %all-gather.12.cloned.1.call-done, bf16[2048,1024]{1,0:T(8,128)(2,1)} %copy-done.65), kind=kOutput, calls=%fused_computation.27 | convolution fusion | flops 4322230272 | bytes 16777216 | tf_op jit(solution)/shard_map/dot_general | solution.py:176
  583.9 14.8 %convolution_convert_fusion.4 = bf16[1024,2048]{1,0:T(8,128)(2,1)} fusion(bf16[1024,1024]{1,0:T(8,128)(2,1)} %get-tuple-element.185, bf16[1024,1024]{1,0:T(8,128)(2,1)} %get-tuple-element.184, bf16[512,2048]{1,0:T(8,128)(2,1)} %collective-permute-done.35, bf16[512,2048]{1,0:T(8,128)(2,1)} %collective-permute-done.34, ...), kind=kOutput, calls=%fused_computation.52 | convolution fusion | flops 8633974784 | bytes 16777216 | tf_op jit(solution)/shard_map/dot_general | solution.py:180
  598.7 10.4 convolution_convert_fusion.7
  609.2 11.6 %convolution_convert_fusion = bf16[2048,2048]{1,0:T(8,128)(2,1)} fusion(bf16[1024,2048]{1,0:T(8,128)(2,1)S(1)} %copy-done.131, bf16[1024,1024]{1,0:T(8,128)(2,1)S(1)} %copy-done.137, bf16[1024,1024]{1,0:T(8,128)(2,1)S(1)} %copy-done.136), kind=kOutput, calls=%fused_computation.13 | convolution fusion | flops 8602517504 | bytes 16777216 | tf_op jit(solution)/shard_map/dot_general | solution.py:186
  620.8 12.9 %fusion.6 = (bf16[1024,1024]{1,0:T(8,128)(2,1)}, bf16[1024,1024]{1,0:T(8,128)(2,1)}) fusion(bf16[1024,2048]{1,0:T(8,128)(2,1)} %copy-done.134, bf16[1024,2048]{1,0:T(8,128)(2,1)} %all-gather.14.cloned.1.call-done, bf16[2048,1024]{1,0:T(8,128)(2,1)} %copy-done.65), kind=kOutput, calls=%fused_computation.24 | convolution fusion | flops 4322230272 | bytes 16777216 | tf_op jit(solution)/shard_map/dot_general | solution.py:176
  633.7 14.6 %convolution_convert_fusion.3 = bf16[1024,2048]{1,0:T(8,128)(2,1)} fusion(bf16[1024,1024]{1,0:T(8,128)(2,1)} %get-tuple-element.183, bf16[1024,1024]{1,0:T(8,128)(2,1)} %get-tuple-element.182, bf16[512,2048]{1,0:T(8,128)(2,1)} %collective-permute-done.35, bf16[512,2048]{1,0:T(8,128)(2,1)} %collective-permute-done.34, ...), kind=kOutput, calls=%fused_computation.51 | convolution fusion | flops 8633974784 | bytes 16777216 | tf_op jit(solution)/shard_map/dot_general | solution.py:180
  649.2 12.1 %add_convert_fusion.1 = bf16[2048,1024]{1,0:T(8,128)(2,1)} fusion(bf16[2048,1024]{1,0:T(8,128)(2,1)} %convolution_convert_fusion.7, bf16[1024,2048]{1,0:T(8,128)(2,1)} %all-gather.14.cloned.1.call-done, bf16[1024,2048]{1,0:T(8,128)(2,1)} %copy-done.134), kind=kOutput, calls=%fused_computation.2 | convolution fusion | flops 4313841664 | bytes 16777216 | tf_op jit(solution)/shard_map/dot_general | solution.py:186
  661.3 35.9 %reduce-scatter.12.cloned.1.call-done = bf16[128,2048]{1,0:T(8,128)(2,1)} async-done(((bf16[1024,2048]{1,0:T(8,128)(2,1)}), bf16[128,2048]{1,0:T(8,128)(2,1)}) %reduce-scatter.12.cloned.1.call-update) | async-done | bytes 524304 | tf_op jit(solution)/shard_map/reduce_scatter | solution.py:846
  697.2 50.7 %reduce-scatter.10.cloned.1.call-done = bf16[128,2048]{1,0:T(8,128)(2,1)} async-done(((bf16[1024,2048]{1,0:T(8,128)(2,1)}), bf16[128,2048]{1,0:T(8,128)(2,1)}) %reduce-scatter.10.cloned.1.call-update) | async-done | bytes 524304 | tf_op jit(solution)/shard_map/reduce_scatter | solution.py:846
  757.0 7.1 shard_map.403.grad_ref
  764.1 13.1 %shard_map.404 = (f32[256,2048]{1,0:T(8,128)}, bf16[8,2,256,512]{3,2,1,0:T(8,128)(2,1)}) custom-call(s32[2]{0:T(128)} %pad_add_fusion.1.span_ref, s32[2,256]{1,0:T(2,128)} %get-tuple-element.262.window_ref, bf16[256,2048]{1,0:T(8,128)(2,1)} %shard_map.393.query_ref, bf16[8,2,256,512]{3,2,1,0:T(8,128)(2,1)} %bitcast.111, bf16[8,2,256,512]{3,2,1,0:T(8,128)(2,1)} %bitcast.112, ...), custom_call_target="tpu_custom_call" | custom-call | flops 10737418240 | bytes 8388608 | tf_op jit(solution)/shard_map/pallas_call | solution.py:601
  778.8 13.1 %add_convert_fusion = bf16[2048,2048]{1,0:T(8,128)(2,1)S(1)} fusion(bf16[2048,2048]{1,0:T(8,128)(2,1)} %convolution_convert_fusion, bf16[1024,2048]{1,0:T(8,128)(2,1)} %all-gather.10.cloned.1.call-done, bf16[1024,1024]{1,0:T(8,128)(2,1)} %get-tuple-element.183, bf16[1024,1024]{1,0:T(8,128)(2,1)S(1)} %copy-done.135), kind=kOutput, calls=%fused_computation | convolution fusion | flops 8610906112 | bytes 25165824 | tf_op jit(solution)/shard_map/dot_general | solution.py:186
  807.7 27.4 %collective-permute-done.80 = bf16[512,1024]{1,0:T(8,128)(2,1)} collective-permute-done((bf16[512,1024]{1,0:T(8,128)(2,1)}, bf16[512,1024]{1,0:T(8,128)(2,1)}, u32[]{:S(2)}, u32[]{:S(2)}) %collective-permute-start.80) | collective-permute-done | bytes 1048608 | tf_op jit(solution)/shard_map/ppermute | solution.py:199
  854.4 5.6 add_convert_fusion.2
  871.6 7.7 shard_map.407
  883.8 7.1 collective-permute-done.71
  909.6 6.0 shard_map.410
  923.0 15.1 %collective-permute-start.74 = (bf16[512,256]{1,0:T(8,128)(2,1)S(1)}, bf16[512,256]{1,0:T(8,128)(2,1)S(1)}, u32[]{:S(2)}, u32[]{:S(2)}) collective-permute-start(bf16[512,256]{1,0:T(8,128)(2,1)S(1)} %get-tuple-element.204), channel_id=1, source_target_pairs={{0,4},{1,3},{2,6},{3,1},{4,0},{5,7},{6,2},{7,5},{8,12},{9,11},{10,... | collective-permute-start | bytes 786440 | tf_op jit(solution)/shard_map/ppermute | solution.py:199
  945.5 8.2 collective-permute-done.73
  969.4 55.6 %collective-permute-done.59 = bf16[512,1024]{1,0:T(8,128)(2,1)} collective-permute-done((bf16[512,1024]{1,0:T(8,128)(2,1)}, bf16[512,1024]{1,0:T(8,128)(2,1)}, u32[]{:S(2)}, u32[]{:S(2)}) %collective-permute-start.59) | collective-permute-done | bytes 1048608 | tf_op jit(solution)/shard_map/ppermute | solution.py:199
  1033.3 9.6 collective-permute-done.65
  1047.8 8.2 collective-permute-done.83
  1078.1 6.7 collective-permute-done.63
  1087.0 8.8 collective-permute-done.62
  (637 shorter events, 360.7 us)
Async XLA Ops:
  9.3 28.0 %collective-permute-start.3 = (bf16[512,128]{1,0:T(8,128)(2,1)S(1)}, bf16[512,128]{1,0:T(8,128)(2,1)S(1)}, u32[]{:S(2)}, u32[]{:S(2)}) collective-permute-start(bf16[512,128]{1,0:T(8,128)(2,1)S(1)} %pad_maximum_fusion.23.refs_0_), channel_id=1, source_target_pairs={{0,6},{1,7},{2,4},{3,5},{4,2},{5,3},{6,0},{7,1},{8,14},{9,15},{10,... | collective-permute-start | bytes 393224 | tf_op jit(solution)/shard_map/ppermute | solution.py:193
  14.5 23.3 %collective-permute-start.7 = (bf16[512,128]{1,0:T(8,128)(2,1)S(1)}, bf16[512,128]{1,0:T(8,128)(2,1)S(1)}, u32[]{:S(2)}, u32[]{:S(2)}) collective-permute-start(bf16[512,128]{1,0:T(8,128)(2,1)S(1)} %pad_maximum_fusion.23.refs_0_), channel_id=1, source_target_pairs={{0,2},{1,3},{2,0},{3,1},{4,6},{5,7},{6,4},{7,5},{8,10},{9,11},{10,... | collective-permute-start | bytes 393224 | tf_op jit(solution)/shard_map/ppermute | solution.py:193
  14.5 23.3 %collective-permute-start.8 = (bf16[512,128]{1,0:T(8,128)(2,1)S(1)}, bf16[512,128]{1,0:T(8,128)(2,1)S(1)}, u32[]{:S(2)}, u32[]{:S(2)}) collective-permute-start(bf16[512,128]{1,0:T(8,128)(2,1)S(1)} %pad_maximum_fusion.23.refs_0_), channel_id=1, source_target_pairs={{0,4},{1,5},{2,6},{3,7},{4,0},{5,1},{6,2},{7,3},{8,12},{9,13},{10,... | collective-permute-start | bytes 393224 | tf_op jit(solution)/shard_map/ppermute | solution.py:193
  27.1 171.4 %all-gather.6.cloned.1.call-start = ((), (), s32[]{:S(2)}) async-start(), calls=%async_computation.7 | async-start | bytes 4718592 | tf_op jit(solution)/shard_map/all_gather | solution.py:743
  43.5 22.3 %collective-permute-start.17 = (bf16[4,512,128]{2,1,0:T(8,128)(2,1)}, bf16[4,512,128]{2,1,0:T(8,128)(2,1)S(1)}, u32[]{:S(2)}, u32[]{:S(2)}) collective-permute-start(bf16[4,512,128]{2,1,0:T(8,128)(2,1)} %shard_map.391.refs_0_), channel_id=1, source_target_pairs={{0,8},{8,0},{16,24},{24,16},{1,9},{9,1},{17,25},{25,17},{2,10},{10... | collective-permute-start | bytes 1572872 | tf_op jit(solution)/shard_map/ppermute | solution.py:193
  44.0 23.1 %collective-permute-start.18 = (bf16[4,512,128]{2,1,0:T(8,128)(2,1)}, bf16[4,512,128]{2,1,0:T(8,128)(2,1)S(1)}, u32[]{:S(2)}, u32[]{:S(2)}) collective-permute-start(bf16[4,512,128]{2,1,0:T(8,128)(2,1)} %shard_map.391.refs_0_), channel_id=1, source_target_pairs={{0,16},{8,24},{16,0},{24,8},{1,17},{9,25},{17,1},{25,9},{2,18},{10... | collective-permute-start | bytes 1572872 | tf_op jit(solution)/shard_map/ppermute | solution.py:193
  78.2 257.6 %all-gather.8.cloned.1.call-start = ((), (), s32[]{:S(2)}) async-start(), calls=%async_computation.8 | async-start | bytes 4718592 | tf_op jit(solution)/shard_map/all_gather | solution.py:782
  80.0 26.4 %collective-permute-start.5 = (bf16[512,256]{1,0:T(8,128)(2,1)S(1)}, bf16[512,256]{1,0:T(8,128)(2,1)S(1)}, u32[]{:S(2)}, u32[]{:S(2)}) collective-permute-start(bf16[512,256]{1,0:T(8,128)(2,1)S(1)} %copy-done.69), channel_id=1, source_target_pairs={{0,4},{1,5},{2,6},{3,7},{4,0},{5,1},{6,2},{7,3},{8,12},{9,13},{10,... | collective-permute-start | bytes 786440 | tf_op jit(solution)/shard_map/ppermute | solution.py:193
  81.7 27.8 %collective-permute-start.6 = (bf16[512,256]{1,0:T(8,128)(2,1)S(1)}, bf16[512,256]{1,0:T(8,128)(2,1)S(1)}, u32[]{:S(2)}, u32[]{:S(2)}) collective-permute-start(bf16[512,256]{1,0:T(8,128)(2,1)S(1)} %copy-done.69), channel_id=1, source_target_pairs={{0,6},{1,7},{2,4},{3,5},{4,2},{5,3},{6,0},{7,1},{8,14},{9,15},{10,... | collective-permute-start | bytes 786440 | tf_op jit(solution)/shard_map/ppermute | solution.py:193
  112.6 24.1 %collective-permute-start.10 = (bf16[4,512,256]{2,1,0:T(8,128)(2,1)}, bf16[4,512,256]{2,1,0:T(8,128)(2,1)S(1)}, u32[]{:S(2)}, u32[]{:S(2)}) collective-permute-start(bf16[4,512,256]{2,1,0:T(8,128)(2,1)} %shard_map.390.refs_0_), channel_id=1, source_target_pairs={{0,8},{8,0},{16,24},{24,16},{1,9},{9,1},{17,25},{25,17},{2,10},{10... | collective-permute-start | bytes 3145736 | tf_op jit(solution)/shard_map/ppermute | solution.py:193
  113.3 24.0 %collective-permute-start.11 = (bf16[4,512,256]{2,1,0:T(8,128)(2,1)}, bf16[4,512,256]{2,1,0:T(8,128)(2,1)S(1)}, u32[]{:S(2)}, u32[]{:S(2)}) collective-permute-start(bf16[4,512,256]{2,1,0:T(8,128)(2,1)} %shard_map.390.refs_0_), channel_id=1, source_target_pairs={{0,16},{8,24},{16,0},{24,8},{1,17},{9,25},{17,1},{25,9},{2,18},{10... | collective-permute-start | bytes 3145736 | tf_op jit(solution)/shard_map/ppermute | solution.py:193
  137.5 26.9 %collective-permute-start.12 = (bf16[4,512,256]{2,1,0:T(8,128)(2,1)S(1)}, bf16[4,512,256]{2,1,0:T(8,128)(2,1)}, u32[]{:S(2)}, u32[]{:S(2)}) collective-permute-start(bf16[4,512,256]{2,1,0:T(8,128)(2,1)S(1)} %broadcast_select_fusion.7), channel_id=1, source_target_pairs={{0,16},{1,9},{2,18},{3,11},{4,20},{5,13},{6,22},{7,15},{8,24},{9,1... | collective-permute-start | bytes 3145736 | tf_op jit(solution)/shard_map/ppermute | solution.py:199
  138.4 43.3 %collective-permute-start.13 = (bf16[4,512,256]{2,1,0:T(8,128)(2,1)S(1)}, bf16[4,512,256]{2,1,0:T(8,128)(2,1)}, u32[]{:S(2)}, u32[]{:S(2)}) collective-permute-start(bf16[4,512,256]{2,1,0:T(8,128)(2,1)S(1)} %copy-done.12), channel_id=1, source_target_pairs={{0,1},{1,0},{2,3},{3,2},{4,5},{5,4},{6,7},{7,6},{8,9},{9,8},{10,11... | collective-permute-start | bytes 3145736 | tf_op jit(solution)/shard_map/ppermute | solution.py:193
  138.4 25.9 %collective-permute-start.23 = (bf16[512,256]{1,0:T(8,128)(2,1)S(1)}, bf16[512,256]{1,0:T(8,128)(2,1)S(1)}, u32[]{:S(2)}, u32[]{:S(2)}) collective-permute-start(bf16[512,256]{1,0:T(8,128)(2,1)S(1)} %copy-done.70), channel_id=1, source_target_pairs={{0,2},{1,3},{2,0},{3,1},{4,6},{5,7},{6,4},{7,5},{8,10},{9,11},{10,... | collective-permute-start | bytes 786440 | tf_op jit(solution)/shard_map/ppermute | solution.py:193
  153.9 34.5 %collective-permute-start.14 = (bf16[4,512,256]{2,1,0:T(8,128)(2,1)S(1)}, bf16[4,512,256]{2,1,0:T(8,128)(2,1)}, u32[]{:S(2)}, u32[]{:S(2)}) collective-permute-start(bf16[4,512,256]{2,1,0:T(8,128)(2,1)S(1)} %collective-permute-done.10.refs_1_), channel_id=1, source_target_pairs={{0,1},{1,0},{2,3},{3,2},{4,5},{5,4},{6,7},{7,6},{8,9},{9,8},{10,11... | collective-permute-start | bytes 3145736 | tf_op jit(solution)/shard_map/ppermute | solution.py:193
  164.3 24.1 %collective-permute-start.15 = (bf16[4,512,256]{2,1,0:T(8,128)(2,1)S(1)}, bf16[4,512,256]{2,1,0:T(8,128)(2,1)}, u32[]{:S(2)}, u32[]{:S(2)}) collective-permute-start(bf16[4,512,256]{2,1,0:T(8,128)(2,1)S(1)} %collective-permute-done.11.refs_2_), channel_id=1, source_target_pairs={{0,1},{1,0},{2,3},{3,2},{4,5},{5,4},{6,7},{7,6},{8,9},{9,8},{10,11... | collective-permute-start | bytes 3145736 | tf_op jit(solution)/shard_map/ppermute | solution.py:193
  164.3 24.1 %collective-permute-start.16 = (bf16[4,512,256]{2,1,0:T(8,128)(2,1)}, bf16[4,512,256]{2,1,0:T(8,128)(2,1)}, u32[]{:S(2)}, u32[]{:S(2)}) collective-permute-start(bf16[4,512,256]{2,1,0:T(8,128)(2,1)} %collective-permute-done.12.refs_3_), channel_id=1, source_target_pairs={{0,1},{1,0},{2,3},{3,2},{4,5},{5,4},{6,7},{7,6},{8,9},{9,8},{10,11... | collective-permute-start | bytes 3145736 | tf_op jit(solution)/shard_map/ppermute | solution.py:193
  180.6 27.7 %collective-permute-start.26 = (bf16[4,512,256]{2,1,0:T(8,128)(2,1)}, bf16[4,512,256]{2,1,0:T(8,128)(2,1)}, u32[]{:S(2)}, u32[]{:S(2)}) collective-permute-start(bf16[4,512,256]{2,1,0:T(8,128)(2,1)} %shard_map.397.refs_0_), channel_id=1, source_target_pairs={{0,8},{8,0},{16,24},{24,16},{1,9},{9,1},{17,25},{25,17},{2,10},{10... | collective-permute-start | bytes 3145736 | tf_op jit(solution)/shard_map/ppermute | solution.py:193
  181.7 26.7 %collective-permute-start.27 = (bf16[4,512,256]{2,1,0:T(8,128)(2,1)}, bf16[4,512,256]{2,1,0:T(8,128)(2,1)}, u32[]{:S(2)}, u32[]{:S(2)}) collective-permute-start(bf16[4,512,256]{2,1,0:T(8,128)(2,1)} %shard_map.397.refs_0_), channel_id=1, source_target_pairs={{0,16},{8,24},{16,0},{24,8},{1,17},{9,25},{17,1},{25,9},{2,18},{10... | collective-permute-start | bytes 3145736 | tf_op jit(solution)/shard_map/ppermute | solution.py:193
  244.2 128.2 %all-gather.10.cloned.1.call-start = ((), (), s32[]{:S(2)}) async-start(), calls=%async_computation.10 | async-start | bytes 4718592 | tf_op jit(solution)/shard_map/all_gather | solution.py:782
  247.5 47.9 %collective-permute-start.34 = (bf16[512,2048]{1,0:T(8,128)(2,1)}, bf16[512,2048]{1,0:T(8,128)(2,1)}, u32[]{:S(2)}, u32[]{:S(2)}) collective-permute-start(bf16[512,2048]{1,0:T(8,128)(2,1)} %constant_dynamic-update-slice_fusion), channel_id=1, source_target_pairs={{0,16},{8,24},{16,0},{24,8},{1,17},{9,25},{17,1},{25,9},{2,18},{10... | collective-permute-start | bytes 6291464 | tf_op jit(solution)/shard_map/ppermute | solution.py:193
  248.5 48.1 %collective-permute-start.33 = (bf16[512,2048]{1,0:T(8,128)(2,1)}, bf16[512,2048]{1,0:T(8,128)(2,1)}, u32[]{:S(2)}, u32[]{:S(2)}) collective-permute-start(bf16[512,2048]{1,0:T(8,128)(2,1)} %constant_dynamic-update-slice_fusion), channel_id=1, source_target_pairs={{0,8},{8,0},{16,24},{24,16},{1,9},{9,1},{17,25},{25,17},{2,10},{10... | collective-permute-start | bytes 6291464 | tf_op jit(solution)/shard_map/ppermute | solution.py:193
  249.4 204.9 %reduce-scatter.8.cloned.1.call-start = ((), (), s32[]{:S(2)}) async-start(), calls=%async_computation.11 | async-start | bytes 4718592 | tf_op jit(solution)/shard_map/reduce_scatter | solution.py:795
  298.4 37.4 %collective-permute-start.35 = (bf16[512,2048]{1,0:T(8,128)(2,1)S(1)}, bf16[512,2048]{1,0:T(8,128)(2,1)}, u32[]{:S(2)}, u32[]{:S(2)}) collective-permute-start(bf16[512,2048]{1,0:T(8,128)(2,1)S(1)} %broadcast_select_fusion.1), channel_id=1, source_target_pairs={{0,16},{1,9},{2,18},{3,11},{4,20},{5,13},{6,22},{7,15},{8,24},{9,1... | collective-permute-start | bytes 6291464 | tf_op jit(solution)/shard_map/ppermute | solution.py:199
  299.0 49.4 %collective-permute-start.36 = (bf16[512,1024]{1,0:T(8,128)(2,1)}, bf16[512,1024]{1,0:T(8,128)(2,1)S(1)}, u32[]{:S(2)}, u32[]{:S(2)}) collective-permute-start(bf16[512,1024]{1,0:T(8,128)(2,1)} %param.33), channel_id=1, source_target_pairs={{0,8},{8,0},{16,24},{24,16},{1,9},{9,1},{17,25},{25,17},{2,10},{10... | collective-permute-start | bytes 3145736 | tf_op jit(solution)/shard_map/ppermute | solution.py:193
  300.7 47.7 %collective-permute-start.37 = (bf16[512,1024]{1,0:T(8,128)(2,1)}, bf16[512,1024]{1,0:T(8,128)(2,1)}, u32[]{:S(2)}, u32[]{:S(2)}) collective-permute-start(bf16[512,1024]{1,0:T(8,128)(2,1)} %param.33), channel_id=1, source_target_pairs={{0,16},{8,24},{16,0},{24,8},{1,17},{9,25},{17,1},{25,9},{2,18},{10... | collective-permute-start | bytes 3145736 | tf_op jit(solution)/shard_map/ppermute | solution.py:193
  393.9 112.7 %reduce-scatter.6.cloned.1.call-start = ((), (), s32[]{:S(2)}) async-start(), calls=%async_computation.9 | async-start | bytes 4718592 | tf_op jit(solution)/shard_map/reduce_scatter | solution.py:795
  394.5 176.7 %all-gather.12.cloned.1.call-start = ((), (), s32[]{:S(2)}) async-start(), calls=%async_computation.12 | async-start | bytes 4718592 | tf_op jit(solution)/shard_map/all_gather | solution.py:833
  422.0 25.2 %collective-permute-start.44 = (bf16[8,64,512]{2,1,0:T(8,128)(2,1)}, bf16[8,64,512]{2,1,0:T(8,128)(2,1)}, u32[]{:S(2)}, u32[]{:S(2)}) collective-permute-start(bf16[8,64,512]{2,1,0:T(8,128)(2,1)} %shard_map.400), channel_id=1, source_target_pairs={{0,16},{8,24},{16,0},{24,8},{1,17},{9,25},{17,1},{25,9},{2,18},{10... | collective-permute-start | bytes 1572872 | tf_op jit(solution)/shard_map/ppermute | solution.py:193
  423.4 23.8 %collective-permute-start.45 = (bf16[8,64,512]{2,1,0:T(8,128)(2,1)}, bf16[8,64,512]{2,1,0:T(8,128)(2,1)}, u32[]{:S(2)}, u32[]{:S(2)}) collective-permute-start(bf16[8,64,512]{2,1,0:T(8,128)(2,1)} %shard_map.400), channel_id=1, source_target_pairs={{0,24},{8,16},{16,8},{24,0},{1,25},{9,17},{17,9},{25,1},{2,26},{10... | collective-permute-start | bytes 1572872 | tf_op jit(solution)/shard_map/ppermute | solution.py:193
  521.5 99.3 %all-gather.14.cloned.1.call-start = ((), (), s32[]{:S(2)}) async-start(), calls=%async_computation.14 | async-start | bytes 4718592 | tf_op jit(solution)/shard_map/all_gather | solution.py:833
  549.8 147.4 %reduce-scatter.12.cloned.1.call-start = ((), (), s32[]{:S(2)}) async-start(), calls=%async_computation.15 | async-start | bytes 4718592 | tf_op jit(solution)/shard_map/reduce_scatter | solution.py:846
  648.3 99.6 %reduce-scatter.10.cloned.1.call-start = ((), (), s32[]{:S(2)}) async-start(), calls=%async_computation.13 | async-start | bytes 4718592 | tf_op jit(solution)/shard_map/reduce_scatter | solution.py:846
  649.1 246.5 %reduce-scatter.14.cloned.1.call-start = ((), (), s32[]{:S(2)}) async-start(), calls=%async_computation.16 | async-start | bytes 4718592 | tf_op jit(solution)/shard_map/reduce_scatter | solution.py:869
  797.5 40.5 %collective-permute-start.77 = (bf16[512,2048]{1,0:T(8,128)(2,1)}, bf16[512,2048]{1,0:T(8,128)(2,1)}, u32[]{:S(2)}, u32[]{:S(2)}) collective-permute-start(bf16[512,2048]{1,0:T(8,128)(2,1)} %get-tuple-element.181), channel_id=1, source_target_pairs={{0,16},{1,9},{2,18},{3,11},{4,20},{5,13},{6,22},{7,15},{8,24},{9,1... | collective-permute-start | bytes 6291464 | tf_op jit(solution)/shard_map/ppermute | solution.py:199
  800.6 34.5 %collective-permute-start.80 = (bf16[512,1024]{1,0:T(8,128)(2,1)}, bf16[512,1024]{1,0:T(8,128)(2,1)}, u32[]{:S(2)}, u32[]{:S(2)}) collective-permute-start(bf16[512,1024]{1,0:T(8,128)(2,1)} %get-tuple-element.187), channel_id=1, source_target_pairs={{0,16},{1,9},{2,18},{3,11},{4,20},{5,13},{6,22},{7,15},{8,24},{9,1... | collective-permute-start | bytes 3145736 | tf_op jit(solution)/shard_map/ppermute | solution.py:199
  801.2 36.8 %collective-permute-start.55 = (bf16[256,2048]{1,0:T(8,128)(2,1)S(1)}, bf16[256,2048]{1,0:T(8,128)(2,1)}, u32[]{:S(2)}, u32[]{:S(2)}) collective-permute-start(bf16[256,2048]{1,0:T(8,128)(2,1)S(1)} %copy-done.27), channel_id=1, source_target_pairs={{0,1},{1,0},{2,3},{3,2},{4,5},{5,4},{6,7},{7,6},{8,9},{9,8},{10,11... | collective-permute-start | bytes 3145736 | tf_op jit(solution)/shard_map/ppermute | solution.py:193
  807.1 217.9 %collective-permute-start.79 = (bf16[512,1024]{1,0:T(8,128)(2,1)}, bf16[512,1024]{1,0:T(8,128)(2,1)}, u32[]{:S(2)}, u32[]{:S(2)}) collective-permute-start(bf16[512,1024]{1,0:T(8,128)(2,1)} %get-tuple-element.186), channel_id=1, source_target_pairs={{0,16},{1,9},{2,18},{3,11},{4,20},{5,13},{6,22},{7,15},{8,24},{9,1... | collective-permute-start | bytes 3145736 | tf_op jit(solution)/shard_map/ppermute | solution.py:199
  864.5 55.0 %collective-permute-start.70 = (bf16[512,1024]{1,0:T(8,128)(2,1)}, bf16[512,1024]{1,0:T(8,128)(2,1)}, u32[]{:S(2)}, u32[]{:S(2)}) collective-permute-start(bf16[512,1024]{1,0:T(8,128)(2,1)} %get-tuple-element.190), channel_id=1, source_target_pairs={{0,16},{1,9},{2,18},{3,11},{4,20},{5,13},{6,22},{7,15},{8,24},{9,1... | collective-permute-start | bytes 3145736 | tf_op jit(solution)/shard_map/ppermute | solution.py:199
  864.5 26.3 %collective-permute-start.71 = (bf16[512,1024]{1,0:T(8,128)(2,1)}, bf16[512,1024]{1,0:T(8,128)(2,1)}, u32[]{:S(2)}, u32[]{:S(2)}) collective-permute-start(bf16[512,1024]{1,0:T(8,128)(2,1)} %get-tuple-element.191), channel_id=1, source_target_pairs={{0,16},{1,9},{2,18},{3,11},{4,20},{5,13},{6,22},{7,15},{8,24},{9,1... | collective-permute-start | bytes 3145736 | tf_op jit(solution)/shard_map/ppermute | solution.py:199
  893.7 25.8 %collective-permute-start.72 = (bf16[512,1024]{1,0:T(8,128)(2,1)}, bf16[512,1024]{1,0:T(8,128)(2,1)}, u32[]{:S(2)}, u32[]{:S(2)}) collective-permute-start(bf16[512,1024]{1,0:T(8,128)(2,1)} %add_convert_fusion.5), channel_id=1, source_target_pairs={{0,8},{1,17},{2,10},{3,19},{4,12},{5,21},{6,14},{7,23},{8,0},{9,25... | collective-permute-start | bytes 3145736 | tf_op jit(solution)/shard_map/ppermute | solution.py:199
  905.3 57.1 %collective-permute-start.60 = (bf16[512,1024]{1,0:T(8,128)(2,1)}, bf16[512,1024]{1,0:T(8,128)(2,1)}, u32[]{:S(2)}, u32[]{:S(2)}) collective-permute-start(bf16[512,1024]{1,0:T(8,128)(2,1)} %get-tuple-element.193), channel_id=1, source_target_pairs={{0,16},{1,9},{2,18},{3,11},{4,20},{5,13},{6,22},{7,15},{8,24},{9,1... | collective-permute-start | bytes 3145736 | tf_op jit(solution)/shard_map/ppermute | solution.py:199
  953.7 111.8 %collective-permute-start.76 = (bf16[512,2048]{1,0:T(8,128)(2,1)}, bf16[512,2048]{1,0:T(8,128)(2,1)}, u32[]{:S(2)}, u32[]{:S(2)}) collective-permute-start(bf16[512,2048]{1,0:T(8,128)(2,1)} %get-tuple-element.180), channel_id=1, source_target_pairs={{0,16},{1,9},{2,18},{3,11},{4,20},{5,13},{6,22},{7,15},{8,24},{9,1... | collective-permute-start | bytes 6291464 | tf_op jit(solution)/shard_map/ppermute | solution.py:199
  955.7 70.3 %collective-permute-start.81 = (bf16[512,1024]{1,0:T(8,128)(2,1)}, bf16[512,1024]{1,0:T(8,128)(2,1)}, u32[]{:S(2)}, u32[]{:S(2)}) collective-permute-start(bf16[512,1024]{1,0:T(8,128)(2,1)} %add_convert_fusion.3), channel_id=1, source_target_pairs={{0,8},{1,17},{2,10},{3,19},{4,12},{5,21},{6,14},{7,23},{8,0},{9,25... | collective-permute-start | bytes 3145736 | tf_op jit(solution)/shard_map/ppermute | solution.py:199
  957.9 67.1 %collective-permute-start.59 = (bf16[512,1024]{1,0:T(8,128)(2,1)}, bf16[512,1024]{1,0:T(8,128)(2,1)}, u32[]{:S(2)}, u32[]{:S(2)}) collective-permute-start(bf16[512,1024]{1,0:T(8,128)(2,1)} %get-tuple-element.192), channel_id=1, source_target_pairs={{0,16},{1,9},{2,18},{3,11},{4,20},{5,13},{6,22},{7,15},{8,24},{9,1... | collective-permute-start | bytes 3145736 | tf_op jit(solution)/shard_map/ppermute | solution.py:199
  962.4 103.1 %collective-permute-start.78 = (bf16[512,2048]{1,0:T(8,128)(2,1)}, bf16[512,2048]{1,0:T(8,128)(2,1)}, u32[]{:S(2)}, u32[]{:S(2)}) collective-permute-start(bf16[512,2048]{1,0:T(8,128)(2,1)} %add_convert_fusion.2), channel_id=1, source_target_pairs={{0,8},{1,17},{2,10},{3,19},{4,12},{5,21},{6,14},{7,23},{8,0},{9,25... | collective-permute-start | bytes 6291464 | tf_op jit(solution)/shard_map/ppermute | solution.py:199
  1044.3 27.9 %collective-permute-start.61 = (bf16[512,1024]{1,0:T(8,128)(2,1)}, bf16[512,1024]{1,0:T(8,128)(2,1)S(1)}, u32[]{:S(2)}, u32[]{:S(2)}) collective-permute-start(bf16[512,1024]{1,0:T(8,128)(2,1)} %add_convert_fusion.7), channel_id=1, source_target_pairs={{0,8},{1,17},{2,10},{3,19},{4,12},{5,21},{6,14},{7,23},{8,0},{9,25... | collective-permute-start | bytes 3145736 | tf_op jit(solution)/shard_map/ppermute | solution.py:199
  1056.8 28.3 %all-to-all-start.1 = ((f32[8,68,128]{2,1,0:T(8,128)}), f32[8,68,128]{2,1,0:T(8,128)S(1)}, u32[]{:S(2)}, u32[]{:S(2)}) async-start(f32[8,68,128]{2,1,0:T(8,128)} %bitcast_add_fusion), calls=%async_computation.6 | async-start | bytes 589824 | tf_op jit(solution)/shard_map/all_to_all | solution.py:944
  (187 other events, 3424.3 us)
Sparse Core Ops, SparseCore 0:
  78.4 62.9 all-gather.5
  244.4 57.7 all-gather.7
  304.4 45.6 all-gather.9
  394.0 60.3 reduce-scatter.7
  456.5 50.0 reduce-scatter.5
  521.6 49.5 all-gather.11
  572.8 45.6 all-gather.13
  648.4 48.7 reduce-scatter.11
  699.5 48.3 reduce-scatter.9
  777.3 66.5 reduce-scatter.13

commit v2 on v1

--- a/solution.py
+++ b/solution.py
@@ -752,7 +752,7 @@
         sine_part,
     )
     attended, inverse = attend(span, jnp.transpose(window), query_scaled, pair_all)
-    out_pieces, _, _ = gather_weight(
+    out_pieces, _, out_last = gather_weight(
         out_weight, pairs, row_total, False, kv_first, query_last, attended
     )
     attention_out = contract(me, attended, out_pieces)
@@ -770,7 +770,7 @@
     )
     feed_low = feed_in.astype(low)
     feed_pieces = xor_gather(
-        jnp.concatenate([gate_weight, up_weight], axis=1), ROW, row_total, feed_low
+        after(jnp.concatenate([gate_weight, up_weight], axis=1), out_last), ROW, row_total, feed_low
     )
     layer_own = jnp.concatenate([per_layer_gate, per_layer_projection], axis=1)
     feed_all = jnp.concatenate(feed_pieces, axis=0)
@@ -785,7 +785,7 @@
         tokens = tokens if done is None else after(tokens, done)
         gate_up = product(tokens, feed_all).astype(low)
         if h == 0:
-            down_pieces = xor_gather(down_weight, ROW, row_total, gate_up)
+            down_pieces = xor_gather(down_weight, ROW, row_total, feed_low)
             down_all = jnp.concatenate(down_pieces, axis=0)
         hidden, hidden_pull = jax.vjp(
             geglu, gate_up[:, :feed_width].astype(wide), gate_up[:, feed_width:].astype(wide)
@@ -838,7 +838,7 @@
                 (tokens, layer_grad, attended_pair, normed_pair)
             )
         else:
-            tokens = after(tokens, done, down_first, feed_first)
+            tokens = after(tokens, done, down_first, *feed_first)
         hidden_grad = product(tokens, down_all)
         gate_grad, up_grad = hidden_pulls[h](hidden_grad)
         feed_grad_low = jnp.concatenate([gate_grad.astype(low), up_grad.astype(low)], axis=1)
@@ -846,12 +846,17 @@
         feed_in_grads.append(lax.psum_scatter(done, COL, scatter_dimension=0, tiled=True))
         if h == 0:
             down_first = product_tn(after(tokens, done), hidden_lows[0]).astype(low)
-            feed_first = product_tn(after(feed_tokens[0], down_first), feed_grad_low).astype(low)
+            feed_first = [
+                product_tn(after(feed_tokens[0], down_first), one.astype(low)).astype(low)
+                for one in (gate_grad, up_grad)
+            ]
     feed_in_grad = jnp.concatenate(feed_in_grads, axis=0).astype(wide)
     down_total = product_tn(after(tokens, done), hidden_lows[1]) + down_first.astype(wide)
     down_total = down_total.astype(low)
-    feed_total = product_tn(after(feed_tokens[1], down_total), feed_grad_low)
-    feed_total = (feed_total + feed_first.astype(wide)).astype(low)
+    gate_total = product_tn(after(feed_tokens[1], down_total), gate_grad.astype(low))
+    gate_total = (gate_total + feed_first[0].astype(wide)).astype(low)
+    up_total = product_tn(after(feed_tokens[1], gate_total), up_grad.astype(low))
+    up_total = (up_total + feed_first[1].astype(wide)).astype(low)
     (
         inputs_grad,
         attention_grad,
@@ -915,8 +920,9 @@
     query_marks = []
     query_weight_grad = scatter_cols(query_total, row_total, pairs, mark, mark, query_marks)
     out_weight_grad = scatter_cols(out_total, row_total, pairs, query_part, normed_grad)
-    down_weight_grad = scatter_rows(down_total, row_total, feed_total, query_marks[0])
-    feed_weight_grad = scatter_rows(feed_total, row_total, pair_parts, marks[-1])
+    down_weight_grad = scatter_rows(down_total, row_total, up_total, query_marks[0])
+    gate_weight_grad = scatter_rows(gate_total, row_total, up_total, marks[-1])
+    up_weight_grad = scatter_rows(up_total, row_total, pair_parts, marks[-1])
     input_part, input_gain_grad = input_pull(after(normed_grad, mark))
     input_total = xor_blocks((inputs_grad + input_part).astype(low), me_row, row_total)
 
@@ -955,8 +961,8 @@
         kv_weight_grad[:, :kv_width],
         kv_weight_grad[:, kv_width:],
         out_weight_grad,
-        feed_weight_grad[:, :feed_width],
-        feed_weight_grad[:, feed_width:],
+        gate_weight_grad,
+        up_weight_grad,
         down_weight_grad,
         laurel_grad[:, :rank],
         laurel_grad[:, rank:],

time: 1110 us -> 1100 us (level)
  waiting for transfers between devices: 524 us -> 503 us
    ppermute x34 -> x37, waiting for transfers between devices: 200 us -> 111 us  [split_hop(): return lax.ppermute(values, (ROW, COL), pairs)]
    ppermute x51, waiting for transfers between devices: 174 us -> 234 us  [hop(): return lax.ppermute(values, axis, [(i, i ^ mask) for i in range(size)])]
    ppermute x34 -> x37, starting transfers between devices: 45.7 us -> 53.9 us  [split_hop(): return lax.ppermute(values, (ROW, COL), pairs)]
    unnamed x282 -> x328, local copies, waits for them, and re-layouts: 25.6 us -> 31.7 us
    dot_general x11 -> x13, matrix products: 64.3 us -> 59.6 us  [product_tn(): lax.dot_general(left, right, (((0,), (0,)), ((), ())), preferred_element_...]
  transfers between devices with their start and end apart: 97 -> 100, of which waited for: 44 -> 48; matrix products, arithmetic and copies ran while one was open for 21% -> 22% of each run, Pallas kernels for 6% -> 6%
where the time goes in v2:
time: 1100 us; the launch traced here: 1090 us
  waiting for transfers between devices  503 us (46%)
  matrix products  157 us (14%)
  starting transfers between devices  140 us (13%)
  other arithmetic  119 us (11%)
  Pallas kernels  96.7 us (9%)
  local copies, waits for them, and re-layouts  56.5 us (5%)
  between operations  19.6 us (2%)
    ppermute x51, waiting for transfers between devices, hop(): return lax.ppermute(values, axis, [(i, i ^ mask) for i in range(size)])  234 us
    reduce_scatter x4, waiting for transfers between devices, local(): lax.psum_scatter(done, COL, scatter_dimension=0, tiled=True)  151 us
    ppermute x37, waiting for transfers between devices, split_hop(): return lax.ppermute(values, (ROW, COL), pairs)  111 us
    ppermute x51, starting transfers between devices, hop(): return lax.ppermute(values, axis, [(i, i ^ mask) for i in range(size)])  75.9 us
    dot_general x13, matrix products, product_tn(): lax.dot_general(left, right, (((0,), (0,)), ((), ())), preferred_element_...  59.6 us
    ppermute x37, starting transfers between devices, split_hop(): return lax.ppermute(values, (ROW, COL), pairs)  53.9 us
    dot_general x8, matrix products, product(): return jnp.dot(left, right, preferred_element_type=jnp.float32)  51.4 us
    dot_general x8, matrix products, product_t(): lax.dot_general(left, right, (((1,), (1,)), ((), ())), preferred_element_...  46.3 us
  transfers between devices with their start and end apart: 100, of which 48 were waited for; matrix products, arithmetic and copies ran while one was open for 22% of the time, Pallas kernels for 6%

profile of v2, /device:TPU:0, one launch (start us, length us, event | category | flops | bytes accessed | tf_op | source)
XLA Modules:
  0.0 1092.3 jit_solution(7749747528911126014)
XLA Ops:
  9.3 5.1 collective-permute-start.3
  15.1 5.4 concatenate.94
  44.5 10.9 collective-permute-done.1
  60.6 5.2 collective-permute-done.17.refs_1_
  70.0 5.6 shard_map.394.columns_ref
  83.3 14.3 %collective-permute-done.4.refs_1_ = bf16[512,256]{1,0:T(8,128)(2,1)S(1)} collective-permute-done((bf16[512,256]{1,0:T(8,128)(2,1)S(1)}, bf16[512,256]{1,0:T(8,128)(2,1)S(1)}, u32[]{:S(2)}, u32[]{:S(2)}) %collective-permute-start.4) | collective-permute-done | bytes 262176 | tf_op jit(solution)/shard_map/ppermute | solution.py:193
  97.6 8.7 collective-permute-done.5.refs_2_
  115.1 21.4 %collective-permute-done.10.refs_1_ = bf16[4,512,256]{2,1,0:T(8,128)(2,1)S(1)} collective-permute-done((bf16[4,512,256]{2,1,0:T(8,128)(2,1)}, bf16[4,512,256]{2,1,0:T(8,128)(2,1)S(1)}, u32[]{:S(2)}, u32[]{:S(2)}) %collective-permute-start.10) | collective-permute-done | bytes 1048608 | tf_op jit(solution)/shard_map/ppermute | solution.py:193
  138.3 15.5 %collective-permute-start.23 = (bf16[512,256]{1,0:T(8,128)(2,1)S(1)}, bf16[512,256]{1,0:T(8,128)(2,1)S(1)}, u32[]{:S(2)}, u32[]{:S(2)}) collective-permute-start(bf16[512,256]{1,0:T(8,128)(2,1)S(1)} %copy-done.78), channel_id=1, source_target_pairs={{0,2},{1,3},{2,0},{3,1},{4,6},{5,7},{6,4},{7,5},{8,10},{9,11},{10,... | collective-permute-start | bytes 786440 | tf_op jit(solution)/shard_map/ppermute | solution.py:193
  154.0 10.2 collective-permute-done.23.refs_1_
  169.5 8.8 collective-permute-done.25.refs_3_
  188.4 7.1 shard_map.392.query_ref
  198.4 9.8 shard_map.396
  213.5 11.3 %collective-permute-done.28.refs_3_ = bf16[4,512,256]{2,1,0:T(8,128)(2,1)} collective-permute-done((bf16[4,512,256]{2,1,0:T(8,128)(2,1)S(1)}, bf16[4,512,256]{2,1,0:T(8,128)(2,1)}, u32[]{:S(2)}, u32[]{:S(2)}) %collective-permute-start.28) | collective-permute-done | bytes 1048608 | tf_op jit(solution)/shard_map/ppermute | solution.py:199
  229.4 7.4 shard_map.398
  251.1 44.6 %collective-permute-done.33 = bf16[512,2048]{1,0:T(8,128)(2,1)} collective-permute-done((bf16[512,2048]{1,0:T(8,128)(2,1)}, bf16[512,2048]{1,0:T(8,128)(2,1)}, u32[]{:S(2)}, u32[]{:S(2)}) %collective-permute-start.33) | collective-permute-done | bytes 2097184 | tf_op jit(solution)/shard_map/ppermute | solution.py:193
  299.5 18.5 %collective-permute-done.36 = bf16[512,1024]{1,0:T(8,128)(2,1)S(1)} collective-permute-done((bf16[512,1024]{1,0:T(8,128)(2,1)S(1)}, bf16[512,1024]{1,0:T(8,128)(2,1)S(1)}, u32[]{:S(2)}, u32[]{:S(2)}) %collective-permute-start.36) | collective-permute-done | bytes 1048608 | tf_op jit(solution)/shard_map/ppermute | solution.py:193
  322.9 29.4 %collective-permute-done.38 = bf16[512,1024]{1,0:T(8,128)(2,1)S(1)} collective-permute-done((bf16[512,1024]{1,0:T(8,128)(2,1)S(1)}, bf16[512,1024]{1,0:T(8,128)(2,1)S(1)}, u32[]{:S(2)}, u32[]{:S(2)}) %collective-permute-start.38) | collective-permute-done | bytes 1048608 | tf_op jit(solution)/shard_map/ppermute | solution.py:199
  361.7 12.8 %convolution_convert_fusion.3 = bf16[1024,2048]{1,0:T(8,128)(2,1)S(1)} fusion(bf16[1024,2048]{1,0:T(8,128)(2,1)} %all-gather.8.cloned.1.call-done, bf16[2048,2048]{1,0:T(8,128)(2,1)} %constant_dynamic-update-slice_fusion), kind=kOutput, calls=%fused_computation.55 | convolution fusion | flops 8592031744 | bytes 16777216 | tf_op jit(solution)/shard_map/dot_general | solution.py:176
  376.5 6.7 convolution_convert_fusion.8
  383.2 12.6 %convolution_convert_fusion.2 = bf16[1024,2048]{1,0:T(8,128)(2,1)S(1)} fusion(bf16[1024,2048]{1,0:T(8,128)(2,1)} %all-gather.10.cloned.1.call-done, bf16[2048,2048]{1,0:T(8,128)(2,1)} %constant_dynamic-update-slice_fusion), kind=kOutput, calls=%fused_computation.54 | convolution fusion | flops 8592031744 | bytes 16777216 | tf_op jit(solution)/shard_map/dot_general | solution.py:176
  397.8 6.7 convolution_convert_fusion.7
  405.5 8.9 collective-permute-start.39
  414.4 5.2 collective-permute-start.40
  439.4 9.1 collective-permute-done.43
  448.5 10.5 collective-permute-done.44
  465.5 51.4 %reduce-scatter.6.cloned.1.call-done = bf16[128,2048]{1,0:T(8,128)(2,1)} async-done(((bf16[1024,2048]{1,0:T(8,128)(2,1)}), bf16[128,2048]{1,0:T(8,128)(2,1)}) %reduce-scatter.6.cloned.1.call-update) | async-done | bytes 524304 | tf_op jit(solution)/shard_map/reduce_scatter | solution.py:795
  581.4 11.8 %fusion.9 = (bf16[1024,1024]{1,0:T(8,128)(2,1)S(1)}, bf16[1024,1024]{1,0:T(8,128)(2,1)S(1)}) fusion(bf16[1024,2048]{1,0:T(8,128)(2,1)} %copy-done.150, bf16[1024,2048]{1,0:T(8,128)(2,1)} %all-gather.12.cloned.1.call-done, bf16[2048,1024]{1,0:T(8,128)(2,1)} %copy-done.71), kind=kOutput, calls=%fused_computation.26 | convolution fusion | flops 4322230272 | bytes 16777216 | tf_op jit(solution)/shard_map/dot_general | solution.py:176
  595.2 12.7 %fusion.31 = bf16[1024,2048]{1,0:T(8,128)(2,1)} fusion(bf16[2048,2048]{1,0:T(8,128)(2,1)} %constant_dynamic-update-slice_fusion, bf16[1024,1024]{1,0:T(8,128)(2,1)S(1)} %get-tuple-element.193, bf16[1024,1024]{1,0:T(8,128)(2,1)S(1)} %get-tuple-element.192), kind=kOutput, calls=%fused_computation.62 | convolution fusion | flops 8600420352 | bytes 16777216 | tf_op jit(solution)/shard_map/dot_general | solution.py:180
  607.8 10.4 convolution_convert_fusion.6
  618.2 6.4 convolution_convert_fusion.4
  624.6 6.2 convolution_convert_fusion.5
  630.8 11.4 %fusion.6 = (bf16[1024,1024]{1,0:T(8,128)(2,1)S(1)}, bf16[1024,1024]{1,0:T(8,128)(2,1)S(1)}) fusion(bf16[1024,2048]{1,0:T(8,128)(2,1)} %copy-done.155, bf16[1024,2048]{1,0:T(8,128)(2,1)} %all-gather.14.cloned.1.call-done, bf16[2048,1024]{1,0:T(8,128)(2,1)} %copy-done.71), kind=kOutput, calls=%fused_computation.23 | convolution fusion | flops 4322230272 | bytes 16777216 | tf_op jit(solution)/shard_map/dot_general | solution.py:176
  644.2 12.6 %fusion.28 = bf16[1024,2048]{1,0:T(8,128)(2,1)} fusion(bf16[2048,2048]{1,0:T(8,128)(2,1)} %constant_dynamic-update-slice_fusion, bf16[1024,1024]{1,0:T(8,128)(2,1)S(1)} %get-tuple-element.191, bf16[1024,1024]{1,0:T(8,128)(2,1)S(1)} %get-tuple-element.190), kind=kOutput, calls=%fused_computation.61 | convolution fusion | flops 8600420352 | bytes 16777216 | tf_op jit(solution)/shard_map/dot_general | solution.py:180
  661.1 44.6 %reduce-scatter.12.cloned.1.call-done = bf16[128,2048]{1,0:T(8,128)(2,1)} async-done(((bf16[1024,2048]{1,0:T(8,128)(2,1)}), bf16[128,2048]{1,0:T(8,128)(2,1)}) %reduce-scatter.12.cloned.1.call-update) | async-done | bytes 524304 | tf_op jit(solution)/shard_map/reduce_scatter | solution.py:846
  705.7 50.7 %reduce-scatter.10.cloned.1.call-done = bf16[128,2048]{1,0:T(8,128)(2,1)} async-done(((bf16[1024,2048]{1,0:T(8,128)(2,1)}), bf16[128,2048]{1,0:T(8,128)(2,1)}) %reduce-scatter.10.cloned.1.call-update) | async-done | bytes 524304 | tf_op jit(solution)/shard_map/reduce_scatter | solution.py:846
  766.2 7.1 shard_map.403.grad_ref
  773.3 13.1 %shard_map.404 = (f32[256,2048]{1,0:T(8,128)}, bf16[8,2,256,512]{3,2,1,0:T(8,128)(2,1)}) custom-call(s32[2]{0:T(128)} %pad_add_fusion.1.span_ref, s32[2,256]{1,0:T(2,128)} %get-tuple-element.272.window_ref, bf16[256,2048]{1,0:T(8,128)(2,1)} %shard_map.393.query_ref, bf16[8,2,256,512]{3,2,1,0:T(8,128)(2,1)} %bitcast.121, bf16[8,2,256,512]{3,2,1,0:T(8,128)(2,1)} %bitcast.122, ...), custom_call_target="tpu_custom_call" | custom-call | flops 10737418240 | bytes 8388608 | tf_op jit(solution)/shard_map/pallas_call | solution.py:601
  786.5 9.8 add_convert_fusion.2
  805.5 5.2 add_convert_fusion
  831.5 19.6 %collective-permute-done.80 = bf16[512,1024]{1,0:T(8,128)(2,1)S(1)} collective-permute-done((bf16[512,1024]{1,0:T(8,128)(2,1)}, bf16[512,1024]{1,0:T(8,128)(2,1)S(1)}, u32[]{:S(2)}, u32[]{:S(2)}) %collective-permute-start.80) | collective-permute-done | bytes 1048608 | tf_op jit(solution)/shard_map/ppermute | solution.py:199
  880.7 7.6 shard_map.407
  917.3 6.0 shard_map.410
  934.6 15.1 %collective-permute-start.74 = (bf16[512,256]{1,0:T(8,128)(2,1)S(1)}, bf16[512,256]{1,0:T(8,128)(2,1)}, u32[]{:S(2)}, u32[]{:S(2)}) collective-permute-start(bf16[512,256]{1,0:T(8,128)(2,1)S(1)} %get-tuple-element.214), channel_id=1, source_target_pairs={{0,4},{1,3},{2,6},{3,1},{4,0},{5,7},{6,2},{7,5},{8,12},{9,11},{10,... | collective-permute-start | bytes 786440 | tf_op jit(solution)/shard_map/ppermute | solution.py:199
  981.7 5.8 collective-permute-done.85
  991.0 43.6 %collective-permute-done.87 = f32[8,68,128]{2,1,0:T(8,128)S(1)} collective-permute-done((f32[8,68,128]{2,1,0:T(8,128)S(1)}, f32[8,68,128]{2,1,0:T(8,128)S(1)}, u32[]{:S(2)}, u32[]{:S(2)}) %collective-permute-start.87) | collective-permute-done | bytes 278560 | tf_op jit(solution)/shard_map/ppermute | solution.py:193
  1065.5 7.2 collective-permute-done.63
  1074.8 8.4 collective-permute-done.62
  (694 shorter events, 394.0 us)
Async XLA Ops:
  9.3 28.0 %collective-permute-start.3 = (bf16[512,128]{1,0:T(8,128)(2,1)S(1)}, bf16[512,128]{1,0:T(8,128)(2,1)S(1)}, u32[]{:S(2)}, u32[]{:S(2)}) collective-permute-start(bf16[512,128]{1,0:T(8,128)(2,1)S(1)} %pad_maximum_fusion.17.refs_0_), channel_id=1, source_target_pairs={{0,6},{1,7},{2,4},{3,5},{4,2},{5,3},{6,0},{7,1},{8,14},{9,15},{10,... | collective-permute-start | bytes 393224 | tf_op jit(solution)/shard_map/ppermute | solution.py:193
  14.5 23.3 %collective-permute-start.8 = (bf16[512,128]{1,0:T(8,128)(2,1)S(1)}, bf16[512,128]{1,0:T(8,128)(2,1)S(1)}, u32[]{:S(2)}, u32[]{:S(2)}) collective-permute-start(bf16[512,128]{1,0:T(8,128)(2,1)S(1)} %pad_maximum_fusion.17.refs_0_), channel_id=1, source_target_pairs={{0,4},{1,5},{2,6},{3,7},{4,0},{5,1},{6,2},{7,3},{8,12},{9,13},{10,... | collective-permute-start | bytes 393224 | tf_op jit(solution)/shard_map/ppermute | solution.py:193
  27.1 171.3 %all-gather.6.cloned.1.call-start = ((), (), s32[]{:S(2)}) async-start(), calls=%async_computation.7 | async-start | bytes 4718592 | tf_op jit(solution)/shard_map/all_gather | solution.py:743
  78.2 283.5 %all-gather.8.cloned.1.call-start = ((), (), s32[]{:S(2)}) async-start(), calls=%async_computation.8 | async-start | bytes 4718592 | tf_op jit(solution)/shard_map/all_gather | solution.py:782
  80.0 26.3 %collective-permute-start.5 = (bf16[512,256]{1,0:T(8,128)(2,1)S(1)}, bf16[512,256]{1,0:T(8,128)(2,1)S(1)}, u32[]{:S(2)}, u32[]{:S(2)}) collective-permute-start(bf16[512,256]{1,0:T(8,128)(2,1)S(1)} %copy-done.77), channel_id=1, source_target_pairs={{0,4},{1,5},{2,6},{3,7},{4,0},{5,1},{6,2},{7,3},{8,12},{9,13},{10,... | collective-permute-start | bytes 786440 | tf_op jit(solution)/shard_map/ppermute | solution.py:193
  81.7 27.8 %collective-permute-start.6 = (bf16[512,256]{1,0:T(8,128)(2,1)S(1)}, bf16[512,256]{1,0:T(8,128)(2,1)S(1)}, u32[]{:S(2)}, u32[]{:S(2)}) collective-permute-start(bf16[512,256]{1,0:T(8,128)(2,1)S(1)} %copy-done.77), channel_id=1, source_target_pairs={{0,6},{1,7},{2,4},{3,5},{4,2},{5,3},{6,0},{7,1},{8,14},{9,15},{10,... | collective-permute-start | bytes 786440 | tf_op jit(solution)/shard_map/ppermute | solution.py:193
  112.5 24.1 %collective-permute-start.10 = (bf16[4,512,256]{2,1,0:T(8,128)(2,1)}, bf16[4,512,256]{2,1,0:T(8,128)(2,1)S(1)}, u32[]{:S(2)}, u32[]{:S(2)}) collective-permute-start(bf16[4,512,256]{2,1,0:T(8,128)(2,1)} %shard_map.390.refs_0_), channel_id=1, source_target_pairs={{0,8},{8,0},{16,24},{24,16},{1,9},{9,1},{17,25},{25,17},{2,10},{10... | collective-permute-start | bytes 3145736 | tf_op jit(solution)/shard_map/ppermute | solution.py:193
  113.2 24.1 %collective-permute-start.11 = (bf16[4,512,256]{2,1,0:T(8,128)(2,1)}, bf16[4,512,256]{2,1,0:T(8,128)(2,1)S(1)}, u32[]{:S(2)}, u32[]{:S(2)}) collective-permute-start(bf16[4,512,256]{2,1,0:T(8,128)(2,1)} %shard_map.390.refs_0_), channel_id=1, source_target_pairs={{0,16},{8,24},{16,0},{24,8},{1,17},{9,25},{17,1},{25,9},{2,18},{10... | collective-permute-start | bytes 3145736 | tf_op jit(solution)/shard_map/ppermute | solution.py:193
  137.4 26.8 %collective-permute-start.12 = (bf16[4,512,256]{2,1,0:T(8,128)(2,1)S(1)}, bf16[4,512,256]{2,1,0:T(8,128)(2,1)}, u32[]{:S(2)}, u32[]{:S(2)}) collective-permute-start(bf16[4,512,256]{2,1,0:T(8,128)(2,1)S(1)} %broadcast_select_fusion.8), channel_id=1, source_target_pairs={{0,16},{1,9},{2,18},{3,11},{4,20},{5,13},{6,22},{7,15},{8,24},{9,1... | collective-permute-start | bytes 3145736 | tf_op jit(solution)/shard_map/ppermute | solution.py:199
  138.3 43.3 %collective-permute-start.13 = (bf16[4,512,256]{2,1,0:T(8,128)(2,1)S(1)}, bf16[4,512,256]{2,1,0:T(8,128)(2,1)}, u32[]{:S(2)}, u32[]{:S(2)}) collective-permute-start(bf16[4,512,256]{2,1,0:T(8,128)(2,1)S(1)} %copy-done.13), channel_id=1, source_target_pairs={{0,1},{1,0},{2,3},{3,2},{4,5},{5,4},{6,7},{7,6},{8,9},{9,8},{10,11... | collective-permute-start | bytes 3145736 | tf_op jit(solution)/shard_map/ppermute | solution.py:193
  138.3 25.9 %collective-permute-start.23 = (bf16[512,256]{1,0:T(8,128)(2,1)S(1)}, bf16[512,256]{1,0:T(8,128)(2,1)S(1)}, u32[]{:S(2)}, u32[]{:S(2)}) collective-permute-start(bf16[512,256]{1,0:T(8,128)(2,1)S(1)} %copy-done.78), channel_id=1, source_target_pairs={{0,2},{1,3},{2,0},{3,1},{4,6},{5,7},{6,4},{7,5},{8,10},{9,11},{10,... | collective-permute-start | bytes 786440 | tf_op jit(solution)/shard_map/ppermute | solution.py:193
  153.8 34.6 %collective-permute-start.14 = (bf16[4,512,256]{2,1,0:T(8,128)(2,1)S(1)}, bf16[4,512,256]{2,1,0:T(8,128)(2,1)}, u32[]{:S(2)}, u32[]{:S(2)}) collective-permute-start(bf16[4,512,256]{2,1,0:T(8,128)(2,1)S(1)} %collective-permute-done.10.refs_1_), channel_id=1, source_target_pairs={{0,1},{1,0},{2,3},{3,2},{4,5},{5,4},{6,7},{7,6},{8,9},{9,8},{10,11... | collective-permute-start | bytes 3145736 | tf_op jit(solution)/shard_map/ppermute | solution.py:193
  164.2 24.2 %collective-permute-start.15 = (bf16[4,512,256]{2,1,0:T(8,128)(2,1)S(1)}, bf16[4,512,256]{2,1,0:T(8,128)(2,1)}, u32[]{:S(2)}, u32[]{:S(2)}) collective-permute-start(bf16[4,512,256]{2,1,0:T(8,128)(2,1)S(1)} %collective-permute-done.11.refs_2_), channel_id=1, source_target_pairs={{0,1},{1,0},{2,3},{3,2},{4,5},{5,4},{6,7},{7,6},{8,9},{9,8},{10,11... | collective-permute-start | bytes 3145736 | tf_op jit(solution)/shard_map/ppermute | solution.py:193
  164.2 24.1 %collective-permute-start.16 = (bf16[4,512,256]{2,1,0:T(8,128)(2,1)}, bf16[4,512,256]{2,1,0:T(8,128)(2,1)}, u32[]{:S(2)}, u32[]{:S(2)}) collective-permute-start(bf16[4,512,256]{2,1,0:T(8,128)(2,1)} %collective-permute-done.12.refs_3_), channel_id=1, source_target_pairs={{0,1},{1,0},{2,3},{3,2},{4,5},{5,4},{6,7},{7,6},{8,9},{9,8},{10,11... | collective-permute-start | bytes 3145736 | tf_op jit(solution)/shard_map/ppermute | solution.py:193
  180.5 27.8 %collective-permute-start.26 = (bf16[4,512,256]{2,1,0:T(8,128)(2,1)}, bf16[4,512,256]{2,1,0:T(8,128)(2,1)}, u32[]{:S(2)}, u32[]{:S(2)}) collective-permute-start(bf16[4,512,256]{2,1,0:T(8,128)(2,1)} %shard_map.397.refs_0_), channel_id=1, source_target_pairs={{0,8},{8,0},{16,24},{24,16},{1,9},{9,1},{17,25},{25,17},{2,10},{10... | collective-permute-start | bytes 3145736 | tf_op jit(solution)/shard_map/ppermute | solution.py:193
  181.6 26.7 %collective-permute-start.27 = (bf16[4,512,256]{2,1,0:T(8,128)(2,1)}, bf16[4,512,256]{2,1,0:T(8,128)(2,1)}, u32[]{:S(2)}, u32[]{:S(2)}) collective-permute-start(bf16[4,512,256]{2,1,0:T(8,128)(2,1)} %shard_map.397.refs_0_), channel_id=1, source_target_pairs={{0,16},{8,24},{16,0},{24,8},{1,17},{9,25},{17,1},{25,9},{2,18},{10... | collective-permute-start | bytes 3145736 | tf_op jit(solution)/shard_map/ppermute | solution.py:193
  243.7 139.5 %all-gather.10.cloned.1.call-start = ((), (), s32[]{:S(2)}) async-start(), calls=%async_computation.10 | async-start | bytes 4718592 | tf_op jit(solution)/shard_map/all_gather | solution.py:782
  246.9 48.8 %collective-permute-start.33 = (bf16[512,2048]{1,0:T(8,128)(2,1)}, bf16[512,2048]{1,0:T(8,128)(2,1)}, u32[]{:S(2)}, u32[]{:S(2)}) collective-permute-start(bf16[512,2048]{1,0:T(8,128)(2,1)} %pad_maximum_fusion), channel_id=1, source_target_pairs={{0,8},{8,0},{16,24},{24,16},{1,9},{9,1},{17,25},{25,17},{2,10},{10... | collective-permute-start | bytes 6291464 | tf_op jit(solution)/shard_map/ppermute | solution.py:193
  248.6 48.8 %collective-permute-start.34 = (bf16[512,2048]{1,0:T(8,128)(2,1)}, bf16[512,2048]{1,0:T(8,128)(2,1)}, u32[]{:S(2)}, u32[]{:S(2)}) collective-permute-start(bf16[512,2048]{1,0:T(8,128)(2,1)} %pad_maximum_fusion), channel_id=1, source_target_pairs={{0,16},{8,24},{16,0},{24,8},{1,17},{9,25},{17,1},{25,9},{2,18},{10... | collective-permute-start | bytes 6291464 | tf_op jit(solution)/shard_map/ppermute | solution.py:193
  248.8 216.7 %reduce-scatter.8.cloned.1.call-start = ((), (), s32[]{:S(2)}) async-start(), calls=%async_computation.11 | async-start | bytes 4718592 | tf_op jit(solution)/shard_map/reduce_scatter | solution.py:795
  248.9 69.2 %collective-permute-start.36 = (bf16[512,1024]{1,0:T(8,128)(2,1)S(1)}, bf16[512,1024]{1,0:T(8,128)(2,1)S(1)}, u32[]{:S(2)}, u32[]{:S(2)}) collective-permute-start(bf16[512,1024]{1,0:T(8,128)(2,1)S(1)} %copy-done.60), channel_id=1, source_target_pairs={{0,8},{8,0},{16,24},{24,16},{1,9},{9,1},{17,25},{25,17},{2,10},{10... | collective-permute-start | bytes 3145736 | tf_op jit(solution)/shard_map/ppermute | solution.py:193
  250.1 68.5 %collective-permute-start.37 = (bf16[512,1024]{1,0:T(8,128)(2,1)S(1)}, bf16[512,1024]{1,0:T(8,128)(2,1)S(1)}, u32[]{:S(2)}, u32[]{:S(2)}) collective-permute-start(bf16[512,1024]{1,0:T(8,128)(2,1)S(1)} %copy-done.60), channel_id=1, source_target_pairs={{0,16},{8,24},{16,0},{24,8},{1,17},{9,25},{17,1},{25,9},{2,18},{10... | collective-permute-start | bytes 3145736 | tf_op jit(solution)/shard_map/ppermute | solution.py:193
  299.2 61.0 %collective-permute-start.35 = (bf16[512,2048]{1,0:T(8,128)(2,1)S(1)}, bf16[512,2048]{1,0:T(8,128)(2,1)S(1)}, u32[]{:S(2)}, u32[]{:S(2)}) collective-permute-start(bf16[512,2048]{1,0:T(8,128)(2,1)S(1)} %broadcast_select_fusion), channel_id=1, source_target_pairs={{0,16},{1,9},{2,18},{3,11},{4,20},{5,13},{6,22},{7,15},{8,24},{9,1... | collective-permute-start | bytes 6291464 | tf_op jit(solution)/shard_map/ppermute | solution.py:199
  318.7 33.6 %collective-permute-start.38 = (bf16[512,1024]{1,0:T(8,128)(2,1)S(1)}, bf16[512,1024]{1,0:T(8,128)(2,1)S(1)}, u32[]{:S(2)}, u32[]{:S(2)}) collective-permute-start(bf16[512,1024]{1,0:T(8,128)(2,1)S(1)} %broadcast_select_fusion.6), channel_id=1, source_target_pairs={{0,16},{1,9},{2,18},{3,11},{4,20},{5,13},{6,22},{7,15},{8,24},{9,1... | collective-permute-start | bytes 3145736 | tf_op jit(solution)/shard_map/ppermute | solution.py:199
  404.6 112.3 %reduce-scatter.6.cloned.1.call-start = ((), (), s32[]{:S(2)}) async-start(), calls=%async_computation.9 | async-start | bytes 4718592 | tf_op jit(solution)/shard_map/reduce_scatter | solution.py:795
  405.2 176.2 %all-gather.12.cloned.1.call-start = ((), (), s32[]{:S(2)}) async-start(), calls=%async_computation.12 | async-start | bytes 4718592 | tf_op jit(solution)/shard_map/all_gather | solution.py:833
  433.7 25.3 %collective-permute-start.44 = (bf16[8,64,512]{2,1,0:T(8,128)(2,1)}, bf16[8,64,512]{2,1,0:T(8,128)(2,1)}, u32[]{:S(2)}, u32[]{:S(2)}) collective-permute-start(bf16[8,64,512]{2,1,0:T(8,128)(2,1)} %shard_map.400), channel_id=1, source_target_pairs={{0,16},{8,24},{16,0},{24,8},{1,17},{9,25},{17,1},{25,9},{2,18},{10... | collective-permute-start | bytes 1572872 | tf_op jit(solution)/shard_map/ppermute | solution.py:193
  433.7 25.3 %collective-permute-start.45 = (bf16[8,64,512]{2,1,0:T(8,128)(2,1)}, bf16[8,64,512]{2,1,0:T(8,128)(2,1)}, u32[]{:S(2)}, u32[]{:S(2)}) collective-permute-start(bf16[8,64,512]{2,1,0:T(8,128)(2,1)} %shard_map.400), channel_id=1, source_target_pairs={{0,24},{8,16},{16,8},{24,0},{1,25},{9,17},{17,9},{25,1},{2,26},{10... | collective-permute-start | bytes 1572872 | tf_op jit(solution)/shard_map/ppermute | solution.py:193
  531.7 99.1 %all-gather.14.cloned.1.call-start = ((), (), s32[]{:S(2)}) async-start(), calls=%async_computation.14 | async-start | bytes 4718592 | tf_op jit(solution)/shard_map/all_gather | solution.py:833
  560.1 145.6 %reduce-scatter.12.cloned.1.call-start = ((), (), s32[]{:S(2)}) async-start(), calls=%async_computation.15 | async-start | bytes 4718592 | tf_op jit(solution)/shard_map/reduce_scatter | solution.py:846
  656.9 99.5 %reduce-scatter.10.cloned.1.call-start = ((), (), s32[]{:S(2)}) async-start(), calls=%async_computation.13 | async-start | bytes 4718592 | tf_op jit(solution)/shard_map/reduce_scatter | solution.py:846
  657.7 245.5 %reduce-scatter.14.cloned.1.call-start = ((), (), s32[]{:S(2)}) async-start(), calls=%async_computation.16 | async-start | bytes 4718592 | tf_op jit(solution)/shard_map/reduce_scatter | solution.py:874
  815.1 36.1 %collective-permute-start.80 = (bf16[512,1024]{1,0:T(8,128)(2,1)}, bf16[512,1024]{1,0:T(8,128)(2,1)S(1)}, u32[]{:S(2)}, u32[]{:S(2)}) collective-permute-start(bf16[512,1024]{1,0:T(8,128)(2,1)} %get-tuple-element.197), channel_id=1, source_target_pairs={{0,16},{1,9},{2,18},{3,11},{4,20},{5,13},{6,22},{7,15},{8,24},{9,1... | collective-permute-start | bytes 3145736 | tf_op jit(solution)/shard_map/ppermute | solution.py:199
  816.0 35.2 %collective-permute-start.55 = (bf16[256,2048]{1,0:T(8,128)(2,1)S(1)}, bf16[256,2048]{1,0:T(8,128)(2,1)}, u32[]{:S(2)}, u32[]{:S(2)}) collective-permute-start(bf16[256,2048]{1,0:T(8,128)(2,1)S(1)} %copy-done.31), channel_id=1, source_target_pairs={{0,1},{1,0},{2,3},{3,2},{4,5},{5,4},{6,7},{7,6},{8,9},{9,8},{10,11... | collective-permute-start | bytes 3145736 | tf_op jit(solution)/shard_map/ppermute | solution.py:193
  822.2 145.9 %collective-permute-start.82 = (bf16[512,1024]{1,0:T(8,128)(2,1)}, bf16[512,1024]{1,0:T(8,128)(2,1)}, u32[]{:S(2)}, u32[]{:S(2)}) collective-permute-start(bf16[512,1024]{1,0:T(8,128)(2,1)} %get-tuple-element.194), channel_id=1, source_target_pairs={{0,16},{1,9},{2,18},{3,11},{4,20},{5,13},{6,22},{7,15},{8,24},{9,1... | collective-permute-start | bytes 3145736 | tf_op jit(solution)/shard_map/ppermute | solution.py:199
  824.5 143.6 %collective-permute-start.84 = (bf16[512,1024]{1,0:T(8,128)(2,1)}, bf16[512,1024]{1,0:T(8,128)(2,1)}, u32[]{:S(2)}, u32[]{:S(2)}) collective-permute-start(bf16[512,1024]{1,0:T(8,128)(2,1)} %add_convert_fusion.3), channel_id=1, source_target_pairs={{0,8},{1,17},{2,10},{3,19},{4,12},{5,21},{6,14},{7,23},{8,0},{9,25... | collective-permute-start | bytes 3145736 | tf_op jit(solution)/shard_map/ppermute | solution.py:199
  872.2 56.2 %collective-permute-start.70 = (bf16[512,1024]{1,0:T(8,128)(2,1)}, bf16[512,1024]{1,0:T(8,128)(2,1)}, u32[]{:S(2)}, u32[]{:S(2)}) collective-permute-start(bf16[512,1024]{1,0:T(8,128)(2,1)} %get-tuple-element.200), channel_id=1, source_target_pairs={{0,16},{1,9},{2,18},{3,11},{4,20},{5,13},{6,22},{7,15},{8,24},{9,1... | collective-permute-start | bytes 3145736 | tf_op jit(solution)/shard_map/ppermute | solution.py:199
  872.2 26.3 %collective-permute-start.71 = (bf16[512,1024]{1,0:T(8,128)(2,1)}, bf16[512,1024]{1,0:T(8,128)(2,1)}, u32[]{:S(2)}, u32[]{:S(2)}) collective-permute-start(bf16[512,1024]{1,0:T(8,128)(2,1)} %get-tuple-element.201), channel_id=1, source_target_pairs={{0,16},{1,9},{2,18},{3,11},{4,20},{5,13},{6,22},{7,15},{8,24},{9,1... | collective-permute-start | bytes 3145736 | tf_op jit(solution)/shard_map/ppermute | solution.py:199
  901.4 29.0 %collective-permute-start.72 = (bf16[512,1024]{1,0:T(8,128)(2,1)}, bf16[512,1024]{1,0:T(8,128)(2,1)}, u32[]{:S(2)}, u32[]{:S(2)}) collective-permute-start(bf16[512,1024]{1,0:T(8,128)(2,1)} %add_convert_fusion.7), channel_id=1, source_target_pairs={{0,8},{1,17},{2,10},{3,19},{4,12},{5,21},{6,14},{7,23},{8,0},{9,25... | collective-permute-start | bytes 3145736 | tf_op jit(solution)/shard_map/ppermute | solution.py:199
  913.0 48.6 %collective-permute-start.60 = (bf16[512,1024]{1,0:T(8,128)(2,1)}, bf16[512,1024]{1,0:T(8,128)(2,1)}, u32[]{:S(2)}, u32[]{:S(2)}) collective-permute-start(bf16[512,1024]{1,0:T(8,128)(2,1)} %get-tuple-element.203), channel_id=1, source_target_pairs={{0,16},{1,9},{2,18},{3,11},{4,20},{5,13},{6,22},{7,15},{8,24},{9,1... | collective-permute-start | bytes 3145736 | tf_op jit(solution)/shard_map/ppermute | solution.py:199
  928.4 27.7 %collective-permute-start.58 = (bf16[512,512]{0,1:T(8,128)(2,1)}, bf16[512,512]{0,1:T(8,128)(2,1)}, u32[]{:S(2)}, u32[]{:S(2)}) collective-permute-start(bf16[512,512]{0,1:T(8,128)(2,1)} %get-tuple-element.207), channel_id=1, source_target_pairs={{0,16},{1,9},{2,18},{3,11},{4,20},{5,13},{6,22},{7,15},{8,24},{9,1... | collective-permute-start | bytes 1572872 | tf_op jit(solution)/shard_map/ppermute | solution.py:199
  956.1 25.4 %collective-permute-start.65 = (bf16[512,512]{0,1:T(8,128)(2,1)}, bf16[512,512]{0,1:T(8,128)(2,1)}, u32[]{:S(2)}, u32[]{:S(2)}) collective-permute-start(bf16[512,512]{0,1:T(8,128)(2,1)} %get-tuple-element.206), channel_id=1, source_target_pairs={{0,16},{1,9},{2,18},{3,11},{4,20},{5,13},{6,22},{7,15},{8,24},{9,1... | collective-permute-start | bytes 1572872 | tf_op jit(solution)/shard_map/ppermute | solution.py:199
  977.6 69.6 %collective-permute-start.79 = (bf16[512,1024]{1,0:T(8,128)(2,1)}, bf16[512,1024]{1,0:T(8,128)(2,1)}, u32[]{:S(2)}, u32[]{:S(2)}) collective-permute-start(bf16[512,1024]{1,0:T(8,128)(2,1)} %get-tuple-element.196), channel_id=1, source_target_pairs={{0,16},{1,9},{2,18},{3,11},{4,20},{5,13},{6,22},{7,15},{8,24},{9,1... | collective-permute-start | bytes 3145736 | tf_op jit(solution)/shard_map/ppermute | solution.py:199
  981.5 70.2 %collective-permute-start.76 = (bf16[512,1024]{1,0:T(8,128)(2,1)}, bf16[512,1024]{1,0:T(8,128)(2,1)}, u32[]{:S(2)}, u32[]{:S(2)}) collective-permute-start(bf16[512,1024]{1,0:T(8,128)(2,1)} %get-tuple-element.198), channel_id=1, source_target_pairs={{0,16},{1,9},{2,18},{3,11},{4,20},{5,13},{6,22},{7,15},{8,24},{9,1... | collective-permute-start | bytes 3145736 | tf_op jit(solution)/shard_map/ppermute | solution.py:199
  987.5 64.2 %collective-permute-start.78 = (bf16[512,1024]{1,0:T(8,128)(2,1)S(1)}, bf16[512,1024]{1,0:T(8,128)(2,1)}, u32[]{:S(2)}, u32[]{:S(2)}) collective-permute-start(bf16[512,1024]{1,0:T(8,128)(2,1)S(1)} %copy-done.58), channel_id=1, source_target_pairs={{0,8},{1,17},{2,10},{3,19},{4,12},{5,21},{6,14},{7,23},{8,0},{9,25... | collective-permute-start | bytes 3145736 | tf_op jit(solution)/shard_map/ppermute | solution.py:199
  987.7 62.5 %collective-permute-start.81 = (bf16[512,1024]{1,0:T(8,128)(2,1)S(1)}, bf16[512,1024]{1,0:T(8,128)(2,1)}, u32[]{:S(2)}, u32[]{:S(2)}) collective-permute-start(bf16[512,1024]{1,0:T(8,128)(2,1)S(1)} %copy-done.59), channel_id=1, source_target_pairs={{0,8},{1,17},{2,10},{3,19},{4,12},{5,21},{6,14},{7,23},{8,0},{9,25... | collective-permute-start | bytes 3145736 | tf_op jit(solution)/shard_map/ppermute | solution.py:199
  989.5 45.0 %collective-permute-start.87 = (f32[8,68,128]{2,1,0:T(8,128)S(1)}, f32[8,68,128]{2,1,0:T(8,128)S(1)}, u32[]{:S(2)}, u32[]{:S(2)}) collective-permute-start(f32[8,68,128]{2,1,0:T(8,128)S(1)} %get-tuple-element.211), channel_id=1, source_target_pairs={{0,24},{8,16},{16,8},{24,0},{1,25},{9,17},{17,9},{25,1},{2,26},{10... | collective-permute-start | bytes 835592 | tf_op jit(solution)/shard_map/ppermute | solution.py:193
  1043.6 29.3 %all-to-all-start.1 = ((f32[8,68,128]{2,1,0:T(8,128)}), f32[8,68,128]{2,1,0:T(8,128)S(1)}, u32[]{:S(2)}, u32[]{:S(2)}) async-start(f32[8,68,128]{2,1,0:T(8,128)} %bitcast_add_fusion), calls=%async_computation.6 | async-start | bytes 589824 | tf_op jit(solution)/shard_map/all_to_all | solution.py:950
  (212 other events, 3475.0 us)
Sparse Core Ops, SparseCore 0:
  78.3 62.9 all-gather.5
  243.8 57.7 all-gather.7
  303.2 45.6 all-gather.9
  404.6 60.8 reduce-scatter.7
  467.7 49.1 reduce-scatter.5
  531.8 49.5 all-gather.11
  583.0 45.6 all-gather.13
  657.0 48.7 reduce-scatter.11
  708.0 48.3 reduce-scatter.9
  786.6 66.5 reduce-scatter.13

commit v3 on v2

--- a/solution.py
+++ b/solution.py
@@ -300,7 +300,7 @@
     height = blocks.shape[2]
     half = jax.ShapeDtypeStruct((row_total, pairs, height, width), total.dtype)
     out_block = pl.BlockSpec((None, pairs, height, width), lambda r, s: (r, 0, 0, 0))
-    keep, give = pl.pallas_call(
+    deal = pl.pallas_call(
         partial(deal_rows_body, pairs),
         out_shape=(half, half),
         grid_spec=pltpu.PrefetchScalarGridSpec(
@@ -314,7 +314,8 @@
         cost_estimate=pl.CostEstimate(
             flops=0, transcendentals=0, bytes_accessed=4 * total.size
         ),
-    )(me, blocks)
+    )
+    keep, give = deal(me, blocks)
     both = add_low(keep, hop(give, COL, 1)).reshape(row_total, pairs * height, width)
     mine = xor_scatter(both, ROW).astype(jnp.bfloat16)
     return xor_scatter(mine.reshape(pairs, height, width), COL)
@@ -364,6 +365,31 @@
         out_shape=jax.ShapeDtypeStruct((2 * pairs,) + own.shape, own.dtype),
         in_specs=[pl.BlockSpec(memory_space=pltpu.SMEM), vmem, vmem],
     )(me, stacked, other)
+
+
+def join_body(me_ref, own_ref, other_ref, out_ref):
+    parity = lax.bitwise_and(me_ref[0], 1)
+    out_ref[parity] = own_ref[...]
+    out_ref[1 - parity] = other_ref[...]
+
+
+def join_pair(me, pieces, j, dones):
+    piece = pieces[j]
+    rows, width = piece.shape
+    if j > 1 and j == len(pieces) - 1:
+        piece = after(piece, dones[j - 2])
+    other = hop(piece, COL, 1)
+    if j > 0:
+        other = after(other, dones[j - 1])
+    vmem = pl.BlockSpec(memory_space=pltpu.VMEM)
+    both = pl.pallas_call(
+        join_body,
+        out_shape=jax.ShapeDtypeStruct((2, rows, width), piece.dtype),
+        in_specs=[pl.BlockSpec(memory_space=pltpu.SMEM), vmem, vmem],
+        out_specs=vmem,
+        cost_estimate=pl.CostEstimate(flops=0, transcendentals=0, bytes_accessed=8 * rows * width),
+    )(me, piece, other)
+    return both.reshape(2 * rows, width)
 
 
 def block_of(ref, index, width):
@@ -774,34 +800,33 @@
     )
     layer_own = jnp.concatenate([per_layer_gate, per_layer_projection], axis=1)
     feed_all = jnp.concatenate(feed_pieces, axis=0)
-    halves = 2
-    part_rows = rows // halves
-    feed_tokens, hidden_pulls, hidden_lows, down_outs = [], [], [], []
-    done = None
-    for h in range(halves):
-        tokens = lax.all_gather(
-            feed_low[h * part_rows : (h + 1) * part_rows], COL, axis=0, tiled=True
-        )
-        tokens = tokens if done is None else after(tokens, done)
+    down_pieces = xor_gather(down_weight, ROW, row_total, feed_low)
+    down_all = jnp.concatenate(down_pieces, axis=0)
+    feed_pieces = xor_gather(feed_low, COL, pairs)
+    feed_pairs, dones = [], []
+    chip = me_col // 2
+    hidden_pulls, hidden_lows = [], []
+    down_part = jnp.zeros((2 * pairs * rows, width), low)
+    for j in range(pairs):
+        tokens = join_pair(me, feed_pieces, j, dones)
+        feed_pairs.append(tokens)
         gate_up = product(tokens, feed_all).astype(low)
-        if h == 0:
-            down_pieces = xor_gather(down_weight, ROW, row_total, feed_low)
-            down_all = jnp.concatenate(down_pieces, axis=0)
         hidden, hidden_pull = jax.vjp(
             geglu, gate_up[:, :feed_width].astype(wide), gate_up[:, feed_width:].astype(wide)
         )
         hidden_low = hidden.astype(low)
         done = product_t(hidden_low, down_all).astype(low)
-        down_outs.append(lax.psum_scatter(done, COL, scatter_dimension=0, tiled=True))
-        feed_tokens.append(tokens)
+        place = (lax.bitwise_xor(chip, j) * (2 * rows), 0)
+        down_part = lax.dynamic_update_slice(down_part, done, place)
+        dones.append(done)
         hidden_pulls.append(hidden_pull)
         hidden_lows.append(hidden_low)
+    down_out = lax.psum_scatter(down_part, COL, scatter_dimension=0, tiled=True).astype(wide)
     layer_group = over_col(me, after(layer_own, done), pairs)
     layer_pieces = direct_gather(layer_group, ROW, row_total)
     layer_all = jnp.concatenate([one.reshape(-1, 2 * embed) for one in layer_pieces], axis=0)
     layer_gate_all = layer_all[:, :embed]
     layer_proj_all = layer_all[:, embed:]
-    down_out = jnp.concatenate(down_outs, axis=0).astype(wide)
     after_feed, feed_pull = jax.vjp(feed_mix, mixed, down_out, gain_list[4])
     after_low = after_feed.astype(low)
     per_pre = product(after_low, layer_gate_all)
@@ -827,36 +852,41 @@
     )
     attended_pair = pair_columns(me, after(attended, down_low), col_total)
     normed_pair = pair_rows(after(normed_low, down_low))
-    feed_in_grads = []
-    done = None
-    for h in range(halves):
-        tokens = lax.all_gather(
-            down_low[h * part_rows : (h + 1) * part_rows], COL, axis=0, tiled=True
-        )
-        if done is None:
+    down_pieces = [down_low]
+    down_pairs, dones = [], []
+    feed_in_part = jnp.zeros((2 * pairs * rows, width), low)
+    feed_grads = []
+    for j in range(pairs):
+        if j == 1:
+            down_pieces = xor_gather(down_low, COL, pairs, dones[0])
+        tokens = join_pair(me, down_pieces, j, dones)
+        if j == pairs - 1:
             tokens, layer_grad, attended_pair, normed_pair = lax.optimization_barrier(
                 (tokens, layer_grad, attended_pair, normed_pair)
             )
-        else:
-            tokens = after(tokens, done, down_first, *feed_first)
+        down_pairs.append(tokens)
         hidden_grad = product(tokens, down_all)
-        gate_grad, up_grad = hidden_pulls[h](hidden_grad)
-        feed_grad_low = jnp.concatenate([gate_grad.astype(low), up_grad.astype(low)], axis=1)
+        gate_grad, up_grad = [one.astype(low) for one in hidden_pulls[j](hidden_grad)]
+        feed_grad_low = jnp.concatenate([gate_grad, up_grad], axis=1)
         done = product_t(feed_grad_low, feed_all).astype(low)
-        feed_in_grads.append(lax.psum_scatter(done, COL, scatter_dimension=0, tiled=True))
-        if h == 0:
-            down_first = product_tn(after(tokens, done), hidden_lows[0]).astype(low)
-            feed_first = [
-                product_tn(after(feed_tokens[0], down_first), one.astype(low)).astype(low)
-                for one in (gate_grad, up_grad)
-            ]
-    feed_in_grad = jnp.concatenate(feed_in_grads, axis=0).astype(wide)
-    down_total = product_tn(after(tokens, done), hidden_lows[1]) + down_first.astype(wide)
-    down_total = down_total.astype(low)
-    gate_total = product_tn(after(feed_tokens[1], down_total), gate_grad.astype(low))
-    gate_total = (gate_total + feed_first[0].astype(wide)).astype(low)
-    up_total = product_tn(after(feed_tokens[1], gate_total), up_grad.astype(low))
-    up_total = (up_total + feed_first[1].astype(wide)).astype(low)
+        place = (lax.bitwise_xor(chip, j) * (2 * rows), 0)
+        feed_in_part = lax.dynamic_update_slice(feed_in_part, done, place)
+        dones.append(done)
+        feed_grads.append((gate_grad, up_grad))
+    feed_in_grad = lax.psum_scatter(
+        feed_in_part, COL, scatter_dimension=0, tiled=True
+    ).astype(wide)
+
+    def over_chips(lefts, rights, marker):
+        total = None
+        for j in range(pairs):
+            part = product_tn(after(lefts[j], marker), rights[j])
+            total = (part if total is None else part + total.astype(wide)).astype(low)
+        return total
+
+    down_total = over_chips(down_pairs, hidden_lows, done)
+    gate_total = over_chips(feed_pairs, [one[0] for one in feed_grads], down_total)
+    up_total = over_chips(feed_pairs, [one[1] for one in feed_grads], gate_total)
     (
         inputs_grad,
         attention_grad,

time: 1100 us -> 1120 us (1.018)
  waiting for transfers between devices: 503 us -> 397 us
  matrix products: 157 us -> 214 us
  Pallas kernels: 96.7 us -> 121 us
  starting transfers between devices: 140 us -> 162 us
  other arithmetic: 119 us -> 132 us
    reduce_scatter x4 -> x2, waiting for transfers between devices: 151 us -> 79.7 us  [the longest x1 42.7 us: local(): lax.psum_scatter(down_part, COL, scatter_dimension=0, tiled=True)]
    ppermute x37 -> x39, waiting for transfers between devices: 111 us -> 81.8 us  [split_hop(): return lax.ppermute(values, (ROW, COL), pairs)]
    dot_general x13 -> x19, matrix products: 59.6 us -> 87.2 us  [product_tn(): lax.dot_general(left, right, (((0,), (0,)), ((), ())), preferred_element_...]
    pallas_call x1 -> x9, Pallas kernels: 3.81 us -> 27.7 us  [the longest x8 23.9 us: join_pair(): pl.pallas_call(join_body, out_shape=jax.ShapeDtypeStruct((2, rows, width)...]
    ppermute x51 -> x63, starting transfers between devices: 75.9 us -> 98.4 us  [hop(): return lax.ppermute(values, axis, [(i, i ^ mask) for i in range(size)])]
    dot_general x8 -> x12, matrix products: 46.3 us -> 61.3 us  [product_t(): lax.dot_general(left, right, (((1,), (1,)), ((), ())), preferred_element_...]
    dot_general x8 -> x12, matrix products: 51.4 us -> 65.8 us  [product(): return jnp.dot(left, right, preferred_element_type=jnp.float32)]
    ppermute x51 -> x63, waiting for transfers between devices: 234 us -> 232 us  [hop(): return lax.ppermute(values, axis, [(i, i ^ mask) for i in range(size)])]
  transfers between devices with their start and end apart: 100 -> 108, of which waited for: 48 -> 41; matrix products, arithmetic and copies ran while one was open for 22% -> 30% of each run, Pallas kernels for 6% -> 7%
where the time goes in v3:
time: 1120 us; the launch traced here: 1110 us
  waiting for transfers between devices  397 us (35%)
  matrix products  214 us (19%)
  starting transfers between devices  162 us (14%)
  other arithmetic  132 us (12%)
  Pallas kernels  121 us (11%)
  local copies, waits for them, and re-layouts  66.7 us (6%)
  between operations  19.4 us (2%)
    ppermute x63, waiting for transfers between devices, hop(): return lax.ppermute(values, axis, [(i, i ^ mask) for i in range(size)])  232 us
    ppermute x63, starting transfers between devices, hop(): return lax.ppermute(values, axis, [(i, i ^ mask) for i in range(size)])  98.4 us
    dot_general x19, matrix products, product_tn(): lax.dot_general(left, right, (((0,), (0,)), ((), ())), preferred_element_...  87.2 us
    ppermute x39, waiting for transfers between devices, split_hop(): return lax.ppermute(values, (ROW, COL), pairs)  81.8 us
    dot_general x12, matrix products, product(): return jnp.dot(left, right, preferred_element_type=jnp.float32)  65.8 us
    dot_general x12, matrix products, product_t(): lax.dot_general(left, right, (((1,), (1,)), ((), ())), preferred_element_...  61.3 us
    ppermute x39, starting transfers between devices, split_hop(): return lax.ppermute(values, (ROW, COL), pairs)  53.9 us
    reduce_scatter x1, waiting for transfers between devices, local(): lax.psum_scatter(down_part, COL, scatter_dimension=0, tiled=True)  42.7 us
  transfers between devices with their start and end apart: 108, of which 41 were waited for; matrix products, arithmetic and copies ran while one was open for 30% of the time, Pallas kernels for 7%

profile of v3, /device:TPU:0, one launch (start us, length us, event | category | flops | bytes accessed | tf_op | source)
XLA Modules:
  0.0 1112.6 jit_solution(13012203896190096260)
XLA Ops:
  44.5 10.9 collective-permute-done.1
  82.7 14.1 %collective-permute-done.4.refs_1_ = bf16[512,256]{1,0:T(8,128)(2,1)S(1)} collective-permute-done((bf16[512,256]{1,0:T(8,128)(2,1)S(1)}, bf16[512,256]{1,0:T(8,128)(2,1)S(1)}, u32[]{:S(2)}, u32[]{:S(2)}) %collective-permute-start.4) | collective-permute-done | bytes 262176 | tf_op jit(solution)/shard_map/ppermute | solution.py:193
  96.8 9.5 collective-permute-done.5.refs_2_
  114.7 20.9 %collective-permute-done.10.refs_1_ = bf16[4,512,256]{2,1,0:T(8,128)(2,1)S(1)} collective-permute-done((bf16[4,512,256]{2,1,0:T(8,128)(2,1)}, bf16[4,512,256]{2,1,0:T(8,128)(2,1)S(1)}, u32[]{:S(2)}, u32[]{:S(2)}) %collective-permute-start.10) | collective-permute-done | bytes 1048608 | tf_op jit(solution)/shard_map/ppermute | solution.py:193
  137.3 15.8 %collective-permute-start.23 = (bf16[512,256]{1,0:T(8,128)(2,1)S(1)}, bf16[512,256]{1,0:T(8,128)(2,1)S(1)}, u32[]{:S(2)}, u32[]{:S(2)}) collective-permute-start(bf16[512,256]{1,0:T(8,128)(2,1)S(1)} %copy-done.85), channel_id=1, source_target_pairs={{0,2},{1,3},{2,0},{3,1},{4,6},{5,7},{6,4},{7,5},{8,10},{9,11},{10,... | collective-permute-start | bytes 786440 | tf_op jit(solution)/shard_map/ppermute | solution.py:193
  153.3 10.2 collective-permute-done.23.refs_1_
  168.8 8.8 collective-permute-done.25.refs_3_
  187.1 7.1 shard_map.392.query_ref
  197.1 10.0 shard_map.396
  213.0 10.7 collective-permute-done.28.refs_3_
  234.3 7.4 shard_map.398
  248.5 9.0 collective-permute-start.40
  257.5 19.4 %collective-permute-done.34 = bf16[512,2048]{1,0:T(8,128)(2,1)} collective-permute-done((bf16[512,2048]{1,0:T(8,128)(2,1)}, bf16[512,2048]{1,0:T(8,128)(2,1)}, u32[]{:S(2)}, u32[]{:S(2)}) %collective-permute-start.34) | collective-permute-done | bytes 2097184 | tf_op jit(solution)/shard_map/ppermute | solution.py:193
  276.9 14.0 %collective-permute-start.42 = (bf16[256,2048]{1,0:T(8,128)(2,1)}, bf16[256,2048]{1,0:T(8,128)(2,1)S(1)}, u32[]{:S(2)}, u32[]{:S(2)}) collective-permute-start(bf16[256,2048]{1,0:T(8,128)(2,1)} %multiply_convert_fusion.4.own_ref), channel_id=1, source_target_pairs={{0,4},{1,5},{2,6},{3,7},{4,0},{5,1},{6,2},{7,3},{8,12},{9,13},{10,... | collective-permute-start | bytes 3145736 | tf_op jit(solution)/shard_map/ppermute | solution.py:193
  310.7 22.4 %collective-permute-done.42.own_ref = bf16[256,2048]{1,0:T(8,128)(2,1)S(1)} collective-permute-done((bf16[256,2048]{1,0:T(8,128)(2,1)}, bf16[256,2048]{1,0:T(8,128)(2,1)S(1)}, u32[]{:S(2)}, u32[]{:S(2)}) %collective-permute-start.42) | collective-permute-done | bytes 1048608 | tf_op jit(solution)/shard_map/ppermute | solution.py:193
  351.3 8.6 convolution_convert_fusion.14
  372.2 8.7 convolution_convert_fusion.13
  388.0 8.7 convolution_convert_fusion.12
  403.9 8.7 convolution_convert_fusion.11
  447.5 10.2 collective-permute-done.50
  457.7 10.4 collective-permute-done.51
  471.1 42.7 %reduce-scatter.4.cloned.1.call-done = bf16[256,2048]{1,0:T(8,128)(2,1)} async-done(((bf16[2048,2048]{1,0:T(8,128)(2,1)}), bf16[256,2048]{1,0:T(8,128)(2,1)}) %reduce-scatter.4.cloned.1.call-update) | async-done | bytes 1048592 | tf_op jit(solution)/shard_map/reduce_scatter | solution.py:824
  553.5 7.1 fusion.36
  566.6 9.5 constant_dynamic-update-slice_fusion.11
  576.1 13.0 %collective-permute-done.54.own_ref = bf16[256,2048]{1,0:T(8,128)(2,1)} collective-permute-done((bf16[256,2048]{1,0:T(8,128)(2,1)}, bf16[256,2048]{1,0:T(8,128)(2,1)}, u32[]{:S(2)}, u32[]{:S(2)}) %collective-permute-start.54) | collective-permute-done | bytes 1048608 | tf_op jit(solution)/shard_map/ppermute | solution.py:193
  604.0 17.7 %collective-permute-done.64 = bf16[64,512]{1,0:T(8,128)(2,1)S(1)} collective-permute-done((bf16[64,512]{1,0:T(8,128)(2,1)S(1)}, bf16[64,512]{1,0:T(8,128)(2,1)S(1)}, u32[]{:S(2)}, u32[]{:S(2)}) %collective-permute-start.64) | collective-permute-done | bytes 65568 | tf_op jit(solution)/shard_map/ppermute | solution.py:199
  624.7 7.1 fusion.33
  631.9 10.1 constant_dynamic-update-slice_fusion.10
  647.0 7.1 fusion.30
  654.1 10.1 constant_dynamic-update-slice_fusion.9
  668.2 7.1 fusion.27
  676.3 9.2 constant_dynamic-update-slice_fusion.8
  694.1 5.9 fusion.134
  704.5 11.3 %add_convert_fusion.6 = bf16[2048,1024]{1,0:T(8,128)(2,1)} fusion(f32[2048,1024]{1,0:T(8,128)} %fusion.134, f32[2048,1024]{1,0:T(8,128)S(1)} %fusion.137, bf16[2048,1024]{1,0:T(8,128)(2,1)} %fusion.142, bf16[512,2048]{1,0:T(8,128)(2,1)S(1)} %bitcast.129, bf16[512,2048]{1,0:T(8,128)(2,1)} %copy-done.75), kind=kOutput, calls=%fused_computation.6 | convolution fusion | flops 2172649472 | bytes 29360128 | tf_op jit(solution)/shard_map/dot_general | solution.py:186
  728.4 9.2 add_convert_fusion.3
  737.6 37.0 %reduce-scatter.6.cloned.1.call-done = bf16[256,2048]{1,0:T(8,128)(2,1)} async-done(((bf16[2048,2048]{1,0:T(8,128)(2,1)}), bf16[256,2048]{1,0:T(8,128)(2,1)}) %reduce-scatter.6.cloned.1.call-update) | async-done | bytes 1048592 | tf_op jit(solution)/shard_map/reduce_scatter | solution.py:876
  784.1 7.1 shard_map.411.grad_ref
  791.2 13.5 %shard_map.412 = (f32[256,2048]{1,0:T(8,128)}, bf16[8,2,256,512]{3,2,1,0:T(8,128)(2,1)}) custom-call(s32[2]{0:T(128)} %pad_add_fusion.1.span_ref, s32[2,256]{1,0:T(2,128)} %get-tuple-element.302.window_ref, bf16[256,2048]{1,0:T(8,128)(2,1)} %shard_map.393.query_ref, bf16[8,2,256,512]{3,2,1,0:T(8,128)(2,1)} %bitcast.169, bf16[8,2,256,512]{3,2,1,0:T(8,128)(2,1)} %bitcast.170, ...), custom_call_target="tpu_custom_call" | custom-call | flops 10737418240 | bytes 8388608 | tf_op jit(solution)/shard_map/pallas_call | solution.py:627
  825.5 9.6 add_convert_fusion
  880.7 7.4 shard_map.415
  892.6 7.3 collective-permute-done.85
  918.9 6.0 shard_map.418
  932.2 15.1 %collective-permute-start.88 = (bf16[512,256]{1,0:T(8,128)(2,1)S(1)}, bf16[512,256]{1,0:T(8,128)(2,1)S(1)}, u32[]{:S(2)}, u32[]{:S(2)}) collective-permute-start(bf16[512,256]{1,0:T(8,128)(2,1)S(1)} %get-tuple-element.248), channel_id=1, source_target_pairs={{0,4},{1,3},{2,6},{3,1},{4,0},{5,7},{6,2},{7,5},{8,12},{9,11},{10,... | collective-permute-start | bytes 786440 | tf_op jit(solution)/shard_map/ppermute | solution.py:199
  954.8 7.6 collective-permute-done.87
  979.3 9.3 collective-permute-done.98
  1007.8 49.5 %collective-permute-done.99 = f32[8,68,128]{2,1,0:T(8,128)S(1)} collective-permute-done((f32[8,68,128]{2,1,0:T(8,128)S(1)}, f32[8,68,128]{2,1,0:T(8,128)S(1)}, u32[]{:S(2)}, u32[]{:S(2)}) %collective-permute-start.99) | collective-permute-done | bytes 278560 | tf_op jit(solution)/shard_map/ppermute | solution.py:193
  1086.0 7.2 collective-permute-done.77
  1095.3 8.4 collective-permute-done.76
  (744 shorter events, 495.8 us)
Async XLA Ops:
  9.3 28.0 %collective-permute-start.3 = (bf16[512,128]{1,0:T(8,128)(2,1)S(1)}, bf16[512,128]{1,0:T(8,128)(2,1)S(1)}, u32[]{:S(2)}, u32[]{:S(2)}) collective-permute-start(bf16[512,128]{1,0:T(8,128)(2,1)S(1)} %pad_maximum_fusion.15.refs_0_), channel_id=1, source_target_pairs={{0,6},{1,7},{2,4},{3,5},{4,2},{5,3},{6,0},{7,1},{8,14},{9,15},{10,... | collective-permute-start | bytes 393224 | tf_op jit(solution)/shard_map/ppermute | solution.py:193
  27.1 170.0 %all-gather.2.cloned.1.call-start = ((), (), s32[]{:S(2)}) async-start(), calls=%async_computation.5 | async-start | bytes 4718592 | tf_op jit(solution)/shard_map/all_gather | solution.py:769
  78.2 435.6 %reduce-scatter.4.cloned.1.call-start = ((), (), s32[]{:S(2)}) async-start(), calls=%async_computation.6 | async-start | bytes 9437184 | tf_op jit(solution)/shard_map/reduce_scatter | solution.py:824
  79.4 26.9 %collective-permute-start.5 = (bf16[512,256]{1,0:T(8,128)(2,1)S(1)}, bf16[512,256]{1,0:T(8,128)(2,1)S(1)}, u32[]{:S(2)}, u32[]{:S(2)}) collective-permute-start(bf16[512,256]{1,0:T(8,128)(2,1)S(1)} %copy-done.84), channel_id=1, source_target_pairs={{0,4},{1,5},{2,6},{3,7},{4,0},{5,1},{6,2},{7,3},{8,12},{9,13},{10,... | collective-permute-start | bytes 786440 | tf_op jit(solution)/shard_map/ppermute | solution.py:193
  81.1 27.3 %collective-permute-start.6 = (bf16[512,256]{1,0:T(8,128)(2,1)S(1)}, bf16[512,256]{1,0:T(8,128)(2,1)S(1)}, u32[]{:S(2)}, u32[]{:S(2)}) collective-permute-start(bf16[512,256]{1,0:T(8,128)(2,1)S(1)} %copy-done.84), channel_id=1, source_target_pairs={{0,6},{1,7},{2,4},{3,5},{4,2},{5,3},{6,0},{7,1},{8,14},{9,15},{10,... | collective-permute-start | bytes 786440 | tf_op jit(solution)/shard_map/ppermute | solution.py:193
  136.3 27.2 %collective-permute-start.12 = (bf16[4,512,256]{2,1,0:T(8,128)(2,1)S(1)}, bf16[4,512,256]{2,1,0:T(8,128)(2,1)}, u32[]{:S(2)}, u32[]{:S(2)}) collective-permute-start(bf16[4,512,256]{2,1,0:T(8,128)(2,1)S(1)} %broadcast_select_fusion.10), channel_id=1, source_target_pairs={{0,16},{1,9},{2,18},{3,11},{4,20},{5,13},{6,22},{7,15},{8,24},{9,1... | collective-permute-start | bytes 3145736 | tf_op jit(solution)/shard_map/ppermute | solution.py:199
  137.3 43.0 %collective-permute-start.13 = (bf16[4,512,256]{2,1,0:T(8,128)(2,1)S(1)}, bf16[4,512,256]{2,1,0:T(8,128)(2,1)}, u32[]{:S(2)}, u32[]{:S(2)}) collective-permute-start(bf16[4,512,256]{2,1,0:T(8,128)(2,1)S(1)} %copy-done.16), channel_id=1, source_target_pairs={{0,1},{1,0},{2,3},{3,2},{4,5},{5,4},{6,7},{7,6},{8,9},{9,8},{10,11... | collective-permute-start | bytes 3145736 | tf_op jit(solution)/shard_map/ppermute | solution.py:193
  137.3 26.2 %collective-permute-start.23 = (bf16[512,256]{1,0:T(8,128)(2,1)S(1)}, bf16[512,256]{1,0:T(8,128)(2,1)S(1)}, u32[]{:S(2)}, u32[]{:S(2)}) collective-permute-start(bf16[512,256]{1,0:T(8,128)(2,1)S(1)} %copy-done.85), channel_id=1, source_target_pairs={{0,2},{1,3},{2,0},{3,1},{4,6},{5,7},{6,4},{7,5},{8,10},{9,11},{10,... | collective-permute-start | bytes 786440 | tf_op jit(solution)/shard_map/ppermute | solution.py:193
  153.1 34.0 %collective-permute-start.14 = (bf16[4,512,256]{2,1,0:T(8,128)(2,1)S(1)}, bf16[4,512,256]{2,1,0:T(8,128)(2,1)}, u32[]{:S(2)}, u32[]{:S(2)}) collective-permute-start(bf16[4,512,256]{2,1,0:T(8,128)(2,1)S(1)} %collective-permute-done.10.refs_1_), channel_id=1, source_target_pairs={{0,1},{1,0},{2,3},{3,2},{4,5},{5,4},{6,7},{7,6},{8,9},{9,8},{10,11... | collective-permute-start | bytes 3145736 | tf_op jit(solution)/shard_map/ppermute | solution.py:193
  179.8 27.3 %collective-permute-start.26 = (bf16[4,512,256]{2,1,0:T(8,128)(2,1)}, bf16[4,512,256]{2,1,0:T(8,128)(2,1)}, u32[]{:S(2)}, u32[]{:S(2)}) collective-permute-start(bf16[4,512,256]{2,1,0:T(8,128)(2,1)} %shard_map.397.refs_0_), channel_id=1, source_target_pairs={{0,8},{8,0},{16,24},{24,16},{1,9},{9,1},{17,25},{25,17},{2,10},{10... | collective-permute-start | bytes 3145736 | tf_op jit(solution)/shard_map/ppermute | solution.py:193
  180.3 26.9 %collective-permute-start.27 = (bf16[4,512,256]{2,1,0:T(8,128)(2,1)}, bf16[4,512,256]{2,1,0:T(8,128)(2,1)}, u32[]{:S(2)}, u32[]{:S(2)}) collective-permute-start(bf16[4,512,256]{2,1,0:T(8,128)(2,1)} %shard_map.397.refs_0_), channel_id=1, source_target_pairs={{0,16},{8,24},{16,0},{24,8},{1,17},{9,25},{17,1},{25,9},{2,18},{10... | collective-permute-start | bytes 3145736 | tf_op jit(solution)/shard_map/ppermute | solution.py:193
  228.0 48.9 %collective-permute-start.34 = (bf16[512,2048]{1,0:T(8,128)(2,1)}, bf16[512,2048]{1,0:T(8,128)(2,1)}, u32[]{:S(2)}, u32[]{:S(2)}) collective-permute-start(bf16[512,2048]{1,0:T(8,128)(2,1)} %pad_maximum_fusion), channel_id=1, source_target_pairs={{0,8},{8,0},{16,24},{24,16},{1,9},{9,1},{17,25},{25,17},{2,10},{10... | collective-permute-start | bytes 6291464 | tf_op jit(solution)/shard_map/ppermute | solution.py:193
  229.8 61.1 %collective-permute-start.35 = (bf16[512,2048]{1,0:T(8,128)(2,1)}, bf16[512,2048]{1,0:T(8,128)(2,1)}, u32[]{:S(2)}, u32[]{:S(2)}) collective-permute-start(bf16[512,2048]{1,0:T(8,128)(2,1)} %pad_maximum_fusion), channel_id=1, source_target_pairs={{0,16},{8,24},{16,0},{24,8},{1,17},{9,25},{17,1},{25,9},{2,18},{10... | collective-permute-start | bytes 6291464 | tf_op jit(solution)/shard_map/ppermute | solution.py:193
  232.3 67.1 %collective-permute-start.37 = (bf16[512,1024]{1,0:T(8,128)(2,1)}, bf16[512,1024]{1,0:T(8,128)(2,1)}, u32[]{:S(2)}, u32[]{:S(2)}) collective-permute-start(bf16[512,1024]{1,0:T(8,128)(2,1)} %param.33), channel_id=1, source_target_pairs={{0,8},{8,0},{16,24},{24,16},{1,9},{9,1},{17,25},{25,17},{2,10},{10... | collective-permute-start | bytes 3145736 | tf_op jit(solution)/shard_map/ppermute | solution.py:193
  232.7 67.1 %collective-permute-start.38 = (bf16[512,1024]{1,0:T(8,128)(2,1)}, bf16[512,1024]{1,0:T(8,128)(2,1)}, u32[]{:S(2)}, u32[]{:S(2)}) collective-permute-start(bf16[512,1024]{1,0:T(8,128)(2,1)} %param.33), channel_id=1, source_target_pairs={{0,16},{8,24},{16,0},{24,8},{1,17},{9,25},{17,1},{25,9},{2,18},{10... | collective-permute-start | bytes 3145736 | tf_op jit(solution)/shard_map/ppermute | solution.py:193
  248.5 62.2 %collective-permute-start.40 = (bf16[256,2048]{1,0:T(8,128)(2,1)}, bf16[256,2048]{1,0:T(8,128)(2,1)}, u32[]{:S(2)}, u32[]{:S(2)}) collective-permute-start(bf16[256,2048]{1,0:T(8,128)(2,1)} %multiply_convert_fusion.4.own_ref), channel_id=1, source_target_pairs={{0,2},{1,3},{2,0},{3,1},{4,6},{5,7},{6,4},{7,5},{8,10},{9,11},{10,... | collective-permute-start | bytes 3145736 | tf_op jit(solution)/shard_map/ppermute | solution.py:193
  276.9 56.2 %collective-permute-start.42 = (bf16[256,2048]{1,0:T(8,128)(2,1)}, bf16[256,2048]{1,0:T(8,128)(2,1)S(1)}, u32[]{:S(2)}, u32[]{:S(2)}) collective-permute-start(bf16[256,2048]{1,0:T(8,128)(2,1)} %multiply_convert_fusion.4.own_ref), channel_id=1, source_target_pairs={{0,4},{1,5},{2,6},{3,7},{4,0},{5,1},{6,2},{7,3},{8,12},{9,13},{10,... | collective-permute-start | bytes 3145736 | tf_op jit(solution)/shard_map/ppermute | solution.py:193
  294.0 54.0 %collective-permute-start.36 = (bf16[512,2048]{1,0:T(8,128)(2,1)}, bf16[512,2048]{1,0:T(8,128)(2,1)}, u32[]{:S(2)}, u32[]{:S(2)}) collective-permute-start(bf16[512,2048]{1,0:T(8,128)(2,1)} %broadcast_select_fusion), channel_id=1, source_target_pairs={{0,16},{1,9},{2,18},{3,11},{4,20},{5,13},{6,22},{7,15},{8,24},{9,1... | collective-permute-start | bytes 6291464 | tf_op jit(solution)/shard_map/ppermute | solution.py:199
  299.4 36.5 %collective-permute-start.33 = (bf16[256,2048]{1,0:T(8,128)(2,1)}, bf16[256,2048]{1,0:T(8,128)(2,1)}, u32[]{:S(2)}, u32[]{:S(2)}) collective-permute-start(bf16[256,2048]{1,0:T(8,128)(2,1)} %multiply_convert_fusion.4.own_ref), channel_id=1, source_target_pairs={{0,1},{1,0},{2,3},{3,2},{4,5},{5,4},{6,7},{7,6},{8,9},{9,8},{10,11... | collective-permute-start | bytes 3145736 | tf_op jit(solution)/shard_map/ppermute | solution.py:193
  302.2 37.2 %collective-permute-start.39 = (bf16[512,1024]{1,0:T(8,128)(2,1)}, bf16[512,1024]{1,0:T(8,128)(2,1)}, u32[]{:S(2)}, u32[]{:S(2)}) collective-permute-start(bf16[512,1024]{1,0:T(8,128)(2,1)} %broadcast_select_fusion.8), channel_id=1, source_target_pairs={{0,16},{1,9},{2,18},{3,11},{4,20},{5,13},{6,22},{7,15},{8,24},{9,1... | collective-permute-start | bytes 3145736 | tf_op jit(solution)/shard_map/ppermute | solution.py:199
  335.8 49.1 %collective-permute-start.44 = (bf16[256,2048]{1,0:T(8,128)(2,1)}, bf16[256,2048]{1,0:T(8,128)(2,1)}, u32[]{:S(2)}, u32[]{:S(2)}) collective-permute-start(bf16[256,2048]{1,0:T(8,128)(2,1)} %broadcast_select_fusion.2), channel_id=1, source_target_pairs={{0,4},{1,3},{2,6},{3,1},{4,0},{5,7},{6,2},{7,5},{8,12},{9,11},{10,... | collective-permute-start | bytes 3145736 | tf_op jit(solution)/shard_map/ppermute | solution.py:199
  335.8 33.4 %collective-permute-start.41 = (bf16[256,2048]{1,0:T(8,128)(2,1)}, bf16[256,2048]{1,0:T(8,128)(2,1)}, u32[]{:S(2)}, u32[]{:S(2)}) collective-permute-start(bf16[256,2048]{1,0:T(8,128)(2,1)} %collective-permute-done.40.own_ref), channel_id=1, source_target_pairs={{0,1},{1,0},{2,3},{3,2},{4,5},{5,4},{6,7},{7,6},{8,9},{9,8},{10,11... | collective-permute-start | bytes 3145736 | tf_op jit(solution)/shard_map/ppermute | solution.py:193
  335.8 49.1 %collective-permute-start.43 = (bf16[256,2048]{1,0:T(8,128)(2,1)S(1)}, bf16[256,2048]{1,0:T(8,128)(2,1)}, u32[]{:S(2)}, u32[]{:S(2)}) collective-permute-start(bf16[256,2048]{1,0:T(8,128)(2,1)S(1)} %collective-permute-done.42.own_ref), channel_id=1, source_target_pairs={{0,1},{1,0},{2,3},{3,2},{4,5},{5,4},{6,7},{7,6},{8,9},{9,8},{10,11... | collective-permute-start | bytes 3145736 | tf_op jit(solution)/shard_map/ppermute | solution.py:193
  418.0 356.6 %reduce-scatter.6.cloned.1.call-start = ((), (), s32[]{:S(2)}) async-start(), calls=%async_computation.7 | async-start | bytes 9437184 | tf_op jit(solution)/shard_map/reduce_scatter | solution.py:876
  540.7 48.4 %collective-permute-start.54 = (bf16[256,2048]{1,0:T(8,128)(2,1)}, bf16[256,2048]{1,0:T(8,128)(2,1)}, u32[]{:S(2)}, u32[]{:S(2)}) collective-permute-start(bf16[256,2048]{1,0:T(8,128)(2,1)} %fusion.39.own_ref), channel_id=1, source_target_pairs={{0,2},{1,3},{2,0},{3,1},{4,6},{5,7},{6,4},{7,5},{8,10},{9,11},{10,... | collective-permute-start | bytes 3145736 | tf_op jit(solution)/shard_map/ppermute | solution.py:193
  542.3 46.8 %collective-permute-start.56 = (bf16[256,2048]{1,0:T(8,128)(2,1)}, bf16[256,2048]{1,0:T(8,128)(2,1)}, u32[]{:S(2)}, u32[]{:S(2)}) collective-permute-start(bf16[256,2048]{1,0:T(8,128)(2,1)} %fusion.39.own_ref), channel_id=1, source_target_pairs={{0,4},{1,5},{2,6},{3,7},{4,0},{5,1},{6,2},{7,3},{8,12},{9,13},{10,... | collective-permute-start | bytes 3145736 | tf_op jit(solution)/shard_map/ppermute | solution.py:193
  543.7 54.8 %collective-permute-start.68 = (bf16[256,2048]{1,0:T(8,128)(2,1)S(1)}, bf16[256,2048]{1,0:T(8,128)(2,1)}, u32[]{:S(2)}, u32[]{:S(2)}) collective-permute-start(bf16[256,2048]{1,0:T(8,128)(2,1)S(1)} %copy-done.13), channel_id=1, source_target_pairs={{0,1},{1,0},{2,3},{3,2},{4,5},{5,4},{6,7},{7,6},{8,9},{9,8},{10,11... | collective-permute-start | bytes 3145736 | tf_op jit(solution)/shard_map/ppermute | solution.py:193
  548.8 40.3 %collective-permute-start.61 = (bf16[256,512]{1,0:T(8,128)(2,1)}, bf16[256,512]{1,0:T(8,128)(2,1)}, u32[]{:S(2)}, u32[]{:S(2)}) collective-permute-start(bf16[256,512]{1,0:T(8,128)(2,1)} %bitcast.34), channel_id=1, source_target_pairs={{0,16},{1,9},{2,18},{3,11},{4,20},{5,13},{6,22},{7,15},{8,24},{9,1... | collective-permute-start | bytes 786440 | tf_op jit(solution)/shard_map/ppermute | solution.py:199
  561.8 27.2 %collective-permute-start.63 = (bf16[256,512]{1,0:T(8,128)(2,1)S(1)}, bf16[256,512]{1,0:T(8,128)(2,1)S(1)}, u32[]{:S(2)}, u32[]{:S(2)}) collective-permute-start(bf16[256,512]{1,0:T(8,128)(2,1)S(1)} %fusion.96), channel_id=1, source_target_pairs={{0,8},{1,17},{2,10},{3,19},{4,12},{5,21},{6,14},{7,23},{8,0},{9,25... | collective-permute-start | bytes 786440 | tf_op jit(solution)/shard_map/ppermute | solution.py:199
  589.1 32.7 %collective-permute-start.55 = (bf16[256,2048]{1,0:T(8,128)(2,1)}, bf16[256,2048]{1,0:T(8,128)(2,1)}, u32[]{:S(2)}, u32[]{:S(2)}) collective-permute-start(bf16[256,2048]{1,0:T(8,128)(2,1)} %collective-permute-done.54.own_ref), channel_id=1, source_target_pairs={{0,1},{1,0},{2,3},{3,2},{4,5},{5,4},{6,7},{7,6},{8,9},{9,8},{10,11... | collective-permute-start | bytes 3145736 | tf_op jit(solution)/shard_map/ppermute | solution.py:193
  594.7 47.4 %collective-permute-start.58 = (bf16[256,2048]{1,0:T(8,128)(2,1)}, bf16[256,2048]{1,0:T(8,128)(2,1)}, u32[]{:S(2)}, u32[]{:S(2)}) collective-permute-start(bf16[256,2048]{1,0:T(8,128)(2,1)} %broadcast_select_fusion.1), channel_id=1, source_target_pairs={{0,4},{1,3},{2,6},{3,1},{4,0},{5,7},{6,2},{7,5},{8,12},{9,11},{10,... | collective-permute-start | bytes 3145736 | tf_op jit(solution)/shard_map/ppermute | solution.py:199
  595.5 48.5 %collective-permute-start.57 = (bf16[256,2048]{1,0:T(8,128)(2,1)}, bf16[256,2048]{1,0:T(8,128)(2,1)}, u32[]{:S(2)}, u32[]{:S(2)}) collective-permute-start(bf16[256,2048]{1,0:T(8,128)(2,1)} %collective-permute-done.56.own_ref), channel_id=1, source_target_pairs={{0,1},{1,0},{2,3},{3,2},{4,5},{5,4},{6,7},{7,6},{8,9},{9,8},{10,11... | collective-permute-start | bytes 3145736 | tf_op jit(solution)/shard_map/ppermute | solution.py:193
  685.6 219.0 %reduce-scatter.8.cloned.1.call-start = ((), (), s32[]{:S(2)}) async-start(), calls=%async_computation.8 | async-start | bytes 4718592 | tf_op jit(solution)/shard_map/reduce_scatter | solution.py:904
  808.2 38.6 %collective-permute-start.97 = (bf16[512,1024]{1,0:T(8,128)(2,1)}, bf16[512,1024]{1,0:T(8,128)(2,1)}, u32[]{:S(2)}, u32[]{:S(2)}) collective-permute-start(bf16[512,1024]{1,0:T(8,128)(2,1)} %get-tuple-element.221), channel_id=1, source_target_pairs={{0,16},{1,9},{2,18},{3,11},{4,20},{5,13},{6,22},{7,15},{8,24},{9,1... | collective-permute-start | bytes 3145736 | tf_op jit(solution)/shard_map/ppermute | solution.py:199
  811.2 35.6 %collective-permute-start.91 = (bf16[512,1024]{1,0:T(8,128)(2,1)}, bf16[512,1024]{1,0:T(8,128)(2,1)}, u32[]{:S(2)}, u32[]{:S(2)}) collective-permute-start(bf16[512,1024]{1,0:T(8,128)(2,1)} %get-tuple-element.225), channel_id=1, source_target_pairs={{0,16},{1,9},{2,18},{3,11},{4,20},{5,13},{6,22},{7,15},{8,24},{9,1... | collective-permute-start | bytes 3145736 | tf_op jit(solution)/shard_map/ppermute | solution.py:199
  846.1 132.0 %collective-permute-start.96 = (bf16[512,1024]{1,0:T(8,128)(2,1)}, bf16[512,1024]{1,0:T(8,128)(2,1)}, u32[]{:S(2)}, u32[]{:S(2)}) collective-permute-start(bf16[512,1024]{1,0:T(8,128)(2,1)} %get-tuple-element.220), channel_id=1, source_target_pairs={{0,16},{1,9},{2,18},{3,11},{4,20},{5,13},{6,22},{7,15},{8,24},{9,1... | collective-permute-start | bytes 3145736 | tf_op jit(solution)/shard_map/ppermute | solution.py:199
  873.6 55.2 %collective-permute-start.84 = (bf16[512,1024]{1,0:T(8,128)(2,1)}, bf16[512,1024]{1,0:T(8,128)(2,1)}, u32[]{:S(2)}, u32[]{:S(2)}) collective-permute-start(bf16[512,1024]{1,0:T(8,128)(2,1)} %get-tuple-element.226), channel_id=1, source_target_pairs={{0,16},{1,9},{2,18},{3,11},{4,20},{5,13},{6,22},{7,15},{8,24},{9,1... | collective-permute-start | bytes 3145736 | tf_op jit(solution)/shard_map/ppermute | solution.py:199
  873.6 26.3 %collective-permute-start.85 = (bf16[512,1024]{1,0:T(8,128)(2,1)}, bf16[512,1024]{1,0:T(8,128)(2,1)}, u32[]{:S(2)}, u32[]{:S(2)}) collective-permute-start(bf16[512,1024]{1,0:T(8,128)(2,1)} %get-tuple-element.227), channel_id=1, source_target_pairs={{0,16},{1,9},{2,18},{3,11},{4,20},{5,13},{6,22},{7,15},{8,24},{9,1... | collective-permute-start | bytes 3145736 | tf_op jit(solution)/shard_map/ppermute | solution.py:199
  914.5 57.9 %collective-permute-start.74 = (bf16[512,1024]{1,0:T(8,128)(2,1)}, bf16[512,1024]{1,0:T(8,128)(2,1)}, u32[]{:S(2)}, u32[]{:S(2)}) collective-permute-start(bf16[512,1024]{1,0:T(8,128)(2,1)} %get-tuple-element.229), channel_id=1, source_target_pairs={{0,16},{1,9},{2,18},{3,11},{4,20},{5,13},{6,22},{7,15},{8,24},{9,1... | collective-permute-start | bytes 3145736 | tf_op jit(solution)/shard_map/ppermute | solution.py:199
  964.9 28.2 %collective-permute-start.73 = (bf16[512,1024]{1,0:T(8,128)(2,1)}, bf16[512,1024]{1,0:T(8,128)(2,1)}, u32[]{:S(2)}, u32[]{:S(2)}) collective-permute-start(bf16[512,1024]{1,0:T(8,128)(2,1)} %get-tuple-element.228), channel_id=1, source_target_pairs={{0,16},{1,9},{2,18},{3,11},{4,20},{5,13},{6,22},{7,15},{8,24},{9,1... | collective-permute-start | bytes 3145736 | tf_op jit(solution)/shard_map/ppermute | solution.py:199
  968.5 26.8 %collective-permute-start.79 = (bf16[512,512]{0,1:T(8,128)(2,1)}, bf16[512,512]{0,1:T(8,128)(2,1)}, u32[]{:S(2)}, u32[]{:S(2)}) collective-permute-start(bf16[512,512]{0,1:T(8,128)(2,1)} %get-tuple-element.240), channel_id=1, source_target_pairs={{0,16},{1,9},{2,18},{3,11},{4,20},{5,13},{6,22},{7,15},{8,24},{9,1... | collective-permute-start | bytes 1572872 | tf_op jit(solution)/shard_map/ppermute | solution.py:199
  972.5 33.1 %collective-permute-start.80 = (bf16[512,512]{0,1:T(8,128)(2,1)}, bf16[512,512]{0,1:T(8,128)(2,1)S(1)}, u32[]{:S(2)}, u32[]{:S(2)}) collective-permute-start(bf16[512,512]{0,1:T(8,128)(2,1)} %add_convert_fusion.19), channel_id=1, source_target_pairs={{0,8},{1,17},{2,10},{3,19},{4,12},{5,21},{6,14},{7,23},{8,0},{9,25... | collective-permute-start | bytes 1572872 | tf_op jit(solution)/shard_map/ppermute | solution.py:199
  993.1 74.6 %collective-permute-start.93 = (bf16[512,1024]{1,0:T(8,128)(2,1)}, bf16[512,1024]{1,0:T(8,128)(2,1)}, u32[]{:S(2)}, u32[]{:S(2)}) collective-permute-start(bf16[512,1024]{1,0:T(8,128)(2,1)} %get-tuple-element.222), channel_id=1, source_target_pairs={{0,16},{1,9},{2,18},{3,11},{4,20},{5,13},{6,22},{7,15},{8,24},{9,1... | collective-permute-start | bytes 3145736 | tf_op jit(solution)/shard_map/ppermute | solution.py:199
  995.3 76.8 %collective-permute-start.90 = (bf16[512,1024]{1,0:T(8,128)(2,1)}, bf16[512,1024]{1,0:T(8,128)(2,1)}, u32[]{:S(2)}, u32[]{:S(2)}) collective-permute-start(bf16[512,1024]{1,0:T(8,128)(2,1)} %get-tuple-element.224), channel_id=1, source_target_pairs={{0,16},{1,9},{2,18},{3,11},{4,20},{5,13},{6,22},{7,15},{8,24},{9,1... | collective-permute-start | bytes 3145736 | tf_op jit(solution)/shard_map/ppermute | solution.py:199
  998.8 73.4 %collective-permute-start.92 = (bf16[512,1024]{1,0:T(8,128)(2,1)S(1)}, bf16[512,1024]{1,0:T(8,128)(2,1)}, u32[]{:S(2)}, u32[]{:S(2)}) collective-permute-start(bf16[512,1024]{1,0:T(8,128)(2,1)S(1)} %copy-done.65), channel_id=1, source_target_pairs={{0,8},{1,17},{2,10},{3,19},{4,12},{5,21},{6,14},{7,23},{8,0},{9,25... | collective-permute-start | bytes 3145736 | tf_op jit(solution)/shard_map/ppermute | solution.py:199
  1004.4 66.3 %collective-permute-start.95 = (bf16[512,1024]{1,0:T(8,128)(2,1)S(1)}, bf16[512,1024]{1,0:T(8,128)(2,1)}, u32[]{:S(2)}, u32[]{:S(2)}) collective-permute-start(bf16[512,1024]{1,0:T(8,128)(2,1)S(1)} %copy-done.66), channel_id=1, source_target_pairs={{0,8},{1,17},{2,10},{3,19},{4,12},{5,21},{6,14},{7,23},{8,0},{9,25... | collective-permute-start | bytes 3145736 | tf_op jit(solution)/shard_map/ppermute | solution.py:199
  1005.6 51.7 %collective-permute-start.99 = (f32[8,68,128]{2,1,0:T(8,128)S(1)}, f32[8,68,128]{2,1,0:T(8,128)S(1)}, u32[]{:S(2)}, u32[]{:S(2)}) collective-permute-start(f32[8,68,128]{2,1,0:T(8,128)S(1)} %get-tuple-element.246), channel_id=1, source_target_pairs={{0,8},{8,0},{16,24},{24,16},{1,9},{9,1},{17,25},{25,17},{2,10},{10... | collective-permute-start | bytes 835592 | tf_op jit(solution)/shard_map/ppermute | solution.py:193
  1064.0 29.4 %all-to-all-start.1 = ((f32[8,68,128]{2,1,0:T(8,128)}), f32[8,68,128]{2,1,0:T(8,128)S(1)}, u32[]{:S(2)}, u32[]{:S(2)}) async-start(f32[8,68,128]{2,1,0:T(8,128)} %bitcast_add_fusion), calls=%async_computation.4 | async-start | bytes 589824 | tf_op jit(solution)/shard_map/all_to_all | solution.py:980
  (228 other events, 3371.5 us)
Sparse Core Ops, SparseCore 0:
  78.3 62.4 all-gather.1
  418.1 95.6 reduce-scatter.3
  685.7 88.8 reduce-scatter.5
  804.8 66.5 reduce-scatter.7

commit v4 on v2

--- a/solution.py
+++ b/solution.py
@@ -919,10 +919,10 @@
     mark = marks[0]
     query_marks = []
     query_weight_grad = scatter_cols(query_total, row_total, pairs, mark, mark, query_marks)
-    out_weight_grad = scatter_cols(out_total, row_total, pairs, query_part, normed_grad)
+    out_weight_grad = scatter_cols(out_total, row_total, pairs, query_part, query_marks[0])
     down_weight_grad = scatter_rows(down_total, row_total, up_total, query_marks[0])
-    gate_weight_grad = scatter_rows(gate_total, row_total, up_total, marks[-1])
-    up_weight_grad = scatter_rows(up_total, row_total, pair_parts, marks[-1])
+    gate_weight_grad = scatter_rows(gate_total, row_total, up_total, query_marks[-1])
+    up_weight_grad = scatter_rows(up_total, row_total, pair_parts, query_marks[-1])
     input_part, input_gain_grad = input_pull(after(normed_grad, mark))
     input_total = xor_blocks((inputs_grad + input_part).astype(low), me_row, row_total)
 

time: 1100 us -> 1070 us (0.973)
  waiting for transfers between devices: 503 us -> 470 us
    ppermute x51, waiting for transfers between devices: 234 us -> 190 us  [hop(): return lax.ppermute(values, axis, [(i, i ^ mask) for i in range(size)])]
    ppermute x37, waiting for transfers between devices: 111 us -> 123 us  [split_hop(): return lax.ppermute(values, (ROW, COL), pairs)]
    unnamed x328 -> x320, local copies, waits for them, and re-layouts: 31.7 us -> 32.7 us
  transfers between devices with their start and end apart: 100 -> 100, of which waited for: 48 -> 44; matrix products, arithmetic and copies ran while one was open for 22% -> 22% of each run, Pallas kernels for 6% -> 6%
where the time goes in v4:
time: 1070 us; the launch traced here: 1060 us
  waiting for transfers between devices  470 us (44%)
  matrix products  153 us (14%)
  starting transfers between devices  147 us (14%)
  other arithmetic  119 us (11%)
  Pallas kernels  96.9 us (9%)
  local copies, waits for them, and re-layouts  57.5 us (5%)
  between operations  19.6 us (2%)
    ppermute x51, waiting for transfers between devices, hop(): return lax.ppermute(values, axis, [(i, i ^ mask) for i in range(size)])  190 us
    reduce_scatter x4, waiting for transfers between devices, local(): lax.psum_scatter(done, COL, scatter_dimension=0, tiled=True)  151 us
    ppermute x37, waiting for transfers between devices, split_hop(): return lax.ppermute(values, (ROW, COL), pairs)  123 us
    ppermute x51, starting transfers between devices, hop(): return lax.ppermute(values, axis, [(i, i ^ mask) for i in range(size)])  79.8 us
    ppermute x37, starting transfers between devices, split_hop(): return lax.ppermute(values, (ROW, COL), pairs)  57.4 us
    dot_general x13, matrix products, product_tn(): lax.dot_general(left, right, (((0,), (0,)), ((), ())), preferred_element_...  55.8 us
    dot_general x8, matrix products, product(): return jnp.dot(left, right, preferred_element_type=jnp.float32)  51.4 us
    dot_general x8, matrix products, product_t(): lax.dot_general(left, right, (((1,), (1,)), ((), ())), preferred_element_...  46.3 us
  transfers between devices with their start and end apart: 100, of which 44 were waited for; matrix products, arithmetic and copies ran while one was open for 22% of the time, Pallas kernels for 6%

profile of v4, /device:TPU:0, one launch (start us, length us, event | category | flops | bytes accessed | tf_op | source)
XLA Modules:
  0.0 1063.9 jit_solution(9333866324331121768)
XLA Ops:
  9.3 5.1 collective-permute-start.3
  15.1 5.4 concatenate.94
  44.5 10.9 %collective-permute-done.1 = bf16[8,80,128]{2,1,0:T(8,128)(2,1)} collective-permute-done((bf16[8,80,128]{2,1,0:T(8,128)(2,1)S(1)}, bf16[8,80,128]{2,1,0:T(8,128)(2,1)}, u32[]{:S(2)}, u32[]{:S(2)}) %collective-permute-start.1) | collective-permute-done | bytes 163872 | tf_op jit(solution)/shard_map/ppermute | solution.py:193
  60.6 5.2 collective-permute-done.17.refs_1_
  70.0 5.6 shard_map.394.columns_ref
  83.3 14.3 %collective-permute-done.4.refs_1_ = bf16[512,256]{1,0:T(8,128)(2,1)S(1)} collective-permute-done((bf16[512,256]{1,0:T(8,128)(2,1)S(1)}, bf16[512,256]{1,0:T(8,128)(2,1)S(1)}, u32[]{:S(2)}, u32[]{:S(2)}) %collective-permute-start.4) | collective-permute-done | bytes 262176 | tf_op jit(solution)/shard_map/ppermute | solution.py:193
  97.6 8.8 collective-permute-done.5.refs_2_
  115.2 21.3 %collective-permute-done.10.refs_1_ = bf16[4,512,256]{2,1,0:T(8,128)(2,1)S(1)} collective-permute-done((bf16[4,512,256]{2,1,0:T(8,128)(2,1)}, bf16[4,512,256]{2,1,0:T(8,128)(2,1)S(1)}, u32[]{:S(2)}, u32[]{:S(2)}) %collective-permute-start.10) | collective-permute-done | bytes 1048608 | tf_op jit(solution)/shard_map/ppermute | solution.py:193
  138.3 15.6 %collective-permute-start.23 = (bf16[512,256]{1,0:T(8,128)(2,1)S(1)}, bf16[512,256]{1,0:T(8,128)(2,1)S(1)}, u32[]{:S(2)}, u32[]{:S(2)}) collective-permute-start(bf16[512,256]{1,0:T(8,128)(2,1)S(1)} %copy-done.76), channel_id=1, source_target_pairs={{0,2},{1,3},{2,0},{3,1},{4,6},{5,7},{6,4},{7,5},{8,10},{9,11},{10,... | collective-permute-start | bytes 786440 | tf_op jit(solution)/shard_map/ppermute | solution.py:193
  154.1 10.2 collective-permute-done.23.refs_1_
  169.5 8.8 collective-permute-done.25.refs_3_
  188.3 7.1 shard_map.392.query_ref
  198.4 9.8 shard_map.396
  213.6 11.1 %collective-permute-done.28.refs_3_ = bf16[4,512,256]{2,1,0:T(8,128)(2,1)} collective-permute-done((bf16[4,512,256]{2,1,0:T(8,128)(2,1)S(1)}, bf16[4,512,256]{2,1,0:T(8,128)(2,1)}, u32[]{:S(2)}, u32[]{:S(2)}) %collective-permute-start.28) | collective-permute-done | bytes 1048608 | tf_op jit(solution)/shard_map/ppermute | solution.py:199
  229.4 7.4 shard_map.398
  251.1 44.6 %collective-permute-done.33 = bf16[512,2048]{1,0:T(8,128)(2,1)} collective-permute-done((bf16[512,2048]{1,0:T(8,128)(2,1)}, bf16[512,2048]{1,0:T(8,128)(2,1)}, u32[]{:S(2)}, u32[]{:S(2)}) %collective-permute-start.33) | collective-permute-done | bytes 2097184 | tf_op jit(solution)/shard_map/ppermute | solution.py:193
  299.6 18.6 %collective-permute-done.36 = bf16[512,1024]{1,0:T(8,128)(2,1)S(1)} collective-permute-done((bf16[512,1024]{1,0:T(8,128)(2,1)S(1)}, bf16[512,1024]{1,0:T(8,128)(2,1)S(1)}, u32[]{:S(2)}, u32[]{:S(2)}) %collective-permute-start.36) | collective-permute-done | bytes 1048608 | tf_op jit(solution)/shard_map/ppermute | solution.py:193
  322.9 29.4 %collective-permute-done.38 = bf16[512,1024]{1,0:T(8,128)(2,1)S(1)} collective-permute-done((bf16[512,1024]{1,0:T(8,128)(2,1)S(1)}, bf16[512,1024]{1,0:T(8,128)(2,1)S(1)}, u32[]{:S(2)}, u32[]{:S(2)}) %collective-permute-start.38) | collective-permute-done | bytes 1048608 | tf_op jit(solution)/shard_map/ppermute | solution.py:199
  361.8 12.8 %convolution_convert_fusion.3 = bf16[1024,2048]{1,0:T(8,128)(2,1)S(1)} fusion(bf16[1024,2048]{1,0:T(8,128)(2,1)} %all-gather.8.cloned.1.call-done, bf16[2048,2048]{1,0:T(8,128)(2,1)} %constant_dynamic-update-slice_fusion), kind=kOutput, calls=%fused_computation.55 | convolution fusion | flops 8592031744 | bytes 16777216 | tf_op jit(solution)/shard_map/dot_general | solution.py:176
  376.5 6.7 convolution_convert_fusion.8
  383.3 12.6 %convolution_convert_fusion.2 = bf16[1024,2048]{1,0:T(8,128)(2,1)S(1)} fusion(bf16[1024,2048]{1,0:T(8,128)(2,1)} %all-gather.10.cloned.1.call-done, bf16[2048,2048]{1,0:T(8,128)(2,1)} %constant_dynamic-update-slice_fusion), kind=kOutput, calls=%fused_computation.54 | convolution fusion | flops 8592031744 | bytes 16777216 | tf_op jit(solution)/shard_map/dot_general | solution.py:176
  397.9 6.7 convolution_convert_fusion.7
  405.5 8.8 collective-permute-start.39
  414.3 5.3 collective-permute-start.40
  439.4 9.1 collective-permute-done.43
  448.5 10.5 collective-permute-done.44
  465.6 51.3 %reduce-scatter.6.cloned.1.call-done = bf16[128,2048]{1,0:T(8,128)(2,1)} async-done(((bf16[1024,2048]{1,0:T(8,128)(2,1)}), bf16[128,2048]{1,0:T(8,128)(2,1)}) %reduce-scatter.6.cloned.1.call-update) | async-done | bytes 524304 | tf_op jit(solution)/shard_map/reduce_scatter | solution.py:795
  581.5 11.8 %fusion.9 = (bf16[1024,1024]{1,0:T(8,128)(2,1)S(1)}, bf16[1024,1024]{1,0:T(8,128)(2,1)S(1)}) fusion(bf16[1024,2048]{1,0:T(8,128)(2,1)} %copy-done.146, bf16[1024,2048]{1,0:T(8,128)(2,1)} %all-gather.12.cloned.1.call-done, bf16[2048,1024]{1,0:T(8,128)(2,1)} %copy-done.70), kind=kOutput, calls=%fused_computation.26 | convolution fusion | flops 4322230272 | bytes 16777216 | tf_op jit(solution)/shard_map/dot_general | solution.py:176
  595.2 12.7 %fusion.31 = bf16[1024,2048]{1,0:T(8,128)(2,1)} fusion(bf16[2048,2048]{1,0:T(8,128)(2,1)} %constant_dynamic-update-slice_fusion, bf16[1024,1024]{1,0:T(8,128)(2,1)S(1)} %get-tuple-element.193, bf16[1024,1024]{1,0:T(8,128)(2,1)S(1)} %get-tuple-element.192), kind=kOutput, calls=%fused_computation.62 | convolution fusion | flops 8600420352 | bytes 16777216 | tf_op jit(solution)/shard_map/dot_general | solution.py:180
  607.9 10.4 convolution_convert_fusion.6
  618.3 6.4 convolution_convert_fusion.4
  624.7 6.2 convolution_convert_fusion.5
  630.9 11.4 %fusion.6 = (bf16[1024,1024]{1,0:T(8,128)(2,1)S(1)}, bf16[1024,1024]{1,0:T(8,128)(2,1)S(1)}) fusion(bf16[1024,2048]{1,0:T(8,128)(2,1)} %copy-done.151, bf16[1024,2048]{1,0:T(8,128)(2,1)} %all-gather.14.cloned.1.call-done, bf16[2048,1024]{1,0:T(8,128)(2,1)} %copy-done.70), kind=kOutput, calls=%fused_computation.23 | convolution fusion | flops 4322230272 | bytes 16777216 | tf_op jit(solution)/shard_map/dot_general | solution.py:176
  644.3 12.6 %fusion.28 = bf16[1024,2048]{1,0:T(8,128)(2,1)} fusion(bf16[2048,2048]{1,0:T(8,128)(2,1)} %constant_dynamic-update-slice_fusion, bf16[1024,1024]{1,0:T(8,128)(2,1)S(1)} %get-tuple-element.191, bf16[1024,1024]{1,0:T(8,128)(2,1)S(1)} %get-tuple-element.190), kind=kOutput, calls=%fused_computation.61 | convolution fusion | flops 8600420352 | bytes 16777216 | tf_op jit(solution)/shard_map/dot_general | solution.py:180
  661.2 44.6 %reduce-scatter.12.cloned.1.call-done = bf16[128,2048]{1,0:T(8,128)(2,1)} async-done(((bf16[1024,2048]{1,0:T(8,128)(2,1)}), bf16[128,2048]{1,0:T(8,128)(2,1)}) %reduce-scatter.12.cloned.1.call-update) | async-done | bytes 524304 | tf_op jit(solution)/shard_map/reduce_scatter | solution.py:846
  705.8 50.7 %reduce-scatter.10.cloned.1.call-done = bf16[128,2048]{1,0:T(8,128)(2,1)} async-done(((bf16[1024,2048]{1,0:T(8,128)(2,1)}), bf16[128,2048]{1,0:T(8,128)(2,1)}) %reduce-scatter.10.cloned.1.call-update) | async-done | bytes 524304 | tf_op jit(solution)/shard_map/reduce_scatter | solution.py:846
  766.3 7.1 shard_map.403.grad_ref
  773.3 13.1 %shard_map.404 = (f32[256,2048]{1,0:T(8,128)}, bf16[8,2,256,512]{3,2,1,0:T(8,128)(2,1)}) custom-call(s32[2]{0:T(128)} %pad_add_fusion.1.span_ref, s32[2,256]{1,0:T(2,128)} %get-tuple-element.272.window_ref, bf16[256,2048]{1,0:T(8,128)(2,1)} %shard_map.393.query_ref, bf16[8,2,256,512]{3,2,1,0:T(8,128)(2,1)} %bitcast.121, bf16[8,2,256,512]{3,2,1,0:T(8,128)(2,1)} %bitcast.122, ...), custom_call_target="tpu_custom_call" | custom-call | flops 10737418240 | bytes 8388608 | tf_op jit(solution)/shard_map/pallas_call | solution.py:601
  786.5 9.8 add_convert_fusion.2
  805.5 5.2 add_convert_fusion
  831.5 19.7 %collective-permute-done.80 = bf16[512,1024]{1,0:T(8,128)(2,1)S(1)} collective-permute-done((bf16[512,1024]{1,0:T(8,128)(2,1)}, bf16[512,1024]{1,0:T(8,128)(2,1)S(1)}, u32[]{:S(2)}, u32[]{:S(2)}) %collective-permute-start.80) | collective-permute-done | bytes 1048608 | tf_op jit(solution)/shard_map/ppermute | solution.py:199
  885.2 7.8 shard_map.407
  911.4 6.0 shard_map.410
  934.5 8.8 collective-permute-done.72
  946.7 15.1 %collective-permute-start.74 = (bf16[512,256]{1,0:T(8,128)(2,1)S(1)}, bf16[512,256]{1,0:T(8,128)(2,1)S(1)}, u32[]{:S(2)}, u32[]{:S(2)}) collective-permute-start(bf16[512,256]{1,0:T(8,128)(2,1)S(1)} %get-tuple-element.214), channel_id=1, source_target_pairs={{0,4},{1,3},{2,6},{3,1},{4,0},{5,7},{6,2},{7,5},{8,12},{9,11},{10,... | collective-permute-start | bytes 786440 | tf_op jit(solution)/shard_map/ppermute | solution.py:199
  973.7 5.3 collective-permute-done.86
  994.6 15.6 %collective-permute-done.73 = bf16[512,256]{1,0:T(8,128)(2,1)S(1)} collective-permute-done((bf16[512,256]{1,0:T(8,128)(2,1)S(1)}, bf16[512,256]{1,0:T(8,128)(2,1)S(1)}, u32[]{:S(2)}, u32[]{:S(2)}) %collective-permute-start.73) | collective-permute-done | bytes 262176 | tf_op jit(solution)/shard_map/ppermute | solution.py:199
  1029.2 13.0 %collective-permute-done.63 = bf16[512,256]{1,0:T(8,128)(2,1)S(1)} collective-permute-done((bf16[512,256]{1,0:T(8,128)(2,1)S(1)}, bf16[512,256]{1,0:T(8,128)(2,1)S(1)}, u32[]{:S(2)}, u32[]{:S(2)}) %collective-permute-start.63) | collective-permute-done | bytes 262176 | tf_op jit(solution)/shard_map/ppermute | solution.py:199
  (686 shorter events, 387.9 us)
Async XLA Ops:
  9.3 28.0 %collective-permute-start.3 = (bf16[512,128]{1,0:T(8,128)(2,1)S(1)}, bf16[512,128]{1,0:T(8,128)(2,1)S(1)}, u32[]{:S(2)}, u32[]{:S(2)}) collective-permute-start(bf16[512,128]{1,0:T(8,128)(2,1)S(1)} %pad_maximum_fusion.17.refs_0_), channel_id=1, source_target_pairs={{0,6},{1,7},{2,4},{3,5},{4,2},{5,3},{6,0},{7,1},{8,14},{9,15},{10,... | collective-permute-start | bytes 393224 | tf_op jit(solution)/shard_map/ppermute | solution.py:193
  14.5 23.3 %collective-permute-start.8 = (bf16[512,128]{1,0:T(8,128)(2,1)S(1)}, bf16[512,128]{1,0:T(8,128)(2,1)S(1)}, u32[]{:S(2)}, u32[]{:S(2)}) collective-permute-start(bf16[512,128]{1,0:T(8,128)(2,1)S(1)} %pad_maximum_fusion.17.refs_0_), channel_id=1, source_target_pairs={{0,4},{1,5},{2,6},{3,7},{4,0},{5,1},{6,2},{7,3},{8,12},{9,13},{10,... | collective-permute-start | bytes 393224 | tf_op jit(solution)/shard_map/ppermute | solution.py:193
  27.1 171.3 %all-gather.6.cloned.1.call-start = ((), (), s32[]{:S(2)}) async-start(), calls=%async_computation.7 | async-start | bytes 4718592 | tf_op jit(solution)/shard_map/all_gather | solution.py:743
  78.2 283.6 %all-gather.8.cloned.1.call-start = ((), (), s32[]{:S(2)}) async-start(), calls=%async_computation.8 | async-start | bytes 4718592 | tf_op jit(solution)/shard_map/all_gather | solution.py:782
  80.0 26.4 %collective-permute-start.5 = (bf16[512,256]{1,0:T(8,128)(2,1)S(1)}, bf16[512,256]{1,0:T(8,128)(2,1)S(1)}, u32[]{:S(2)}, u32[]{:S(2)}) collective-permute-start(bf16[512,256]{1,0:T(8,128)(2,1)S(1)} %copy-done.75), channel_id=1, source_target_pairs={{0,4},{1,5},{2,6},{3,7},{4,0},{5,1},{6,2},{7,3},{8,12},{9,13},{10,... | collective-permute-start | bytes 786440 | tf_op jit(solution)/shard_map/ppermute | solution.py:193
  81.7 27.8 %collective-permute-start.6 = (bf16[512,256]{1,0:T(8,128)(2,1)S(1)}, bf16[512,256]{1,0:T(8,128)(2,1)S(1)}, u32[]{:S(2)}, u32[]{:S(2)}) collective-permute-start(bf16[512,256]{1,0:T(8,128)(2,1)S(1)} %copy-done.75), channel_id=1, source_target_pairs={{0,6},{1,7},{2,4},{3,5},{4,2},{5,3},{6,0},{7,1},{8,14},{9,15},{10,... | collective-permute-start | bytes 786440 | tf_op jit(solution)/shard_map/ppermute | solution.py:193
  112.5 24.0 %collective-permute-start.10 = (bf16[4,512,256]{2,1,0:T(8,128)(2,1)}, bf16[4,512,256]{2,1,0:T(8,128)(2,1)S(1)}, u32[]{:S(2)}, u32[]{:S(2)}) collective-permute-start(bf16[4,512,256]{2,1,0:T(8,128)(2,1)} %shard_map.390.refs_0_), channel_id=1, source_target_pairs={{0,8},{8,0},{16,24},{24,16},{1,9},{9,1},{17,25},{25,17},{2,10},{10... | collective-permute-start | bytes 3145736 | tf_op jit(solution)/shard_map/ppermute | solution.py:193
  113.2 23.9 %collective-permute-start.11 = (bf16[4,512,256]{2,1,0:T(8,128)(2,1)}, bf16[4,512,256]{2,1,0:T(8,128)(2,1)S(1)}, u32[]{:S(2)}, u32[]{:S(2)}) collective-permute-start(bf16[4,512,256]{2,1,0:T(8,128)(2,1)} %shard_map.390.refs_0_), channel_id=1, source_target_pairs={{0,16},{8,24},{16,0},{24,8},{1,17},{9,25},{17,1},{25,9},{2,18},{10... | collective-permute-start | bytes 3145736 | tf_op jit(solution)/shard_map/ppermute | solution.py:193
  137.3 27.0 %collective-permute-start.12 = (bf16[4,512,256]{2,1,0:T(8,128)(2,1)S(1)}, bf16[4,512,256]{2,1,0:T(8,128)(2,1)}, u32[]{:S(2)}, u32[]{:S(2)}) collective-permute-start(bf16[4,512,256]{2,1,0:T(8,128)(2,1)S(1)} %broadcast_select_fusion.8), channel_id=1, source_target_pairs={{0,16},{1,9},{2,18},{3,11},{4,20},{5,13},{6,22},{7,15},{8,24},{9,1... | collective-permute-start | bytes 3145736 | tf_op jit(solution)/shard_map/ppermute | solution.py:199
  138.3 43.3 %collective-permute-start.13 = (bf16[4,512,256]{2,1,0:T(8,128)(2,1)S(1)}, bf16[4,512,256]{2,1,0:T(8,128)(2,1)}, u32[]{:S(2)}, u32[]{:S(2)}) collective-permute-start(bf16[4,512,256]{2,1,0:T(8,128)(2,1)S(1)} %copy-done.12), channel_id=1, source_target_pairs={{0,1},{1,0},{2,3},{3,2},{4,5},{5,4},{6,7},{7,6},{8,9},{9,8},{10,11... | collective-permute-start | bytes 3145736 | tf_op jit(solution)/shard_map/ppermute | solution.py:193
  138.3 26.0 %collective-permute-start.23 = (bf16[512,256]{1,0:T(8,128)(2,1)S(1)}, bf16[512,256]{1,0:T(8,128)(2,1)S(1)}, u32[]{:S(2)}, u32[]{:S(2)}) collective-permute-start(bf16[512,256]{1,0:T(8,128)(2,1)S(1)} %copy-done.76), channel_id=1, source_target_pairs={{0,2},{1,3},{2,0},{3,1},{4,6},{5,7},{6,4},{7,5},{8,10},{9,11},{10,... | collective-permute-start | bytes 786440 | tf_op jit(solution)/shard_map/ppermute | solution.py:193
  153.9 34.4 %collective-permute-start.14 = (bf16[4,512,256]{2,1,0:T(8,128)(2,1)S(1)}, bf16[4,512,256]{2,1,0:T(8,128)(2,1)}, u32[]{:S(2)}, u32[]{:S(2)}) collective-permute-start(bf16[4,512,256]{2,1,0:T(8,128)(2,1)S(1)} %collective-permute-done.10.refs_1_), channel_id=1, source_target_pairs={{0,1},{1,0},{2,3},{3,2},{4,5},{5,4},{6,7},{7,6},{8,9},{9,8},{10,11... | collective-permute-start | bytes 3145736 | tf_op jit(solution)/shard_map/ppermute | solution.py:193
  164.3 24.1 %collective-permute-start.15 = (bf16[4,512,256]{2,1,0:T(8,128)(2,1)S(1)}, bf16[4,512,256]{2,1,0:T(8,128)(2,1)}, u32[]{:S(2)}, u32[]{:S(2)}) collective-permute-start(bf16[4,512,256]{2,1,0:T(8,128)(2,1)S(1)} %collective-permute-done.11.refs_2_), channel_id=1, source_target_pairs={{0,1},{1,0},{2,3},{3,2},{4,5},{5,4},{6,7},{7,6},{8,9},{9,8},{10,11... | collective-permute-start | bytes 3145736 | tf_op jit(solution)/shard_map/ppermute | solution.py:193
  164.3 24.1 %collective-permute-start.16 = (bf16[4,512,256]{2,1,0:T(8,128)(2,1)}, bf16[4,512,256]{2,1,0:T(8,128)(2,1)}, u32[]{:S(2)}, u32[]{:S(2)}) collective-permute-start(bf16[4,512,256]{2,1,0:T(8,128)(2,1)} %collective-permute-done.12.refs_3_), channel_id=1, source_target_pairs={{0,1},{1,0},{2,3},{3,2},{4,5},{5,4},{6,7},{7,6},{8,9},{9,8},{10,11... | collective-permute-start | bytes 3145736 | tf_op jit(solution)/shard_map/ppermute | solution.py:193
  180.6 27.6 %collective-permute-start.26 = (bf16[4,512,256]{2,1,0:T(8,128)(2,1)}, bf16[4,512,256]{2,1,0:T(8,128)(2,1)}, u32[]{:S(2)}, u32[]{:S(2)}) collective-permute-start(bf16[4,512,256]{2,1,0:T(8,128)(2,1)} %shard_map.397.refs_0_), channel_id=1, source_target_pairs={{0,8},{8,0},{16,24},{24,16},{1,9},{9,1},{17,25},{25,17},{2,10},{10... | collective-permute-start | bytes 3145736 | tf_op jit(solution)/shard_map/ppermute | solution.py:193
  181.6 26.7 %collective-permute-start.27 = (bf16[4,512,256]{2,1,0:T(8,128)(2,1)}, bf16[4,512,256]{2,1,0:T(8,128)(2,1)}, u32[]{:S(2)}, u32[]{:S(2)}) collective-permute-start(bf16[4,512,256]{2,1,0:T(8,128)(2,1)} %shard_map.397.refs_0_), channel_id=1, source_target_pairs={{0,16},{8,24},{16,0},{24,8},{1,17},{9,25},{17,1},{25,9},{2,18},{10... | collective-permute-start | bytes 3145736 | tf_op jit(solution)/shard_map/ppermute | solution.py:193
  243.7 139.5 %all-gather.10.cloned.1.call-start = ((), (), s32[]{:S(2)}) async-start(), calls=%async_computation.10 | async-start | bytes 4718592 | tf_op jit(solution)/shard_map/all_gather | solution.py:782
  246.9 48.8 %collective-permute-start.33 = (bf16[512,2048]{1,0:T(8,128)(2,1)}, bf16[512,2048]{1,0:T(8,128)(2,1)}, u32[]{:S(2)}, u32[]{:S(2)}) collective-permute-start(bf16[512,2048]{1,0:T(8,128)(2,1)} %pad_maximum_fusion), channel_id=1, source_target_pairs={{0,8},{8,0},{16,24},{24,16},{1,9},{9,1},{17,25},{25,17},{2,10},{10... | collective-permute-start | bytes 6291464 | tf_op jit(solution)/shard_map/ppermute | solution.py:193
  248.7 48.8 %collective-permute-start.34 = (bf16[512,2048]{1,0:T(8,128)(2,1)}, bf16[512,2048]{1,0:T(8,128)(2,1)}, u32[]{:S(2)}, u32[]{:S(2)}) collective-permute-start(bf16[512,2048]{1,0:T(8,128)(2,1)} %pad_maximum_fusion), channel_id=1, source_target_pairs={{0,16},{8,24},{16,0},{24,8},{1,17},{9,25},{17,1},{25,9},{2,18},{10... | collective-permute-start | bytes 6291464 | tf_op jit(solution)/shard_map/ppermute | solution.py:193
  248.9 216.7 %reduce-scatter.8.cloned.1.call-start = ((), (), s32[]{:S(2)}) async-start(), calls=%async_computation.11 | async-start | bytes 4718592 | tf_op jit(solution)/shard_map/reduce_scatter | solution.py:795
  248.9 69.2 %collective-permute-start.36 = (bf16[512,1024]{1,0:T(8,128)(2,1)S(1)}, bf16[512,1024]{1,0:T(8,128)(2,1)S(1)}, u32[]{:S(2)}, u32[]{:S(2)}) collective-permute-start(bf16[512,1024]{1,0:T(8,128)(2,1)S(1)} %copy-done.56), channel_id=1, source_target_pairs={{0,8},{8,0},{16,24},{24,16},{1,9},{9,1},{17,25},{25,17},{2,10},{10... | collective-permute-start | bytes 3145736 | tf_op jit(solution)/shard_map/ppermute | solution.py:193
  250.0 68.6 %collective-permute-start.37 = (bf16[512,1024]{1,0:T(8,128)(2,1)S(1)}, bf16[512,1024]{1,0:T(8,128)(2,1)S(1)}, u32[]{:S(2)}, u32[]{:S(2)}) collective-permute-start(bf16[512,1024]{1,0:T(8,128)(2,1)S(1)} %copy-done.56), channel_id=1, source_target_pairs={{0,16},{8,24},{16,0},{24,8},{1,17},{9,25},{17,1},{25,9},{2,18},{10... | collective-permute-start | bytes 3145736 | tf_op jit(solution)/shard_map/ppermute | solution.py:193
  299.3 61.0 %collective-permute-start.35 = (bf16[512,2048]{1,0:T(8,128)(2,1)S(1)}, bf16[512,2048]{1,0:T(8,128)(2,1)S(1)}, u32[]{:S(2)}, u32[]{:S(2)}) collective-permute-start(bf16[512,2048]{1,0:T(8,128)(2,1)S(1)} %broadcast_select_fusion), channel_id=1, source_target_pairs={{0,16},{1,9},{2,18},{3,11},{4,20},{5,13},{6,22},{7,15},{8,24},{9,1... | collective-permute-start | bytes 6291464 | tf_op jit(solution)/shard_map/ppermute | solution.py:199
  318.7 33.6 %collective-permute-start.38 = (bf16[512,1024]{1,0:T(8,128)(2,1)S(1)}, bf16[512,1024]{1,0:T(8,128)(2,1)S(1)}, u32[]{:S(2)}, u32[]{:S(2)}) collective-permute-start(bf16[512,1024]{1,0:T(8,128)(2,1)S(1)} %broadcast_select_fusion.6), channel_id=1, source_target_pairs={{0,16},{1,9},{2,18},{3,11},{4,20},{5,13},{6,22},{7,15},{8,24},{9,1... | collective-permute-start | bytes 3145736 | tf_op jit(solution)/shard_map/ppermute | solution.py:199
  404.6 112.3 %reduce-scatter.6.cloned.1.call-start = ((), (), s32[]{:S(2)}) async-start(), calls=%async_computation.9 | async-start | bytes 4718592 | tf_op jit(solution)/shard_map/reduce_scatter | solution.py:795
  405.2 176.2 %all-gather.12.cloned.1.call-start = ((), (), s32[]{:S(2)}) async-start(), calls=%async_computation.12 | async-start | bytes 4718592 | tf_op jit(solution)/shard_map/all_gather | solution.py:833
  433.8 25.3 %collective-permute-start.44 = (bf16[8,64,512]{2,1,0:T(8,128)(2,1)}, bf16[8,64,512]{2,1,0:T(8,128)(2,1)}, u32[]{:S(2)}, u32[]{:S(2)}) collective-permute-start(bf16[8,64,512]{2,1,0:T(8,128)(2,1)} %shard_map.400), channel_id=1, source_target_pairs={{0,16},{8,24},{16,0},{24,8},{1,17},{9,25},{17,1},{25,9},{2,18},{10... | collective-permute-start | bytes 1572872 | tf_op jit(solution)/shard_map/ppermute | solution.py:193
  433.8 25.3 %collective-permute-start.45 = (bf16[8,64,512]{2,1,0:T(8,128)(2,1)}, bf16[8,64,512]{2,1,0:T(8,128)(2,1)}, u32[]{:S(2)}, u32[]{:S(2)}) collective-permute-start(bf16[8,64,512]{2,1,0:T(8,128)(2,1)} %shard_map.400), channel_id=1, source_target_pairs={{0,24},{8,16},{16,8},{24,0},{1,25},{9,17},{17,9},{25,1},{2,26},{10... | collective-permute-start | bytes 1572872 | tf_op jit(solution)/shard_map/ppermute | solution.py:193
  531.8 99.1 %all-gather.14.cloned.1.call-start = ((), (), s32[]{:S(2)}) async-start(), calls=%async_computation.14 | async-start | bytes 4718592 | tf_op jit(solution)/shard_map/all_gather | solution.py:833
  560.2 145.6 %reduce-scatter.12.cloned.1.call-start = ((), (), s32[]{:S(2)}) async-start(), calls=%async_computation.15 | async-start | bytes 4718592 | tf_op jit(solution)/shard_map/reduce_scatter | solution.py:846
  657.0 99.6 %reduce-scatter.10.cloned.1.call-start = ((), (), s32[]{:S(2)}) async-start(), calls=%async_computation.13 | async-start | bytes 4718592 | tf_op jit(solution)/shard_map/reduce_scatter | solution.py:846
  657.7 240.8 %reduce-scatter.14.cloned.1.call-start = ((), (), s32[]{:S(2)}) async-start(), calls=%async_computation.16 | async-start | bytes 4718592 | tf_op jit(solution)/shard_map/reduce_scatter | solution.py:874
  815.1 36.0 %collective-permute-start.80 = (bf16[512,1024]{1,0:T(8,128)(2,1)}, bf16[512,1024]{1,0:T(8,128)(2,1)S(1)}, u32[]{:S(2)}, u32[]{:S(2)}) collective-permute-start(bf16[512,1024]{1,0:T(8,128)(2,1)} %get-tuple-element.197), channel_id=1, source_target_pairs={{0,16},{1,9},{2,18},{3,11},{4,20},{5,13},{6,22},{7,15},{8,24},{9,1... | collective-permute-start | bytes 3145736 | tf_op jit(solution)/shard_map/ppermute | solution.py:199
  816.0 35.1 %collective-permute-start.55 = (bf16[256,2048]{1,0:T(8,128)(2,1)S(1)}, bf16[256,2048]{1,0:T(8,128)(2,1)}, u32[]{:S(2)}, u32[]{:S(2)}) collective-permute-start(bf16[256,2048]{1,0:T(8,128)(2,1)S(1)} %copy-done.27), channel_id=1, source_target_pairs={{0,1},{1,0},{2,3},{3,2},{4,5},{5,4},{6,7},{7,6},{8,9},{9,8},{10,11... | collective-permute-start | bytes 3145736 | tf_op jit(solution)/shard_map/ppermute | solution.py:193
  822.3 109.6 %collective-permute-start.82 = (bf16[512,1024]{1,0:T(8,128)(2,1)}, bf16[512,1024]{1,0:T(8,128)(2,1)}, u32[]{:S(2)}, u32[]{:S(2)}) collective-permute-start(bf16[512,1024]{1,0:T(8,128)(2,1)} %get-tuple-element.194), channel_id=1, source_target_pairs={{0,16},{1,9},{2,18},{3,11},{4,20},{5,13},{6,22},{7,15},{8,24},{9,1... | collective-permute-start | bytes 3145736 | tf_op jit(solution)/shard_map/ppermute | solution.py:199
  824.5 107.8 %collective-permute-start.84 = (bf16[512,1024]{1,0:T(8,128)(2,1)}, bf16[512,1024]{1,0:T(8,128)(2,1)}, u32[]{:S(2)}, u32[]{:S(2)}) collective-permute-start(bf16[512,1024]{1,0:T(8,128)(2,1)} %add_convert_fusion.3), channel_id=1, source_target_pairs={{0,8},{1,17},{2,10},{3,19},{4,12},{5,21},{6,14},{7,23},{8,0},{9,25... | collective-permute-start | bytes 3145736 | tf_op jit(solution)/shard_map/ppermute | solution.py:199
  872.2 60.5 %collective-permute-start.70 = (bf16[512,1024]{1,0:T(8,128)(2,1)}, bf16[512,1024]{1,0:T(8,128)(2,1)}, u32[]{:S(2)}, u32[]{:S(2)}) collective-permute-start(bf16[512,1024]{1,0:T(8,128)(2,1)} %get-tuple-element.200), channel_id=1, source_target_pairs={{0,16},{1,9},{2,18},{3,11},{4,20},{5,13},{6,22},{7,15},{8,24},{9,1... | collective-permute-start | bytes 3145736 | tf_op jit(solution)/shard_map/ppermute | solution.py:199
  872.2 26.3 %collective-permute-start.71 = (bf16[512,1024]{1,0:T(8,128)(2,1)}, bf16[512,1024]{1,0:T(8,128)(2,1)}, u32[]{:S(2)}, u32[]{:S(2)}) collective-permute-start(bf16[512,1024]{1,0:T(8,128)(2,1)} %get-tuple-element.201), channel_id=1, source_target_pairs={{0,16},{1,9},{2,18},{3,11},{4,20},{5,13},{6,22},{7,15},{8,24},{9,1... | collective-permute-start | bytes 3145736 | tf_op jit(solution)/shard_map/ppermute | solution.py:199
  885.2 40.2 %collective-permute-start.60 = (bf16[512,1024]{1,0:T(8,128)(2,1)}, bf16[512,1024]{1,0:T(8,128)(2,1)}, u32[]{:S(2)}, u32[]{:S(2)}) collective-permute-start(bf16[512,1024]{1,0:T(8,128)(2,1)} %get-tuple-element.203), channel_id=1, source_target_pairs={{0,16},{1,9},{2,18},{3,11},{4,20},{5,13},{6,22},{7,15},{8,24},{9,1... | collective-permute-start | bytes 3145736 | tf_op jit(solution)/shard_map/ppermute | solution.py:199
  925.4 41.0 %collective-permute-start.59 = (bf16[512,1024]{1,0:T(8,128)(2,1)}, bf16[512,1024]{1,0:T(8,128)(2,1)S(1)}, u32[]{:S(2)}, u32[]{:S(2)}) collective-permute-start(bf16[512,1024]{1,0:T(8,128)(2,1)} %get-tuple-element.202), channel_id=1, source_target_pairs={{0,16},{1,9},{2,18},{3,11},{4,20},{5,13},{6,22},{7,15},{8,24},{9,1... | collective-permute-start | bytes 3145736 | tf_op jit(solution)/shard_map/ppermute | solution.py:199
  931.9 56.6 %collective-permute-start.65 = (bf16[512,512]{0,1:T(8,128)(2,1)}, bf16[512,512]{0,1:T(8,128)(2,1)}, u32[]{:S(2)}, u32[]{:S(2)}) collective-permute-start(bf16[512,512]{0,1:T(8,128)(2,1)} %get-tuple-element.206), channel_id=1, source_target_pairs={{0,16},{1,9},{2,18},{3,11},{4,20},{5,13},{6,22},{7,15},{8,24},{9,1... | collective-permute-start | bytes 1572872 | tf_op jit(solution)/shard_map/ppermute | solution.py:199
  932.3 59.2 %collective-permute-start.66 = (bf16[512,512]{0,1:T(8,128)(2,1)}, bf16[512,512]{0,1:T(8,128)(2,1)}, u32[]{:S(2)}, u32[]{:S(2)}) collective-permute-start(bf16[512,512]{0,1:T(8,128)(2,1)} %add_convert_fusion.13), channel_id=1, source_target_pairs={{0,8},{1,17},{2,10},{3,19},{4,12},{5,21},{6,14},{7,23},{8,0},{9,25... | collective-permute-start | bytes 1572872 | tf_op jit(solution)/shard_map/ppermute | solution.py:199
  932.7 39.0 %collective-permute-start.85 = (f32[8,68,128]{2,1,0:T(8,128)S(1)}, f32[8,68,128]{2,1,0:T(8,128)S(1)}, u32[]{:S(2)}, u32[]{:S(2)}) collective-permute-start(f32[8,68,128]{2,1,0:T(8,128)S(1)} %get-tuple-element.212), channel_id=1, source_target_pairs={{0,8},{8,0},{16,24},{24,16},{1,9},{9,1},{17,25},{25,17},{2,10},{10... | collective-permute-start | bytes 835592 | tf_op jit(solution)/shard_map/ppermute | solution.py:193
  971.7 71.2 %collective-permute-start.79 = (bf16[512,1024]{1,0:T(8,128)(2,1)}, bf16[512,1024]{1,0:T(8,128)(2,1)}, u32[]{:S(2)}, u32[]{:S(2)}) collective-permute-start(bf16[512,1024]{1,0:T(8,128)(2,1)} %get-tuple-element.196), channel_id=1, source_target_pairs={{0,16},{1,9},{2,18},{3,11},{4,20},{5,13},{6,22},{7,15},{8,24},{9,1... | collective-permute-start | bytes 3145736 | tf_op jit(solution)/shard_map/ppermute | solution.py:199
  979.1 66.4 %collective-permute-start.76 = (bf16[512,1024]{1,0:T(8,128)(2,1)}, bf16[512,1024]{1,0:T(8,128)(2,1)}, u32[]{:S(2)}, u32[]{:S(2)}) collective-permute-start(bf16[512,1024]{1,0:T(8,128)(2,1)} %get-tuple-element.198), channel_id=1, source_target_pairs={{0,16},{1,9},{2,18},{3,11},{4,20},{5,13},{6,22},{7,15},{8,24},{9,1... | collective-permute-start | bytes 3145736 | tf_op jit(solution)/shard_map/ppermute | solution.py:199
  981.6 36.8 %collective-permute-start.61 = (bf16[512,1024]{1,0:T(8,128)(2,1)}, bf16[512,1024]{1,0:T(8,128)(2,1)S(1)}, u32[]{:S(2)}, u32[]{:S(2)}) collective-permute-start(bf16[512,1024]{1,0:T(8,128)(2,1)} %add_convert_fusion.9), channel_id=1, source_target_pairs={{0,8},{1,17},{2,10},{3,19},{4,12},{5,21},{6,14},{7,23},{8,0},{9,25... | collective-permute-start | bytes 3145736 | tf_op jit(solution)/shard_map/ppermute | solution.py:199
  985.1 57.9 %all-to-all-start.1 = ((f32[8,68,128]{2,1,0:T(8,128)}), f32[8,68,128]{2,1,0:T(8,128)S(1)}, u32[]{:S(2)}, u32[]{:S(2)}) async-start(f32[8,68,128]{2,1,0:T(8,128)} %bitcast_add_fusion), calls=%async_computation.6 | async-start | bytes 589824 | tf_op jit(solution)/shard_map/all_to_all | solution.py:950
  1010.1 35.3 %collective-permute-start.81 = (bf16[512,1024]{1,0:T(8,128)(2,1)S(1)}, bf16[512,1024]{1,0:T(8,128)(2,1)}, u32[]{:S(2)}, u32[]{:S(2)}) collective-permute-start(bf16[512,1024]{1,0:T(8,128)(2,1)S(1)} %copy-done.55), channel_id=1, source_target_pairs={{0,8},{1,17},{2,10},{3,19},{4,12},{5,21},{6,14},{7,23},{8,0},{9,25... | collective-permute-start | bytes 3145736 | tf_op jit(solution)/shard_map/ppermute | solution.py:199
  (208 other events, 3502.7 us)
Sparse Core Ops, SparseCore 0:
  78.4 62.9 all-gather.5
  243.8 57.7 all-gather.7
  303.3 45.6 all-gather.9
  404.7 60.8 reduce-scatter.7
  467.7 49.1 reduce-scatter.5
  531.9 49.5 all-gather.11
  583.1 45.6 all-gather.13
  657.0 48.7 reduce-scatter.11
  708.1 48.3 reduce-scatter.9
  786.6 66.5 reduce-scatter.13
